TPU v7x, 32 devices: a whole 2x2x4 slice. The times are simulated.
32 devices in a mesh: seg: 4 (over x, core), space: 8 (over z, y).
Axes of the slice: x: 2, y: 2, z: 4, core: 2. Of those that a mesh axis runs over, the one named last changes fastest.
Arguments:
- directions: float32 [4, 16, 32, 64, 128], P('seg', None, 'space'), may hold values from -100 to 100
- adjoint: float32 [4, 32, 64, 128], P('seg', 'space'), may hold values from -1000 to 1000
- velocity: float32 [4, 3, 32, 64, 128], P('seg', None, 'space'), may hold values from -1 to 1
- diffusivity: float32 [4, 32, 64, 128], P('seg', 'space'), may hold values from 0.05 to 0.15
- objective_source: float32 [4, 32, 64, 128], P('seg', 'space'), may hold values from -6 to 6
- segment_start: int32 [4], P('seg'), may hold values from 0 to 999
Outputs:
- basis_rows: float32 [4, 16, 32, 64, 128], P('seg', None, 'space')
- factor_upper: float32 [4, 16, 16], P('seg')
- coefficients: float32 [4, 16], P('seg')
- shadow: float32 [4, 32, 64, 128], P('seg', 'space')
- gradient: float32 [32, 64, 128], P('space', 'seg')
All inputs are finite; a program needn't handle non-finite values.
Results may differ from a plain program's by a relative error of at most 0.0003.
Values sent between devices are 32-bit elements; how exact they have to be, the bound alone decides.
No kernel may reach another device: no remote copies, remote signals or barrier semaphores. Data moves between devices by JAX's collectives and lax.ppermute only.
A program may use at most 64 MiB of HBM per device.

v0:
```python
import math

import jax
import jax.numpy as jnp
from jax import lax
from jax.sharding import PartitionSpec as P


def with_halo(array, sides, width):
    for axis, dim in sides:
        size, length = (lax.axis_size(axis), array.shape[dim])
        up = [(i, (i + 1) % size) for i in range(size)]
        down = [(j, i) for i, j in up]
        last = lax.slice_in_dim(array, length - width, length, axis=dim)
        first = lax.slice_in_dim(array, 0, width, axis=dim)
        before = lax.ppermute(last, axis, up)
        after = lax.ppermute(first, axis, down)
        array = jnp.concatenate([before, array, after], axis=dim)
    return array


def modulation(window_start, section):
    phase_step = (window_start + 2 - section) % 64
    return 1.0 + 0.5 * jnp.sin(2.0 * math.pi * phase_step.astype(jnp.float32) / 64.0)


def advance(extended, diffusivity, velocity, strength):
    middle = extended[:, 1:-1]
    forward_x = extended[:, 2:]
    behind_x = extended[:, :-2]
    wall_zero = jnp.zeros_like(middle[:, :, :1])
    forward_y = jnp.concatenate([middle[:, :, 1:], wall_zero], axis=2)
    behind_y = jnp.concatenate([wall_zero, middle[:, :, :-1]], axis=2)
    forward_z = jnp.roll(middle, -1, axis=3)
    behind_z = jnp.roll(middle, 1, axis=3)
    laplace = forward_x + behind_x + forward_y + behind_y + forward_z + behind_z - 6.0 * middle
    transport = (
        velocity[0] * (forward_x - behind_x)
        + velocity[1] * (forward_y - behind_y)
        + velocity[2] * (forward_z - behind_z)
    )
    return middle + diffusivity * laplace + 0.5 * strength * transport


def body(directions, adjoint, velocity, diffusivity, objective_source, segment_start):
    count_dirs = directions.shape[1]
    stacked = jnp.concatenate([directions[0], adjoint[0][None]], axis=0)
    flow = velocity[0]
    spread = diffusivity[0]
    source = objective_source[0]
    window_start = segment_start[0]
    first_adjoint = source
    for section in (1, 2):
        extended = with_halo(stacked, (("space", 1),), 1)
        stacked = advance(extended, spread, flow, modulation(window_start, section))
        stacked = stacked.at[-1].add(source)
        if section == 1:
            first_adjoint = stacked[-1]
    flattened = stacked.reshape(count_dirs + 1, -1)
    cell_count = flattened.shape[1] * lax.axis_size("space")
    partial_sums = jnp.dot(
        flattened[:count_dirs], flattened[:count_dirs].T, precision=lax.Precision.HIGHEST
    )
    summed = lax.psum(partial_sums, "space") / cell_count
    triangle = jnp.linalg.cholesky(summed)
    inverse = jax.scipy.linalg.solve_triangular(
        triangle, jnp.eye(count_dirs, dtype=triangle.dtype), lower=True
    )
    basis_rows = jnp.dot(inverse, flattened[:count_dirs], precision=lax.Precision.HIGHEST)
    local_along = jnp.dot(basis_rows, flattened[count_dirs], precision=lax.Precision.HIGHEST)
    coefficients = lax.psum(local_along, "space") / cell_count
    shadow = flattened[count_dirs] - jnp.dot(
        coefficients, basis_rows, precision=lax.Precision.HIGHEST
    )
    shadow = shadow.reshape(source.shape)
    gradient = lax.psum_scatter(first_adjoint + shadow, "seg", scatter_dimension=1, tiled=True)
    basis_out = basis_rows.reshape((1,) + directions.shape[1:])
    return (basis_out, triangle.T[None], coefficients[None], shadow[None], gradient)


def solution(mesh):
    return jax.shard_map(
        body,
        mesh=mesh,
        in_specs=(
            P("seg", None, "space", None, None),
            P("seg", "space", None, None),
            P("seg", None, "space", None, None),
            P("seg", "space", None, None),
            P("seg", "space", None, None),
            P("seg"),
        ),
        out_specs=(
            P("seg", None, "space", None, None),
            P("seg", None, None),
            P("seg", None),
            P("seg", "space", None, None),
            P("space", "seg", None),
        ),
        check_vma=False,
    )
```

profile of v0, /device:TPU:0, one launch (start us, length us, event | category | flops | bytes accessed | tf_op | source)
XLA Modules:
  0.0 164.7 jit_solution(1982176983148332593)
XLA Ops:
  7.2 2.8 %copy.51 = f32[1,16,4,64,128]{4,1,3,2,0:T(8,128)S(1)} copy(f32[1,16,4,64,128]{4,3,2,1,0:T(8,128)} %param.10) | data formatting | bytes 4194304 | tf_op args[0]
  10.3 6.1 %collective-permute-start = (f32[17,1,64,128]{3,2,1,0:T(8,128)S(1)}, f32[17,1,64,128]{3,2,1,0:T(8,128)}, u32[]{:S(2)}, u32[]{:S(2)}) collective-permute-start(f32[17,1,64,128]{3,2,1,0:T(8,128)S(1)} %copy.28), channel_id=1, source_target_pairs={{1,0},{2,1},{3,2},{4,3},{5,4},{6,5},{7,6},{0,7},{9,8},{10,9},{11,1... | collective-permute-start | bytes 1671176 | tf_op jit(solution)/shard_map/ppermute | solution.py:17
  17.3 3.0 %fusion.4 = (f32[17,4,63,128]{3,0,2,1:T(8,128)}, f32[17,4,63,128]{3,0,2,1:T(8,128)}) fusion(f32[16,4,64,128]{3,0,2,1:T(8,128)S(1)} %bitcast.60, f32[1,4,64,128]{3,0,2,1:T(1,128)S(1)} %bitcast.67), kind=kLoop, calls=%fused_computation.33 | loop fusion | flops 1096704 | bytes 6615040 | tf_op jit(solution)/shard_map/concatenate | solution.py:47
  23.9 14.1 %collective-permute-done = f32[17,1,64,128]{3,2,1,0:T(8,128)} collective-permute-done((f32[17,1,64,128]{3,2,1,0:T(8,128)S(1)}, f32[17,1,64,128]{3,2,1,0:T(8,128)}, u32[]{:S(2)}, u32[]{:S(2)}) %collective-permute-start) | collective-permute-done | bytes 557088 | tf_op jit(solution)/shard_map/ppermute | solution.py:17
  38.0 1.4 copy.29
  39.4 1.4 copy.31
  40.9 5.5 %multiply_add_fusion.1 = f32[17,4,64,128]{3,0,2,1:T(8,128)S(1)} fusion(f32[1,4,64,128]{3,0,2,1:T(1,128)S(1)} %bitcast.70, f32[16,4,64,128]{3,0,2,1:T(8,128)S(1)} %bitcast.63, f32[17,4,64,127]{3,0,2,1:T(8,128)S(1)} %get-tuple-element.57, f32[17,4,64,1]{3,0,2,1:T(8,128)S(1)} %get-tuple-element.59, f32[17,4,64,1]{3,0,2,1:T(8,128)S(1)} %get-tuple-element.58, ...), kind=kLoop, calls=%fused_computation.32 | loop fusion | flops 14483456 | bytes 14938116 | tf_op jit(solution)/shard_map/add | solution.py:42
  46.6 2.6 %scatter-add.4 = f32[17,4,64,128]{3,0,2,1:T(8,128)S(1)} dynamic-update-slice(f32[17,4,64,128]{3,0,2,1:T(8,128)S(1)} %multiply_add_fusion.1, f32[1,4,64,128]{3,0,2,1:T(1,128)S(1)} %slice_add_fusion.1, s32[]{:T(128)} %constant.129.clone.1, s32[]{:T(128)} %constant.123.clone.1, s32[]{:T(128)} %constant.123.clone.1, s32[]{:T(128)} %constant.123.clone.1) | dynamic-update-slice | bytes 262148 | tf_op jit(solution)/shard_map/scatter-add | solution.py:56
  50.5 4.8 %collective-permute-start.2 = (f32[17,1,64,128]{3,2,1,0:T(8,128)S(1)}, f32[17,1,64,128]{3,2,1,0:T(8,128)S(1)}, u32[]{:S(2)}, u32[]{:S(2)}) collective-permute-start(f32[17,1,64,128]{3,2,1,0:T(8,128)S(1)} %copy.33), channel_id=1, source_target_pairs={{1,0},{2,1},{3,2},{4,3},{5,4},{6,5},{7,6},{0,7},{9,8},{10,9},{11,1... | collective-permute-start | bytes 1671176 | tf_op jit(solution)/shard_map/ppermute | solution.py:17
  55.4 2.0 %fusion.22 = (f32[17,4,63,128]{3,0,2,1:T(8,128)S(1)}, f32[17,4,63,128]{3,0,2,1:T(8,128)}) fusion(f32[17,4,64,128]{3,0,2,1:T(8,128)S(1)} %scatter-add.4), kind=kLoop, calls=%fused_computation.68 | loop fusion | bytes 8773632 | tf_op jit(solution)/shard_map/slice | solution.py:32
  58.4 18.2 %collective-permute-done.2 = f32[17,1,64,128]{3,2,1,0:T(8,128)S(1)} collective-permute-done((f32[17,1,64,128]{3,2,1,0:T(8,128)S(1)}, f32[17,1,64,128]{3,2,1,0:T(8,128)S(1)}, u32[]{:S(2)}, u32[]{:S(2)}) %collective-permute-start.2) | collective-permute-done | bytes 557088 | tf_op jit(solution)/shard_map/ppermute | solution.py:17
  76.6 1.2 copy.34
  77.8 1.2 copy.36
  79.0 5.9 %multiply_add_fusion = f32[17,4,64,128]{3,0,2,1:T(8,128)S(1)} fusion(f32[17,4,64,128]{3,0,2,1:T(8,128)S(1)} %scatter-add.4, f32[17,4,64,127]{3,0,2,1:T(8,128)S(1)} %get-tuple-element.49, f32[17,4,64,1]{3,0,2,1:T(8,128)S(1)} %get-tuple-element.51, f32[17,4,64,1]{3,0,2,1:T(8,128)S(1)} %get-tuple-element.50, f32[17,4,64,127]{3,0,2,1:T(8,128)S(1)} %get-tuple-element.48, ...), kind=kLoop, calls=%fused_computation.31 | loop fusion | flops 12812288 | bytes 14938116 | tf_op jit(solution)/shard_map/add | solution.py:42
  84.9 2.9 %convolution_bitcast_fusion = f32[16,16]{0,1:T(8,128)S(1)} fusion(f32[17,4,64,128]{3,0,2,1:T(8,128)S(1)} %multiply_add_fusion), kind=kOutput, calls=%fused_computation.39 | convolution fusion | flops 100663296 | bytes 2098176 | tf_op jit(solution)/shard_map/dot_general | solution.py:61
  89.0 20.7 %psum.14 = f32[16,16]{0,1:T(8,128)S(1)} all-reduce(f32[16,16]{0,1:T(8,128)S(1)} %convolution_bitcast_fusion), channel_id=1, replica_groups=mesh['seg'=4,'space'=8] {'space'}, use_global_device_ids=true, to_apply=%region_0.1 | all-reduce | flops 256 | bytes 2048 | tf_op jit(solution)/shard_map/psum | solution.py:64
  109.8 1.5 cholesky.17
  112.6 1.2 custom-call.7
  114.7 2.8 %fusion.6 = f32[16,32768]{1,0:T(8,128)S(1)} fusion(f32[16,16]{1,0:T(8,128)S(1)} %fusion.11, f32[2,8,256,128]{3,2,1,0:T(8,128)S(1)} %bitcast.65), kind=kOutput, calls=%fused_computation.35 | convolution fusion | flops 100663296 | bytes 4195328 | tf_op jit(solution)/shard_map/dot_general | solution.py:69
  117.6 2.6 %convolution_bitcast_fusion.1 = f32[16]{0:T(128)S(1)} fusion(f32[16,32768]{1,0:T(8,128)S(1)} %fusion.6, f32[32768,1]{0,1:T(1,128)S(1)} %bitcast.72), kind=kOutput, calls=%fused_computation.40 | convolution fusion | flops 6291456 | bytes 2228288 | tf_op jit(solution)/shard_map/dot_general | solution.py:70
  120.1 17.1 %psum.15 = f32[16]{0:T(128)S(1)} all-reduce(f32[16]{0:T(128)S(1)} %convolution_bitcast_fusion.1), channel_id=1, replica_groups=mesh['seg'=4,'space'=8] {'space'}, use_global_device_ids=true, to_apply=%region_3.4 | all-reduce | flops 16 | bytes 128 | tf_op jit(solution)/shard_map/psum | solution.py:71
  137.3 1.1 fusion.15
  139.8 1.7 %copy.45 = f32[2,8,256,128]{3,2,1,0:T(8,128)} copy(f32[2,8,256,128]{3,1,2,0:T(8,128)S(1)} %bitcast.64) | data formatting | bytes 4194304
  142.0 15.8 %reduce-scatter.2.cloned.1.call-done = f32[4,16,128]{2,1,0:T(8,128)} async-done(((f32[4,64,128]{2,1,0:T(8,128)}), f32[4,16,128]{2,1,0:T(8,128)}) %reduce-scatter.2.cloned.1.call-update) | async-done | bytes 32784 | tf_op jit(solution)/shard_map/reduce_scatter | solution.py:76
  (58 shorter events, 11.8 us)
Async XLA Ops:
  7.2 2.9 %copy-start.3 = (f32[1,4,64,128]{3,2,1,0:T(8,128)S(1)}, f32[1,4,64,128]{3,2,1,0:T(8,128)}, u32[]{:S(2)}) copy-start(f32[1,4,64,128]{3,2,1,0:T(8,128)} %param.11) | copy-start | bytes 393220
  7.2 150.7 %reduce-scatter.2.cloned.1.call-start = ((), (), s32[]{:S(2)}) async-start(), calls=%async_computation.1 | async-start | bytes 163840 | tf_op jit(solution)/shard_map/reduce_scatter | solution.py:76
  10.1 12.7 %copy-start = (f32[1,16,4,64,128]{4,1,3,2,0:T(8,128)}, f32[1,16,4,64,128]{4,1,3,2,0:T(8,128)S(1)}, u32[]{:S(2)}) copy-start(f32[1,16,4,64,128]{4,1,3,2,0:T(8,128)S(1)} %copy.51) | copy-start | bytes 6291460
  10.3 27.7 %collective-permute-start = (f32[17,1,64,128]{3,2,1,0:T(8,128)S(1)}, f32[17,1,64,128]{3,2,1,0:T(8,128)}, u32[]{:S(2)}, u32[]{:S(2)}) collective-permute-start(f32[17,1,64,128]{3,2,1,0:T(8,128)S(1)} %copy.28), channel_id=1, source_target_pairs={{1,0},{2,1},{3,2},{4,3},{5,4},{6,5},{7,6},{0,7},{9,8},{10,9},{11,1... | collective-permute-start | bytes 1671176 | tf_op jit(solution)/shard_map/ppermute | solution.py:17
  17.3 3.0 %copy-start.12 = (f32[1,3,4,64,128]{4,3,2,1,0:T(8,128)S(1)}, f32[1,3,4,64,128]{4,3,2,1,0:T(8,128)}, u32[]{:S(2)}) copy-start(f32[1,3,4,64,128]{4,3,2,1,0:T(8,128)} %param.12) | copy-start | bytes 1179652
  17.3 22.1 %collective-permute-start.1 = (f32[17,1,64,128]{3,2,1,0:T(8,128)}, f32[17,1,64,128]{3,2,1,0:T(8,128)}, u32[]{:S(2)}, u32[]{:S(2)}) collective-permute-start(f32[17,1,64,128]{3,2,1,0:T(8,128)} %copy.30), channel_id=1, source_target_pairs={{0,1},{1,2},{2,3},{3,4},{4,5},{5,6},{6,7},{7,0},{8,9},{9,10},{10,1... | collective-permute-start | bytes 1671176 | tf_op jit(solution)/shard_map/ppermute | solution.py:16
  22.8 18.0 %copy-start.2 = (f32[17,4,63,128]{3,0,2,1:T(8,128)S(1)}, f32[17,4,63,128]{3,0,2,1:T(8,128)}, u32[]{:S(2)}) copy-start(f32[17,4,63,128]{3,0,2,1:T(8,128)} %get-tuple-element.54) | copy-start | bytes 6580228
  22.8 18.0 %copy-start.4 = (f32[4,64,128]{2,1,0:T(8,128)S(1)}, f32[4,64,128]{2,1,0:T(8,128)}, u32[]{:S(2)}) copy-start(f32[4,64,128]{2,1,0:T(8,128)} %get-tuple-element.62) | copy-start | bytes 393220
  22.8 18.0 %copy-start.8 = (f32[1,4,64,128]{3,2,1,0:T(8,128)S(1)}, f32[1,4,64,128]{3,2,1,0:T(8,128)}, u32[]{:S(2)}) copy-start(f32[1,4,64,128]{3,2,1,0:T(8,128)} %param.13) | copy-start | bytes 393220
  23.9 17.0 %copy-start.1 = (f32[1,16,4,64,128]{4,1,3,2,0:T(8,128)S(1)}, f32[1,16,4,64,128]{4,1,3,2,0:T(8,128)}, u32[]{:S(2)}) copy-start(f32[1,16,4,64,128]{4,1,3,2,0:T(8,128)} %copy-done) | copy-start | bytes 6291460
  40.9 5.6 %copy-start.10 = (f32[1,4,64,128]{3,2,1,0:T(8,128)S(1)}, f32[1,4,64,128]{3,2,1,0:T(8,128)}, u32[]{:S(2)}) copy-start(f32[1,4,64,128]{3,2,1,0:T(8,128)} %param.14) | copy-start | bytes 393220
  46.6 3.7 %copy-start.6 = (f32[1,4,64,128]{3,0,2,1:T(1,128)}, f32[1,4,64,128]{3,0,2,1:T(1,128)S(1)}, u32[]{:S(2)}) copy-start(f32[1,4,64,128]{3,0,2,1:T(1,128)S(1)} %slice_add_fusion.1) | copy-start | bytes 393220
  50.5 26.0 %collective-permute-start.2 = (f32[17,1,64,128]{3,2,1,0:T(8,128)S(1)}, f32[17,1,64,128]{3,2,1,0:T(8,128)S(1)}, u32[]{:S(2)}, u32[]{:S(2)}) collective-permute-start(f32[17,1,64,128]{3,2,1,0:T(8,128)S(1)} %copy.33), channel_id=1, source_target_pairs={{1,0},{2,1},{3,2},{4,3},{5,4},{6,5},{7,6},{0,7},{9,8},{10,9},{11,1... | collective-permute-start | bytes 1671176 | tf_op jit(solution)/shard_map/ppermute | solution.py:17
  55.4 22.4 %collective-permute-start.3 = (f32[17,1,64,128]{3,2,1,0:T(8,128)S(1)}, f32[17,1,64,128]{3,2,1,0:T(8,128)S(1)}, u32[]{:S(2)}, u32[]{:S(2)}) collective-permute-start(f32[17,1,64,128]{3,2,1,0:T(8,128)S(1)} %copy.35), channel_id=1, source_target_pairs={{0,1},{1,2},{2,3},{3,4},{4,5},{5,6},{6,7},{7,0},{8,9},{9,10},{10,1... | collective-permute-start | bytes 1671176 | tf_op jit(solution)/shard_map/ppermute | solution.py:16
  57.4 21.7 %copy-start.5 = (f32[4,64,128]{2,1,0:T(8,128)S(1)}, f32[4,64,128]{2,1,0:T(8,128)}, u32[]{:S(2)}) copy-start(f32[4,64,128]{2,1,0:T(8,128)} %get-tuple-element.62) | copy-start | bytes 393220
  57.4 21.7 %copy-start.9 = (f32[1,4,64,128]{3,2,1,0:T(8,128)S(1)}, f32[1,4,64,128]{3,2,1,0:T(8,128)}, u32[]{:S(2)}) copy-start(f32[1,4,64,128]{3,2,1,0:T(8,128)} %param.13) | copy-start | bytes 393220
  117.6 20.9 %copy-start.7 = (f32[1,4,64,128]{3,0,2,1:T(1,128)S(1)}, f32[1,4,64,128]{3,0,2,1:T(1,128)}, u32[]{:S(2)}) copy-start(f32[1,4,64,128]{3,0,2,1:T(1,128)} %copy-done.6) | copy-start | bytes 393220
  138.4 19.4 %copy-start.11 = (f32[32768]{0:T(1024)}, f32[32768]{0:T(1024)S(1)}, u32[]{:S(2)}) copy-start(f32[32768]{0:T(1024)S(1)} %sub.40) | copy-start | bytes 393220
Sparse Core Ops, SparseCore 0:
  139.3 18.5 reduce-scatter.1
where the time goes:
time: 165 us
  waiting for transfers between devices  48.1 us (29%)
  blocking collectives  37.8 us (23%)
  other arithmetic  22.9 us (14%)
  local copies, waits for them, and re-layouts  20.1 us (12%)
  between operations  15.2 us (9%)
  starting transfers between devices  11 us (7%)
  matrix products  9.58 us (6%)
    ppermute x2, waiting for transfers between devices, with_halo(): after = lax.ppermute(first, axis, down)  32.3 us
    psum x1, blocking collectives, body(): summed = lax.psum(partial_sums, 'space') / cell_count  20.7 us
    psum x1, blocking collectives, body(): coefficients = lax.psum(local_along, 'space') / cell_count  17.1 us
    reduce_scatter x1, waiting for transfers between devices, body(): lax.psum_scatter(first_adjoint + shadow, 'seg', scatter_dimension=1, tile...  15.8 us
    add x2, other arithmetic, advance(): return middle + diffusivity * laplace + 0.5 * strength * transport  11.4 us
    ppermute x2, starting transfers between devices, with_halo(): after = lax.ppermute(first, axis, down)  10.9 us
    unnamed x29, local copies, waits for them, and re-layouts  5.3 us
    concatenate x4, other arithmetic, body(): stacked = jnp.concatenate([directions[0], adjoint[0][None]], axis=0)  5.09 us
  transfers between devices with their start and end apart: 5, of which 3 were waited for; matrix products, arithmetic and copies ran while one was open for 9% of the time, Pallas kernels for 0%

commit v1 on v0

v1 whole, which is shorter than its diff:
```python
import functools
import math

import jax
import jax.numpy as jnp
from jax import lax
from jax.experimental import pallas as pl
from jax.experimental.pallas import tpu as pltpu
from jax.sharding import PartitionSpec as P

SUB = 8
HIGH = lax.Precision.HIGHEST
VMEM_SPEC = pl.BlockSpec(memory_space=pltpu.VMEM)
SMEM_SPEC = pl.BlockSpec(memory_space=pltpu.SMEM)
ANY_SPEC = pl.BlockSpec(memory_space=pl.ANY)


def modulation(window_start, section):
    phase_step = (window_start + 2 - section) % 64
    return 1.0 + 0.5 * jnp.sin(2.0 * math.pi * phase_step.astype(jnp.float32) / 64.0)


def call(body, name, outs, specs, args, scratch=(), flops=0, moved=0):
    return pl.pallas_call(
        body,
        out_shape=outs,
        in_specs=specs,
        out_specs=jax.tree.map(lambda _: VMEM_SPEC, outs) if name != "pack" else [ANY_SPEC] * len(outs),
        scratch_shapes=scratch,
        name=name,
        cost_estimate=pl.CostEstimate(flops=flops, transcendentals=0, bytes_accessed=moved),
        compiler_params=pltpu.CompilerParams(vmem_limit_bytes=40 * 1024 * 1024),
    )(*args)


def layer_of(odd, position, layers):
    return position + odd * (layers - 1 - 2 * position)


def pack_kernel(count, layers, place, dirs, adj, first, second, sems):
    odd = place[0]
    copies = []
    for slot, (out, position) in enumerate(((first, layers - 1), (second, 0))):
        layer = layer_of(odd, position, layers)
        copies.append(pltpu.make_async_copy(dirs.at[:, layer], out.at[pl.ds(0, count)], sems.at[slot, 0]))
        copies.append(pltpu.make_async_copy(adj.at[layer], out.at[count], sems.at[slot, 1]))
    for copy in copies:
        copy.start()
    for copy in copies:
        copy.wait()


def coefficients_at(vel, dif, layer, half, sign, rows, first_row, last_row):
    spread = dif[layer, rows, :]
    ax = (half * sign) * vel[0, layer, rows, :]
    ay = half * vel[1, layer, rows, :]
    az = half * vel[2, layer, rows, :]
    up, down = spread + ay, spread - ay
    row = lax.broadcasted_iota(jnp.int32, spread.shape, 0)
    if last_row:
        up = jnp.where(row == spread.shape[0] - 1, 0.0, up)
    if first_row:
        down = jnp.where(row == 0, 0.0, down)
    return 1.0 - 6.0 * spread, spread + ax, spread - ax, up, down, spread + az, spread - az


def stencil(vel, dif, src, layer, half, sign, fields, rows_total, width, middle, toward, away, store):
    for base in range(0, rows_total, SUB):
        rows = slice(base, base + SUB)
        first_row, last_row = base == 0, base + SUB == rows_total
        c0, cxp, cxm, cyp, cym, czp, czm = coefficients_at(
            vel, dif, layer, half, sign, rows, first_row, last_row
        )
        for field in range(fields):
            tile = middle(field, rows)
            if last_row:
                above = pltpu.roll(tile, SUB - 1, 0)
            else:
                above = middle(field, slice(base + 1, base + 1 + SUB))
            if first_row:
                below = pltpu.roll(tile, 1, 0)
            else:
                below = middle(field, slice(base - 1, base - 1 + SUB))
            total = c0 * tile + cxp * toward(field, rows) + cxm * away(field, rows)
            total = total + (cyp * above + cym * below)
            total = total + (czp * pltpu.roll(tile, width - 1, 1) + czm * pltpu.roll(tile, 1, 1))
            if field == fields - 1:
                total = total + src[layer, rows, :]
            store(field, rows, total)


def reader(dirs, adj, count, layer):
    def read(field, rows):
        return dirs[field, layer, rows, :] if field < count else adj[layer, rows, :]

    return read


def plain(ref, *lead):
    def read(field, rows):
        return ref[(*lead, field, rows, slice(None))]

    return read


def writer(ref, *lead):
    def write(field, rows, value):
        ref[(*lead, field, rows, slice(None))] = value

    return write


def first_kernel(count, layers, place, half, dirs, adj, halo, vel, dif, src, edge, inner):
    odd, sign = place[0], (1 - 2 * place[0]).astype(jnp.float32)
    _, _, ny, nz = dirs.shape
    for position in range(layers - 1, 0, -1):
        layer = layer_of(odd, position, layers)
        last = position == layers - 1
        toward = plain(halo) if last else reader(dirs, adj, count, layer_of(odd, position + 1, layers))
        stencil(
            vel, dif, src, layer, half[0], sign, count + 1, ny, nz,
            reader(dirs, adj, count, layer), toward,
            reader(dirs, adj, count, layer_of(odd, position - 1, layers)),
            writer(edge) if last else writer(inner, position - 1),
        )


def second_kernel(count, layers, place, half, dirs, adj, halo, vel, dif, src, edge):
    odd, sign = place[0], (1 - 2 * place[0]).astype(jnp.float32)
    _, _, ny, nz = dirs.shape
    layer = layer_of(odd, 0, layers)
    stencil(
        vel, dif, src, layer, half[0], sign, count + 1, ny, nz,
        reader(dirs, adj, count, layer), reader(dirs, adj, count, layer_of(odd, 1, layers)), plain(halo),
        writer(edge),
    )


def add_products(ref, lead, count, ny, nz, total):
    step = 2 * SUB if ny % (2 * SUB) == 0 else SUB
    for base in range(0, ny, step):
        parts = [
            ref[(*lead, slice(None), slice(row, row + SUB), slice(None))].reshape((count + 1) * SUB, nz)
            for row in range(base, base + step, SUB)
        ]
        block = jnp.concatenate(parts, axis=1) if len(parts) > 1 else parts[0]
        total = total + lax.dot_general(
            block[: count * SUB], block, (((1,), (1,)), ((), ())),
            precision=HIGH, preferred_element_type=jnp.float32,
        )
    return total


def third_kernel(count, layers, place, half, bottom, inner, top, halo, vel, dif, src, out, products):
    odd, sign = place[0], (1 - 2 * place[0]).astype(jnp.float32)
    _, ny, nz = bottom.shape

    def at(position):
        if position == 0:
            return plain(bottom)
        if position == layers:
            return plain(halo)
        return plain(top) if position == layers - 1 else plain(inner, position - 1)

    total = jnp.zeros(products.shape, jnp.float32)
    for position in range(1, layers):
        layer = layer_of(odd, position, layers)
        stencil(
            vel, dif, src, layer, half[1], sign, count + 1, ny, nz,
            at(position), at(position + 1), at(position - 1), writer(out, position - 1),
        )
    for position in range(1, layers):
        total = add_products(out, (position - 1,), count, ny, nz, total)
    products[...] = total


def fourth_kernel(count, layers, place, half, bottom, above, halo, vel, dif, src, products, out, gram):
    odd, sign = place[0], (1 - 2 * place[0]).astype(jnp.float32)
    _, ny, nz = bottom.shape
    stencil(
        vel, dif, src, layer_of(odd, 0, layers), half[1], sign, count + 1, ny, nz,
        plain(bottom), plain(above), plain(halo), writer(out),
    )
    total = add_products(out, (), count, ny, nz, products[...])
    rows = lax.broadcasted_iota(jnp.int32, total.shape, 0)
    columns = lax.broadcasted_iota(jnp.int32, total.shape, 1)
    total = jnp.where(rows % SUB == columns % SUB, total, 0.0)
    total = total.reshape(count, SUB, total.shape[1]).sum(axis=1)
    width = gram.shape[1]
    gather = (
        lax.broadcasted_iota(jnp.int32, (total.shape[1], width), 0) // SUB
        == lax.broadcasted_iota(jnp.int32, (total.shape[1], width), 1)
    ).astype(jnp.float32)
    gram[...] = jnp.dot(total, gather, precision=HIGH, preferred_element_type=jnp.float32)


def solve_kernel(count, layers, pieces, cells, place, gram, upper, bottom, early, solved, shadow, *parts):
    odd, seg = place[0], place[1]
    _, ny, nz = bottom.shape
    shape = gram.shape
    row = lax.broadcasted_iota(jnp.int32, shape, 0)
    lane = lax.broadcasted_iota(jnp.int32, shape, 1)
    table = jnp.where(lane <= count, gram[...] / cells, 0.0)
    table = jnp.where(lane == row + count + 1, 1.0, table)
    for k in range(count):
        pivot_row = table[k : k + 1, :]
        root = jnp.sqrt(pivot_row[:, k : k + 1])
        scaled = pivot_row / root
        column = table[:, k : k + 1] / root
        table = jnp.where(row == k, scaled, jnp.where(row > k, table - column * scaled, table))
    table = jnp.where((lane < count) & (lane < row), 0.0, table)
    solved[...] = table
    weights = jnp.sum(table[:, count : count + 1] * table, axis=0, keepdims=True)
    splat = [
        jnp.broadcast_to(weights[:, count + 1 + j : count + 2 + j], (SUB, nz)) for j in range(count)
    ]
    for position in range(layers):
        layer = layer_of(odd, position, layers)
        read = plain(bottom) if position == 0 else plain(upper, position - 1)
        for base in range(0, ny, SUB):
            rows = slice(base, base + SUB)
            total = read(count, rows)
            for j in range(count):
                total = total - splat[j] * read(j, rows)
            shadow[layer, rows, :] = total
    step = ny // pieces
    for k, part in enumerate(parts):
        begin = pl.multiple_of((seg ^ k) * step, step)
        rows = pl.ds(begin, step)
        part[...] = shadow[:, rows, :] + early[:, rows, :]


def basis_kernel(count, layers, place, solved, upper, bottom, out):
    odd = place[0]
    _, ny, nz = bottom.shape
    block = min(ny, 8 * SUB)
    for position in range(layers):
        layer = layer_of(odd, position, layers)
        read = plain(bottom) if position == 0 else plain(upper, position - 1)
        for base in range(0, ny, block):
            rows = slice(base, base + block)
            for i in range(count):
                total = solved[i, count + 1] * read(0, rows)
                for j in range(1, i + 1):
                    total = total + solved[i, count + 1 + j] * read(j, rows)
                out[i, layer, rows, :] = total


def body(directions, adjoint, velocity, diffusivity, objective_source, segment_start):
    dirs, adj, vel, dif, src = (
        directions[0], adjoint[0], velocity[0], diffusivity[0], objective_source[0],
    )
    count, layers, ny, nz = dirs.shape
    spaces, segs = lax.axis_size("space"), lax.axis_size("seg")
    assert spaces % 2 == 0 and layers >= 2 and segs & (segs - 1) == 0 and spaces & (spaces - 1) == 0
    odd = lax.axis_index("space") % 2
    place = jnp.stack([odd, lax.axis_index("seg")]).astype(jnp.int32)
    half = jnp.stack([0.5 * modulation(segment_start[0], k) for k in (1, 2)])
    pair_one = [(i, i ^ 1) for i in range(spaces)]
    pair_two = [(i, (i + 1) % spaces if i % 2 else (i - 1) % spaces) for i in range(spaces)]
    f32 = functools.partial(jax.ShapeDtypeStruct, dtype=jnp.float32)
    edge = f32((count + 1, ny, nz))
    field_bytes = 4 * (count + 1) * ny * nz
    vs, ss = VMEM_SPEC, SMEM_SPEC

    send_one, send_two = call(
        functools.partial(pack_kernel, count, layers), "pack", [edge, edge],
        [ss, ANY_SPEC, ANY_SPEC], (place, dirs, adj),
        scratch=[pltpu.SemaphoreType.DMA((2, 2))], moved=4 * field_bytes,
    )
    halo_one = lax.ppermute(send_one, "space", pair_one)
    halo_two = lax.ppermute(send_two, "space", pair_two)
    top, inner = call(
        functools.partial(first_kernel, count, layers), "first",
        [edge, f32((max(layers - 2, 1), count + 1, ny, nz))],
        [ss, ss, vs, vs, vs, vs, vs, vs], (place, half, dirs, adj, halo_one, vel, dif, src),
        flops=13 * layers * field_bytes // 4, moved=2 * layers * field_bytes,
    )
    next_one = lax.ppermute(top, "space", pair_one)
    bottom = call(
        functools.partial(second_kernel, count, layers), "second", edge,
        [ss, ss, vs, vs, vs, vs, vs, vs], (place, half, dirs, adj, halo_two, vel, dif, src),
        flops=13 * field_bytes // 4, moved=layers * field_bytes,
    )
    next_two = lax.ppermute(bottom, "space", pair_two)
    products_shape = f32((count * SUB, (count + 1) * SUB))
    upper, products = call(
        functools.partial(third_kernel, count, layers), "third",
        [f32((layers - 1, count + 1, ny, nz)), products_shape],
        [ss, ss] + [vs] * 7, (place, half, bottom, inner, top, next_one, vel, dif, src),
        flops=60 * layers * field_bytes // 4, moved=2 * layers * field_bytes,
    )
    lowest, gram = call(
        functools.partial(fourth_kernel, count, layers), "fourth", [edge, f32((count, 128))],
        [ss, ss] + [vs] * 7,
        (place, half, bottom, inner[0] if layers > 2 else top, next_two, vel, dif, src, products),
        flops=60 * field_bytes // 4, moved=4 * field_bytes,
    )
    reach = 1
    while reach < spaces:
        gram = gram + lax.ppermute(gram, "space", [(i, i ^ reach) for i in range(spaces)])
        reach *= 2
    early_layers = [top[count]]
    early_layers = [bottom[count]] + [inner[p, count] for p in range(layers - 2)] + early_layers
    early = jnp.stack(early_layers)
    early = jnp.where(odd == 1, early[::-1], early)
    piece = f32((layers, ny // segs, nz))
    solved, shadow, *parts = call(
        functools.partial(solve_kernel, count, layers, segs, float(layers * ny * nz * spaces)), "solve",
        [f32((count, 128)), f32((layers, ny, nz))] + [piece] * segs,
        [ss] + [vs] * 4, (place, gram, upper, lowest, early),
        flops=2 * layers * field_bytes, moved=layers * field_bytes,
    )
    gradient = parts[0]
    for k in range(1, segs):
        gradient = gradient + lax.ppermute(parts[k], "seg", [(i, i ^ k) for i in range(segs)])
    basis = call(
        functools.partial(basis_kernel, count, layers), "basis", f32((count, layers, ny, nz)),
        [ss, ss, vs, vs], (place, solved, upper, lowest),
        flops=count * layers * field_bytes // 4, moved=2 * layers * field_bytes,
    )
    return (
        basis[None], solved[None, :, :count], solved[None, :, count], shadow[None], gradient,
    )


def solution(mesh):
    return jax.shard_map(
        body,
        mesh=mesh,
        in_specs=(
            P("seg", None, "space", None, None),
            P("seg", "space", None, None),
            P("seg", None, "space", None, None),
            P("seg", "space", None, None),
            P("seg", "space", None, None),
            P("seg"),
        ),
        out_specs=(
            P("seg", None, "space", None, None),
            P("seg", None, None),
            P("seg", None),
            P("seg", "space", None, None),
            P("space", "seg", None),
        ),
        check_vma=False,
    )
```

time: 165 us -> 91.7 us (0.56)
  blocking collectives: 37.8 us -> 0 us
  other arithmetic: 22.9 us -> 0.81 us
  Pallas kernels: 0 us -> 17 us
  between operations: 15.2 us -> 1.57 us
  local copies, waits for them, and re-layouts: 20.1 us -> 8.57 us
  matrix products: 9.58 us -> 0 us
  starting transfers between devices: 11 us -> 19.3 us
  waiting for transfers between devices: 48.1 us -> 44 us
    psum x2 -> x0, blocking collectives: 37.8 us -> none  [the longest x1 20.7 us: body(): summed = lax.psum(partial_sums, 'space') / cell_count]
    pallas_call x0 -> x7, Pallas kernels: none -> 17 us  [call(): pl.pallas_call(body, out_shape=outs, in_specs=specs, out_specs=jax.tree.m...]
    reduce_scatter x1 -> x0, waiting for transfers between devices: 15.8 us -> none  [body(): lax.psum_scatter(first_adjoint + shadow, 'seg', scatter_dimension=1, tile...]
    add x5 -> x4, other arithmetic: 13.3 us -> 0.64 us  [the longest x1 0.63 us: body(): gradient + lax.ppermute(parts[k], 'seg', [(i, i ^ k) for i in range(segs)])]
    ppermute x4 -> x10, waiting for transfers between devices: 32.3 us -> 44 us  [the longest x1 20.3 us: body(): halo_one = lax.ppermute(send_one, 'space', pair_one)]
    dot_general x4 -> x0, matrix products: 9.39 us -> none  [the longest x1 2.87 us: body(): jnp.dot(flattened[:count_dirs], flattened[:count_dirs].T, precision=lax.P...]
    ppermute x4 -> x10, starting transfers between devices: 10.9 us -> 19.3 us  [the longest x3 5.47 us: body(): lax.ppermute(gram, 'space', [(i, i ^ reach) for i in range(spaces)])]
    ppermute x4 -> x0, local copies, waits for them, and re-layouts: 5.23 us -> none  [the longest x2 2.63 us: with_halo(): before = lax.ppermute(last, axis, up)]
  transfers between devices with their start and end apart: 5 -> 10, of which waited for: 3 -> 5; matrix products, arithmetic and copies ran while one was open for 9% -> 4% of each run, Pallas kernels for 0% -> 11%
where the time goes in v1:
time: 91.7 us; the launch traced here: 91.2 us
  waiting for transfers between devices  44 us (48%)
  starting transfers between devices  19.3 us (21%)
  Pallas kernels  17 us (19%)
  local copies, waits for them, and re-layouts  8.57 us (9%)
  between operations  1.57 us (2%)
    ppermute x1, waiting for transfers between devices, body(): halo_one = lax.ppermute(send_one, 'space', pair_one)  20.3 us
    ppermute x1, waiting for transfers between devices, body(): next_one = lax.ppermute(top, 'space', pair_one)  18 us
    pallas_call x7, Pallas kernels, call(): pl.pallas_call(body, out_shape=outs, in_specs=specs, out_specs=jax.tree.m...  17 us
    ppermute x3, waiting for transfers between devices, body(): lax.ppermute(gram, 'space', [(i, i ^ reach) for i in range(spaces)])  5.67 us
    ppermute x3, starting transfers between devices, body(): lax.ppermute(gram, 'space', [(i, i ^ reach) for i in range(spaces)])  5.47 us
    unnamed x24, local copies, waits for them, and re-layouts  5.32 us
    ppermute x1, starting transfers between devices, body(): next_two = lax.ppermute(bottom, 'space', pair_two)  3.61 us
    ppermute x1, starting transfers between devices, body(): halo_two = lax.ppermute(send_two, 'space', pair_two)  3.54 us
  transfers between devices with their start and end apart: 10, of which 5 were waited for; matrix products, arithmetic and copies ran while one was open for 4% of the time, Pallas kernels for 11%

profile of v1, /device:TPU:0, one launch (start us, length us, event | category | flops | bytes accessed | tf_op | source)
XLA Modules:
  0.0 91.2 jit_solution(8451488938082355155)
XLA Ops:
  0.7 1.6 %copy-done = f32[1,16,4,64,128]{4,3,2,1,0:T(8,128)S(1)} copy-done((f32[1,16,4,64,128]{4,3,2,1,0:T(8,128)S(1)}, f32[1,16,4,64,128]{4,3,2,1,0:T(8,128)}, u32[]{:S(2)}) %copy-start) | copy-done | bytes 2097176
  2.3 0.9 copy-done.9
  3.2 1.6 %pack.1 = (f32[17,64,128]{2,1,0:T(8,128)}, f32[17,64,128]{2,1,0:T(8,128)}) custom-call(s32[2]{0:T(128)S(1)} %pad_add_fusion.place, f32[16,4,64,128]{3,2,1,0:T(8,128)S(1)} %bitcast.25, f32[4,64,128]{2,1,0:T(8,128)S(1)} %bitcast.40), custom_call_target="tpu_custom_call" | custom-call | bytes 2228224 | tf_op jit(solution)/shard_map/pack/pallas_call | solution.py:24
  4.8 3.1 %collective-permute-start.1 = (f32[17,64,128]{2,1,0:T(8,128)}, f32[17,64,128]{2,1,0:T(8,128)S(1)}, u32[]{:S(2)}, u32[]{:S(2)}) collective-permute-start(f32[17,64,128]{2,1,0:T(8,128)} %get-tuple-element.20), channel_id=1, source_target_pairs={{0,1},{1,0},{2,3},{3,2},{4,5},{5,4},{6,7},{7,6},{8,9},{9,8},{10,11... | collective-permute-start | bytes 1671176 | tf_op jit(solution)/shard_map/ppermute | solution.py:271
  7.9 3.5 %collective-permute-start = (f32[17,64,128]{2,1,0:T(8,128)}, f32[17,64,128]{2,1,0:T(8,128)}, u32[]{:S(2)}, u32[]{:S(2)}) collective-permute-start(f32[17,64,128]{2,1,0:T(8,128)} %get-tuple-element.19), channel_id=1, source_target_pairs={{0,7},{1,2},{2,1},{3,4},{4,3},{5,6},{6,5},{7,0},{8,15},{9,10},{10,... | collective-permute-start | bytes 1671176 | tf_op jit(solution)/shard_map/ppermute | solution.py:272
  12.3 20.3 %collective-permute-done.1.halo = f32[17,64,128]{2,1,0:T(8,128)S(1)} collective-permute-done((f32[17,64,128]{2,1,0:T(8,128)}, f32[17,64,128]{2,1,0:T(8,128)S(1)}, u32[]{:S(2)}, u32[]{:S(2)}) %collective-permute-start.1) | collective-permute-done | bytes 557088 | tf_op jit(solution)/shard_map/ppermute | solution.py:271
  32.6 1.0 %copy-done.2 = f32[1,3,4,64,128]{4,3,2,1,0:T(8,128)S(1)} copy-done((f32[1,3,4,64,128]{4,3,2,1,0:T(8,128)S(1)}, f32[1,3,4,64,128]{4,3,2,1,0:T(8,128)}, u32[]{:S(2)}) %copy-start.2) | copy-done | bytes 393240
  35.5 2.3 %first.1 = (f32[17,64,128]{2,1,0:T(8,128)}, f32[2,17,64,128]{3,2,1,0:T(8,128)S(1)}) custom-call(s32[2]{0:T(128)S(1)} %pad_add_fusion.place, f32[2]{0:T(128)S(1)} %pad_maximum_fusion.1.half, f32[16,4,64,128]{3,2,1,0:T(8,128)S(1)} %bitcast.26, f32[4,64,128]{2,1,0:T(8,128)S(1)} %bitcast.41, f32[17,64,128]{2,1,0:T(8,128)S(1)} %collective-permute-done.1.halo, ...), custom_call_target="tpu_custom_call" | custom-call | flops 7241728 | bytes 4456448 | tf_op jit(solution)/shard_map/first/pallas_call | solution.py:24
  37.8 1.7 %collective-permute-start.3 = (f32[17,64,128]{2,1,0:T(8,128)}, f32[17,64,128]{2,1,0:T(8,128)}, u32[]{:S(2)}, u32[]{:S(2)}) collective-permute-start(f32[17,64,128]{2,1,0:T(8,128)} %get-tuple-element.22.top), channel_id=1, source_target_pairs={{0,1},{1,0},{2,3},{3,2},{4,5},{5,4},{6,7},{7,6},{8,9},{9,8},{10,11... | collective-permute-start | bytes 1671176 | tf_op jit(solution)/shard_map/ppermute | solution.py:279
  39.5 1.4 %second.1.bottom = f32[17,64,128]{2,1,0:T(8,128)S(1)} custom-call(s32[2]{0:T(128)S(1)} %pad_add_fusion.place, f32[2]{0:T(128)S(1)} %pad_maximum_fusion.1.half, f32[16,4,64,128]{3,2,1,0:T(8,128)S(1)} %bitcast.27, f32[4,64,128]{2,1,0:T(8,128)S(1)} %bitcast.42, f32[17,64,128]{2,1,0:T(8,128)} %collective-permute-done.halo, f32[3,4,64,128]{3,2,1,0:T(8,128)S(1)} %bitcast.29, ...), custom_call_target="tpu_custom_call" | custom-call | flops 1810432 | bytes 2228224 | tf_op jit(solution)/shard_map/second/pallas_call | solution.py:24
  41.0 3.6 %collective-permute-start.2 = (f32[17,64,128]{2,1,0:T(8,128)S(1)}, f32[17,64,128]{2,1,0:T(8,128)}, u32[]{:S(2)}, u32[]{:S(2)}) collective-permute-start(f32[17,64,128]{2,1,0:T(8,128)S(1)} %second.1.bottom), channel_id=1, source_target_pairs={{0,7},{1,2},{2,1},{3,4},{4,3},{5,6},{6,5},{7,0},{8,15},{9,10},{10,... | collective-permute-start | bytes 1671176 | tf_op jit(solution)/shard_map/ppermute | solution.py:285
  44.6 1.2 %slice_bitcast_fusion.above = f32[17,64,128]{2,1,0:T(8,128)S(1)} fusion(f32[2,17,64,128]{3,2,1,0:T(8,128)} %copy-done.4), kind=kLoop, calls=%fused_computation | loop fusion | bytes 1114112 | tf_op jit(solution)/shard_map/squeeze | solution.py:296
  45.8 18.0 %collective-permute-done.3.halo = f32[17,64,128]{2,1,0:T(8,128)} collective-permute-done((f32[17,64,128]{2,1,0:T(8,128)}, f32[17,64,128]{2,1,0:T(8,128)}, u32[]{:S(2)}, u32[]{:S(2)}) %collective-permute-start.3) | collective-permute-done | bytes 557088 | tf_op jit(solution)/shard_map/ppermute | solution.py:279
  63.8 3.3 %third.1 = (f32[3,17,64,128]{3,2,1,0:T(8,128)S(1)}, f32[128,136]{1,0:T(8,128)S(1)}) custom-call(s32[2]{0:T(128)S(1)} %pad_add_fusion.place, f32[2]{0:T(128)S(1)} %pad_maximum_fusion.1.half, f32[17,64,128]{2,1,0:T(8,128)S(1)} %second.1.bottom, f32[2,17,64,128]{3,2,1,0:T(8,128)S(1)} %copy-done.5, f32[17,64,128]{2,1,0:T(8,128)} %get-tuple-element.22.top, ...), custom_call_target="tpu_custom_call" | custom-call | flops 33423360 | bytes 4456448 | tf_op jit(solution)/shard_map/third/pallas_call | solution.py:24
  67.1 2.1 %fourth.1 = (f32[17,64,128]{2,1,0:T(8,128)S(1)}, f32[16,128]{1,0:T(8,128)S(1)}) custom-call(s32[2]{0:T(128)S(1)} %pad_add_fusion.place, f32[2]{0:T(128)S(1)} %pad_maximum_fusion.1.half, f32[17,64,128]{2,1,0:T(8,128)S(1)} %second.1.bottom, f32[17,64,128]{2,1,0:T(8,128)S(1)} %slice_bitcast_fusion.above, f32[17,64,128]{2,1,0:T(8,128)} %collective-permute-done.2.halo, ...), custom_call_target="tpu_custom_call" | custom-call | flops 8355840 | bytes 2228224 | tf_op jit(solution)/shard_map/fourth/pallas_call | solution.py:24
  69.2 1.5 %collective-permute-start.4 = (f32[16,128]{1,0:T(8,128)S(1)}, f32[16,128]{1,0:T(8,128)S(1)}, u32[]{:S(2)}, u32[]{:S(2)}) collective-permute-start(f32[16,128]{1,0:T(8,128)S(1)} %get-tuple-element.24), channel_id=1, source_target_pairs={{0,1},{1,0},{2,3},{3,2},{4,5},{5,4},{6,7},{7,6},{8,9},{9,8},{10,11... | collective-permute-start | bytes 24584 | tf_op jit(solution)/shard_map/ppermute | solution.py:301
  71.4 1.4 %collective-permute-done.4 = f32[16,128]{1,0:T(8,128)S(1)} collective-permute-done((f32[16,128]{1,0:T(8,128)S(1)}, f32[16,128]{1,0:T(8,128)S(1)}, u32[]{:S(2)}, u32[]{:S(2)}) %collective-permute-start.4) | collective-permute-done | bytes 8224 | tf_op jit(solution)/shard_map/ppermute | solution.py:301
  72.8 1.5 %collective-permute-start.5 = (f32[16,128]{1,0:T(8,128)S(1)}, f32[16,128]{1,0:T(8,128)S(1)}, u32[]{:S(2)}, u32[]{:S(2)}) collective-permute-start(f32[16,128]{1,0:T(8,128)S(1)} %add.47), channel_id=1, source_target_pairs={{0,2},{1,3},{2,0},{3,1},{4,6},{5,7},{6,4},{7,5},{8,10},{9,11},{10,... | collective-permute-start | bytes 24584 | tf_op jit(solution)/shard_map/ppermute | solution.py:301
  74.4 2.2 %collective-permute-done.5 = f32[16,128]{1,0:T(8,128)S(1)} collective-permute-done((f32[16,128]{1,0:T(8,128)S(1)}, f32[16,128]{1,0:T(8,128)S(1)}, u32[]{:S(2)}, u32[]{:S(2)}) %collective-permute-start.5) | collective-permute-done | bytes 8224 | tf_op jit(solution)/shard_map/ppermute | solution.py:301
  76.6 2.5 %collective-permute-start.6 = (f32[16,128]{1,0:T(8,128)S(1)}, f32[16,128]{1,0:T(8,128)S(1)}, u32[]{:S(2)}, u32[]{:S(2)}) collective-permute-start(f32[16,128]{1,0:T(8,128)S(1)} %add.48), channel_id=1, source_target_pairs={{0,4},{1,5},{2,6},{3,7},{4,0},{5,1},{6,2},{7,3},{8,12},{9,13},{10,... | collective-permute-start | bytes 24584 | tf_op jit(solution)/shard_map/ppermute | solution.py:301
  79.0 2.1 %collective-permute-done.6 = f32[16,128]{1,0:T(8,128)S(1)} collective-permute-done((f32[16,128]{1,0:T(8,128)S(1)}, f32[16,128]{1,0:T(8,128)S(1)}, u32[]{:S(2)}, u32[]{:S(2)}) %collective-permute-start.6) | collective-permute-done | bytes 8224 | tf_op jit(solution)/shard_map/ppermute | solution.py:301
  81.1 3.0 %solve.1 = (f32[16,128]{1,0:T(8,128)S(1)}, f32[4,64,128]{2,1,0:T(8,128)}, f32[4,16,128]{2,1,0:T(8,128)S(1)}, f32[4,16,128]{2,1,0:T(8,128)S(1)}, f32[4,16,128]{2,1,0:T(8,128)S(1)}, /*index=5*/f32[4,16,128]{2,1,0:T(8,128)S(1)}) custom-call(s32[2]{0:T(128)S(1)} %pad_add_fusion.place, f32[16,128]{1,0:T(8,128)S(1)} %add.49.gram, ...), custom_call_target="tpu_custom_call" | custom-call | flops 4456448 | bytes 2228224 | tf_op jit(solution)/shard_map/solve/pallas_call | solution.py:24
  84.1 1.4 %collective-permute-start.8 = (f32[4,16,128]{2,1,0:T(8,128)S(1)}, f32[4,16,128]{2,1,0:T(8,128)S(1)}, u32[]{:S(2)}, u32[]{:S(2)}) collective-permute-start(f32[4,16,128]{2,1,0:T(8,128)S(1)} %get-tuple-element.31), channel_id=1, source_target_pairs={{0,16},{8,24},{16,0},{24,8},{1,17},{9,25},{17,1},{25,9},{2,18},{10... | collective-permute-start | bytes 98312 | tf_op jit(solution)/shard_map/ppermute | solution.py:316
  87.3 3.3 %basis.1 = f32[16,4,64,128]{3,2,1,0:T(8,128)} custom-call(s32[2]{0:T(128)S(1)} %pad_add_fusion.place, f32[16,128]{1,0:T(8,128)S(1)} %get-tuple-element.27.solved, f32[3,17,64,128]{3,2,1,0:T(8,128)S(1)} %get-tuple-element.25.upper, f32[17,64,128]{2,1,0:T(8,128)S(1)} %get-tuple-element.26.bottom), custom_call_target="tpu_custom_call" | custom-call | flops 8912896 | bytes 4456448 | tf_op jit(solution)/shard_map/basis/pallas_call | solution.py:24
  (41 shorter events, 5.2 us)
Async XLA Ops:
  0.7 1.6 %copy-start = (f32[1,16,4,64,128]{4,3,2,1,0:T(8,128)S(1)}, f32[1,16,4,64,128]{4,3,2,1,0:T(8,128)}, u32[]{:S(2)}) copy-start(f32[1,16,4,64,128]{4,3,2,1,0:T(8,128)} %param.6) | copy-start | bytes 6291460
  2.3 0.9 copy-start.9
  3.2 29.4 %copy-start.1 = (f32[1,16,4,64,128]{4,3,2,1,0:T(8,128)S(1)}, f32[1,16,4,64,128]{4,3,2,1,0:T(8,128)}, u32[]{:S(2)}) copy-start(f32[1,16,4,64,128]{4,3,2,1,0:T(8,128)} %param.6) | copy-start | bytes 6291460
  3.2 29.4 %copy-start.6 = (f32[1,4,64,128]{3,2,1,0:T(8,128)S(1)}, f32[1,4,64,128]{3,2,1,0:T(8,128)}, u32[]{:S(2)}) copy-start(f32[1,4,64,128]{3,2,1,0:T(8,128)} %param.9) | copy-start | bytes 393220
  4.8 27.8 %collective-permute-start.1 = (f32[17,64,128]{2,1,0:T(8,128)}, f32[17,64,128]{2,1,0:T(8,128)S(1)}, u32[]{:S(2)}, u32[]{:S(2)}) collective-permute-start(f32[17,64,128]{2,1,0:T(8,128)} %get-tuple-element.20), channel_id=1, source_target_pairs={{0,1},{1,0},{2,3},{3,2},{4,5},{5,4},{6,7},{7,6},{8,9},{9,8},{10,11... | collective-permute-start | bytes 1671176 | tf_op jit(solution)/shard_map/ppermute | solution.py:271
  7.9 31.6 %collective-permute-start = (f32[17,64,128]{2,1,0:T(8,128)}, f32[17,64,128]{2,1,0:T(8,128)}, u32[]{:S(2)}, u32[]{:S(2)}) collective-permute-start(f32[17,64,128]{2,1,0:T(8,128)} %get-tuple-element.19), channel_id=1, source_target_pairs={{0,7},{1,2},{2,1},{3,4},{4,3},{5,6},{6,5},{7,0},{8,15},{9,10},{10,... | collective-permute-start | bytes 1671176 | tf_op jit(solution)/shard_map/ppermute | solution.py:272
  32.6 1.0 %copy-start.2 = (f32[1,3,4,64,128]{4,3,2,1,0:T(8,128)S(1)}, f32[1,3,4,64,128]{4,3,2,1,0:T(8,128)}, u32[]{:S(2)}) copy-start(f32[1,3,4,64,128]{4,3,2,1,0:T(8,128)} %param.8) | copy-start | bytes 1179652
  33.6 0.9 copy-start.7
  34.5 0.9 copy-start.10
  35.4 4.1 %copy-start.3 = (f32[1,3,4,64,128]{4,3,2,1,0:T(8,128)S(1)}, f32[1,3,4,64,128]{4,3,2,1,0:T(8,128)}, u32[]{:S(2)}) copy-start(f32[1,3,4,64,128]{4,3,2,1,0:T(8,128)} %param.8) | copy-start | bytes 1179652
  35.4 4.1 %copy-start.8 = (f32[1,4,64,128]{3,2,1,0:T(8,128)S(1)}, f32[1,4,64,128]{3,2,1,0:T(8,128)}, u32[]{:S(2)}) copy-start(f32[1,4,64,128]{3,2,1,0:T(8,128)} %param.10) | copy-start | bytes 393220
  35.4 4.1 %copy-start.11 = (f32[1,4,64,128]{3,2,1,0:T(8,128)S(1)}, f32[1,4,64,128]{3,2,1,0:T(8,128)}, u32[]{:S(2)}) copy-start(f32[1,4,64,128]{3,2,1,0:T(8,128)} %param.7) | copy-start | bytes 393220
  37.7 3.2 %copy-start.4 = (f32[2,17,64,128]{3,2,1,0:T(8,128)}, f32[2,17,64,128]{3,2,1,0:T(8,128)S(1)}, u32[]{:S(2)}) copy-start(f32[2,17,64,128]{3,2,1,0:T(8,128)S(1)} %get-tuple-element.21.inner) | copy-start | bytes 3342340
  37.8 26.0 %collective-permute-start.3 = (f32[17,64,128]{2,1,0:T(8,128)}, f32[17,64,128]{2,1,0:T(8,128)}, u32[]{:S(2)}, u32[]{:S(2)}) collective-permute-start(f32[17,64,128]{2,1,0:T(8,128)} %get-tuple-element.22.top), channel_id=1, source_target_pairs={{0,1},{1,0},{2,3},{3,2},{4,5},{5,4},{6,7},{7,6},{8,9},{9,8},{10,11... | collective-permute-start | bytes 1671176 | tf_op jit(solution)/shard_map/ppermute | solution.py:279
  41.0 26.1 %collective-permute-start.2 = (f32[17,64,128]{2,1,0:T(8,128)S(1)}, f32[17,64,128]{2,1,0:T(8,128)}, u32[]{:S(2)}, u32[]{:S(2)}) collective-permute-start(f32[17,64,128]{2,1,0:T(8,128)S(1)} %second.1.bottom), channel_id=1, source_target_pairs={{0,7},{1,2},{2,1},{3,4},{4,3},{5,6},{6,5},{7,0},{8,15},{9,10},{10,... | collective-permute-start | bytes 1671176 | tf_op jit(solution)/shard_map/ppermute | solution.py:285
  44.6 19.2 %copy-start.5 = (f32[2,17,64,128]{3,2,1,0:T(8,128)S(1)}, f32[2,17,64,128]{3,2,1,0:T(8,128)}, u32[]{:S(2)}) copy-start(f32[2,17,64,128]{3,2,1,0:T(8,128)} %copy-done.4) | copy-start | bytes 3342340
  69.2 3.7 %collective-permute-start.4 = (f32[16,128]{1,0:T(8,128)S(1)}, f32[16,128]{1,0:T(8,128)S(1)}, u32[]{:S(2)}, u32[]{:S(2)}) collective-permute-start(f32[16,128]{1,0:T(8,128)S(1)} %get-tuple-element.24), channel_id=1, source_target_pairs={{0,1},{1,0},{2,3},{3,2},{4,5},{5,4},{6,7},{7,6},{8,9},{9,8},{10,11... | collective-permute-start | bytes 24584 | tf_op jit(solution)/shard_map/ppermute | solution.py:301
  72.8 3.7 %collective-permute-start.5 = (f32[16,128]{1,0:T(8,128)S(1)}, f32[16,128]{1,0:T(8,128)S(1)}, u32[]{:S(2)}, u32[]{:S(2)}) collective-permute-start(f32[16,128]{1,0:T(8,128)S(1)} %add.47), channel_id=1, source_target_pairs={{0,2},{1,3},{2,0},{3,1},{4,6},{5,7},{6,4},{7,5},{8,10},{9,11},{10,... | collective-permute-start | bytes 24584 | tf_op jit(solution)/shard_map/ppermute | solution.py:301
  76.6 4.5 %collective-permute-start.6 = (f32[16,128]{1,0:T(8,128)S(1)}, f32[16,128]{1,0:T(8,128)S(1)}, u32[]{:S(2)}, u32[]{:S(2)}) collective-permute-start(f32[16,128]{1,0:T(8,128)S(1)} %add.48), channel_id=1, source_target_pairs={{0,4},{1,5},{2,6},{3,7},{4,0},{5,1},{6,2},{7,3},{8,12},{9,13},{10,... | collective-permute-start | bytes 24584 | tf_op jit(solution)/shard_map/ppermute | solution.py:301
  84.1 6.5 %collective-permute-start.7 = (f32[4,16,128]{2,1,0:T(8,128)S(1)}, f32[4,16,128]{2,1,0:T(8,128)S(1)}, u32[]{:S(2)}, u32[]{:S(2)}) collective-permute-start(f32[4,16,128]{2,1,0:T(8,128)S(1)} %get-tuple-element.30), channel_id=1, source_target_pairs={{0,8},{8,0},{16,24},{24,16},{1,9},{9,1},{17,25},{25,17},{2,10},{10... | collective-permute-start | bytes 98312 | tf_op jit(solution)/shard_map/ppermute | solution.py:316
  84.1 6.5 %collective-permute-start.8 = (f32[4,16,128]{2,1,0:T(8,128)S(1)}, f32[4,16,128]{2,1,0:T(8,128)S(1)}, u32[]{:S(2)}, u32[]{:S(2)}) collective-permute-start(f32[4,16,128]{2,1,0:T(8,128)S(1)} %get-tuple-element.31), channel_id=1, source_target_pairs={{0,16},{8,24},{16,0},{24,8},{1,17},{9,25},{17,1},{25,9},{2,18},{10... | collective-permute-start | bytes 98312 | tf_op jit(solution)/shard_map/ppermute | solution.py:316
  85.5 5.1 %collective-permute-start.9 = (f32[4,16,128]{2,1,0:T(8,128)S(1)}, f32[4,16,128]{2,1,0:T(8,128)S(1)}, u32[]{:S(2)}, u32[]{:S(2)}) collective-permute-start(f32[4,16,128]{2,1,0:T(8,128)S(1)} %get-tuple-element.32), channel_id=1, source_target_pairs={{0,24},{8,16},{16,8},{24,0},{1,25},{9,17},{17,9},{25,1},{2,26},{10... | collective-permute-start | bytes 98312 | tf_op jit(solution)/shard_map/ppermute | solution.py:316

commit v2 on v1

v2 whole, which is shorter than its diff:
```python
import functools
import math

import jax
import jax.numpy as jnp
from jax import lax
from jax.experimental import pallas as pl
from jax.experimental.pallas import tpu as pltpu
from jax.sharding import PartitionSpec as P


SUB = 8
HIGH = lax.Precision.HIGHEST
VMEM_SPEC = pl.BlockSpec(memory_space=pltpu.VMEM)
SMEM_SPEC = pl.BlockSpec(memory_space=pltpu.SMEM)
ANY_SPEC = pl.BlockSpec(memory_space=pl.ANY)
HBM_SPEC = pl.BlockSpec(memory_space=pltpu.HBM)


def modulation(window_start, section):
    phase_step = (window_start + 2 - section) % 64
    return 1.0 + 0.5 * jnp.sin(2.0 * math.pi * phase_step.astype(jnp.float32) / 64.0)


def call(body, outs, specs, args, scratch=(), flops=0, moved=0):
    return pl.pallas_call(
        body,
        out_shape=outs,
        in_specs=specs,
        out_specs=jax.tree.map(lambda _: VMEM_SPEC, outs),
        scratch_shapes=scratch,
        cost_estimate=pl.CostEstimate(flops=flops, transcendentals=0, bytes_accessed=moved),
        compiler_params=pltpu.CompilerParams(vmem_limit_bytes=20 * 1024 * 1024),
    )(*args)


def layer_of(odd, position, layers):
    return position + odd * (layers - 1 - 2 * position)


def pack_kernel(count, layers, positions, cuts, place, dirs, adj, *rest):
    outs, sems = rest[:-1], rest[-1]
    odd = place[0]
    copies = []
    for k, (out, position) in enumerate(zip(outs, positions)):
        layer = layer_of(odd, position, layers)
        stop = min(cuts[k + 1], count)
        size = stop - cuts[k]
        copies.append(
            pltpu.make_async_copy(dirs.at[pl.ds(cuts[k], size), layer], out.at[pl.ds(0, size)], sems.at[k])
        )
        if cuts[k + 1] > count:
            copies.append(pltpu.make_async_copy(adj.at[layer], out.at[size], sems.at[2]))
    for copy in copies:
        copy.start()
    for copy in copies:
        copy.wait()


def coefficients_at(vel, dif, layer, half, sign, rows, first_row, last_row):
    spread = dif[layer, rows, :]
    ax = (half * sign) * vel[0, layer, rows, :]
    ay = half * vel[1, layer, rows, :]
    az = half * vel[2, layer, rows, :]
    up, down = spread + ay, spread - ay
    row = lax.broadcasted_iota(jnp.int32, spread.shape, 0)
    if last_row:
        up = jnp.where(row == spread.shape[0] - 1, 0.0, up)
    if first_row:
        down = jnp.where(row == 0, 0.0, down)
    return 1.0 - 6.0 * spread, spread + ax, spread - ax, up, down, spread + az, spread - az


def stencil(
    vel, dif, src, layer, half, sign, fields, count, rows_total, width, middle, toward, away, store
):
    for base in range(0, rows_total, SUB):
        rows = slice(base, base + SUB)
        first_row, last_row = base == 0, base + SUB == rows_total
        c0, cxp, cxm, cyp, cym, czp, czm = coefficients_at(
            vel, dif, layer, half, sign, rows, first_row, last_row
        )
        for field in fields:
            tile = middle(field, rows)
            if last_row:
                above = pltpu.roll(tile, SUB - 1, 0)
            else:
                above = middle(field, slice(base + 1, base + 1 + SUB))
            if first_row:
                below = pltpu.roll(tile, 1, 0)
            else:
                below = middle(field, slice(base - 1, base - 1 + SUB))
            total = c0 * tile + cxp * toward(field, rows) + cxm * away(field, rows)
            total = total + (cyp * above + cym * below)
            total = total + (czp * pltpu.roll(tile, width - 1, 1) + czm * pltpu.roll(tile, 1, 1))
            if field == count:
                total = total + src[layer, rows, :]
            store(field, rows, total)


def reader(dirs, adj, count, layer):
    def read(field, rows):
        return dirs[field, layer, rows, :] if field < count else adj[layer, rows, :]

    return read


def plain(ref, *lead):
    def read(field, rows):
        return ref[(*lead, field, rows, slice(None))]

    return read


def joined(first, second):
    cut = first.shape[0]

    def read(field, rows):
        return first[field, rows, :] if field < cut else second[field - cut, rows, :]

    return read


def writer(ref, *lead, start=0):
    def write(field, rows, value):
        ref[(*lead, field - start, rows, slice(None))] = value

    return write


def sign_of(place):
    return (1 - 2 * place[0]).astype(jnp.float32)


def inner_kernel(count, layers, place, half, dirs, adj, vel, dif, src, inner):
    odd = place[0]
    _, _, ny, nz = dirs.shape
    for position in range(1, layers - 1):
        near, here, far = (layer_of(odd, position + k, layers) for k in (1, 0, -1))
        stencil(
            vel, dif, src, here, half[0], sign_of(place), range(count + 1), count, ny, nz,
            reader(dirs, adj, count, here), reader(dirs, adj, count, near), reader(dirs, adj, count, far),
            writer(inner, position - 1),
        )


def bottom_kernel(count, layers, place, half, dirs, adj, halo, vel, dif, src, edge):
    odd = place[0]
    _, _, ny, nz = dirs.shape
    here, near = layer_of(odd, 0, layers), layer_of(odd, 1, layers)
    stencil(
        vel, dif, src, here, half[0], sign_of(place), range(count + 1), count, ny, nz,
        reader(dirs, adj, count, here), reader(dirs, adj, count, near), plain(halo), writer(edge),
    )


def top_kernel(count, layers, start, place, half, dirs, adj, halo, vel, dif, src, order, edge):
    odd = place[0]
    _, _, ny, nz = dirs.shape
    here, far = layer_of(odd, layers - 1, layers), layer_of(odd, layers - 2, layers)

    def toward(field, rows):
        return halo[field - start, rows, :]

    stencil(
        vel, dif, src, here, half[0], sign_of(place), range(start, start + edge.shape[0]), count, ny, nz,
        reader(dirs, adj, count, here), toward, reader(dirs, adj, count, far), writer(edge, start=start),
    )


def add_products(tiles, count, ny, total):
    step = 2 * SUB if ny % (2 * SUB) == 0 else SUB
    for base in range(0, ny, step):
        parts = [tiles(slice(row, row + SUB)) for row in range(base, base + step, SUB)]
        block = jnp.concatenate(parts, axis=1) if len(parts) > 1 else parts[0]
        total = total + lax.dot_general(
            block[: count * SUB], block, (((1,), (1,)), ((), ())),
            precision=HIGH, preferred_element_type=jnp.float32,
        )
    return total


def flat(tile):
    return tile.reshape(tile.shape[0] * tile.shape[1], tile.shape[2])


def middle_kernel(
    count, layers, place, half, bottom, inner, top_a, top_b, vel, dif, src, out, products, early
):
    odd = place[0]
    _, ny, nz = bottom.shape

    def at(position):
        if position == 0:
            return plain(bottom)
        return joined(top_a, top_b) if position == layers - 1 else plain(inner, position - 1)

    for position in range(1, layers - 1):
        stencil(
            vel, dif, src, layer_of(odd, position, layers), half[1], sign_of(place), range(count + 1),
            count, ny, nz, at(position), at(position + 1), at(position - 1), writer(out, position - 1),
        )
    for position in range(layers):
        early[layer_of(odd, position, layers)] = at(position)(count, slice(0, ny))
    total = jnp.zeros(products.shape, jnp.float32)
    for position in range(1, layers - 1):
        total = add_products(lambda rows: flat(out[position - 1, :, rows, :]), count, ny, total)
    products[...] = total


def low_kernel(count, layers, place, half, bottom, inner, halo, vel, dif, src, before, out, products):
    odd = place[0]
    _, ny, nz = bottom.shape
    stencil(
        vel, dif, src, layer_of(odd, 0, layers), half[1], sign_of(place), range(count + 1), count, ny, nz,
        plain(bottom), plain(inner, 0), plain(halo), writer(out),
    )
    products[...] = add_products(lambda rows: flat(out[:, rows, :]), count, ny, before[...])


def high_stencil(count, layers, start, place, half, top, inner, halo, vel, dif, src, out):
    _, ny, nz = top.shape

    def middle(field, rows):
        return top[field - start, rows, :]

    def toward(field, rows):
        return halo[field - start, rows, :]

    stencil(
        vel, dif, src, layer_of(place[0], layers - 1, layers), half[1], sign_of(place),
        range(start, start + out.shape[0]), count, ny, nz, middle, toward, plain(inner, layers - 3),
        writer(out, start=start),
    )


def high_a_kernel(count, layers, place, half, top, inner, halo, vel, dif, src, order, out):
    high_stencil(count, layers, 0, place, half, top, inner, halo, vel, dif, src, out)


def high_b_kernel(
    count, layers, place, half, top, inner, halo, vel, dif, src, before, out_a, out, gram
):
    start = out_a.shape[0]
    _, ny, _ = top.shape
    high_stencil(count, layers, start, place, half, top, inner, halo, vel, dif, src, out)
    total = add_products(
        lambda rows: jnp.concatenate([flat(out_a[:, rows, :]), flat(out[:, rows, :])], axis=0),
        count, ny, before[...],
    )
    rows = lax.broadcasted_iota(jnp.int32, total.shape, 0)
    columns = lax.broadcasted_iota(jnp.int32, total.shape, 1)
    total = jnp.where(rows % SUB == columns % SUB, total, 0.0)
    total = total.reshape(count, SUB, total.shape[1]).sum(axis=1)
    width = gram.shape[1]
    gather = (
        lax.broadcasted_iota(jnp.int32, (total.shape[1], width), 0) // SUB
        == lax.broadcasted_iota(jnp.int32, (total.shape[1], width), 1)
    ).astype(jnp.float32)
    gram[...] = jnp.dot(total, gather, precision=HIGH, preferred_element_type=jnp.float32)


def result_at(position, layers, low, mid, high_a, high_b):
    if position == 0:
        return plain(low)
    return joined(high_a, high_b) if position == layers - 1 else plain(mid, position - 1)


def solve_kernel(
    count, layers, pieces, cells, place, gram, low, mid, high_a, high_b, early,
    solved, factor, along, shadow, *parts,
):
    odd, seg = place[0], place[1]
    _, ny, nz = low.shape
    shape = gram.shape
    row = lax.broadcasted_iota(jnp.int32, shape, 0)
    lane = lax.broadcasted_iota(jnp.int32, shape, 1)
    table = jnp.where(lane <= count, gram[...] / cells, 0.0)
    table = jnp.where(lane == row + count + 1, 1.0, table)
    for k in range(count):
        pivot_row = table[k : k + 1, :]
        root = jnp.sqrt(pivot_row[:, k : k + 1])
        scaled = pivot_row / root
        column = table[:, k : k + 1] / root
        table = jnp.where(row == k, scaled, jnp.where(row > k, table - column * scaled, table))
    table = jnp.where((lane < count) & (lane < row), 0.0, table)
    solved[...] = table
    weights = jnp.sum(table[:, count : count + 1] * table, axis=0, keepdims=True)
    splat = [
        jnp.broadcast_to(weights[:, count + 1 + j : count + 2 + j], (SUB, nz)) for j in range(count)
    ]
    for position in range(layers):
        layer = layer_of(odd, position, layers)
        read = result_at(position, layers, low, mid, high_a, high_b)
        for base in range(0, ny, SUB):
            rows = slice(base, base + SUB)
            total = read(count, rows)
            for j in range(count):
                total = total - splat[j] * read(j, rows)
            shadow[layer, rows, :] = total
    step = ny // pieces
    for k, part in enumerate(parts):
        begin = pl.multiple_of((seg ^ k) * step, step)
        rows = pl.ds(begin, step)
        part[...] = shadow[:, rows, :] + early[:, rows, :]
    factor[...] = table[:, :count]
    eye = (
        lax.broadcasted_iota(jnp.int32, (count, count), 0) == lax.broadcasted_iota(jnp.int32, (count, count), 1)
    )
    along[...] = jnp.sum(jnp.where(eye, table[:, count : count + 1], 0.0), axis=0, keepdims=True)


def basis_kernel(count, layers, place, solved, low, mid, high_a, high_b, out):
    odd = place[0]
    _, ny, _ = low.shape
    block = min(ny, 8 * SUB)
    for position in range(layers):
        layer = layer_of(odd, position, layers)
        read = result_at(position, layers, low, mid, high_a, high_b)
        for base in range(0, ny, block):
            rows = slice(base, base + block)
            for i in range(count):
                total = solved[i, count + 1] * read(0, rows)
                for j in range(1, i + 1):
                    total = total + solved[i, count + 1 + j] * read(j, rows)
                out[i, layer, rows, :] = total


def window(directions, adjoint, velocity, diffusivity, objective_source, segment_start):
    dirs, adj, vel, dif, src = (
        directions[0], adjoint[0], velocity[0], diffusivity[0], objective_source[0],
    )
    count, layers, ny, nz = dirs.shape
    fields, part_a = count + 1, (count + 2) // 2
    spaces, segs = lax.axis_size("space"), lax.axis_size("seg")
    assert spaces & (spaces - 1) == 0 and segs & (segs - 1) == 0 and layers >= 3
    odd = lax.axis_index("space") % 2
    place = jnp.stack([odd, lax.axis_index("seg")]).astype(jnp.int32)
    half = jnp.stack([0.5 * modulation(segment_start[0], k) for k in (1, 2)])
    pair_one = [(i, i ^ 1) for i in range(spaces)]
    pair_two = [(i, (i + 1) % spaces if i % 2 else (i - 1) % spaces) for i in range(spaces)]
    f32 = functools.partial(jax.ShapeDtypeStruct, dtype=jnp.float32)
    edge, edge_a, edge_b = (f32((n, ny, nz)) for n in (fields, part_a, fields - part_a))
    layer_bytes = 4 * fields * ny * nz
    layer_flops = 13 * fields * ny * nz
    vs, ss, hs, anys = VMEM_SPEC, SMEM_SPEC, HBM_SPEC, ANY_SPEC
    flow = (vel, dif, src)

    dirs_hbm, adj_hbm = (pltpu.with_memory_space_constraint(x, pltpu.HBM) for x in (dirs, adj))
    near_a, near_b = call(
        functools.partial(pack_kernel, count, layers, (layers - 1, layers - 1), (0, part_a, fields)),
        [edge_a, edge_b], [ss, hs, hs], (place, dirs_hbm, adj_hbm),
        scratch=[pltpu.SemaphoreType.DMA((3,))], moved=2 * layer_bytes,
    )
    halo_a = lax.ppermute(near_a, "space", pair_one)
    halo_b = lax.ppermute(near_b, "space", pair_one)
    (far,) = call(
        functools.partial(pack_kernel, count, layers, (0,), (0, fields)),
        [edge], [ss, hs, hs], (place, dirs_hbm, adj_hbm),
        scratch=[pltpu.SemaphoreType.DMA((3,))], moved=2 * layer_bytes,
    )
    halo_far = lax.ppermute(far, "space", pair_two)
    inner = call(
        functools.partial(inner_kernel, count, layers), f32((layers - 2, fields, ny, nz)),
        [ss, ss] + [vs] * 5, (place, half, dirs, adj) + flow,
        flops=(layers - 2) * layer_flops, moved=6 * layer_bytes,
    )
    bottom = call(
        functools.partial(bottom_kernel, count, layers), edge,
        [ss, ss] + [vs] * 6, (place, half, dirs, adj, halo_far) + flow,
        flops=layer_flops, moved=4 * layer_bytes,
    )
    bottom_far = lax.ppermute(bottom, "space", pair_two)
    top_a = call(
        functools.partial(top_kernel, count, layers, 0), edge_a,
        [ss, ss] + [vs] * 6 + [anys], (place, half, dirs, adj, halo_a) + flow + (bottom,),
        flops=layer_flops // 2, moved=2 * layer_bytes,
    )
    near_top_a = lax.ppermute(top_a, "space", pair_one)
    top_b = call(
        functools.partial(top_kernel, count, layers, part_a), edge_b,
        [ss, ss] + [vs] * 6 + [anys], (place, half, dirs, adj, halo_b) + flow + (top_a,),
        flops=layer_flops // 2, moved=2 * layer_bytes,
    )
    near_top_b = lax.ppermute(top_b, "space", pair_one)
    mid, products, early = call(
        functools.partial(middle_kernel, count, layers),
        [f32((layers - 2, fields, ny, nz)), f32((count * SUB, fields * SUB)), f32((layers, ny, nz))],
        [ss, ss] + [vs] * 7, (place, half, bottom, inner, top_a, top_b) + flow,
        flops=4 * (layers - 2) * layer_flops, moved=6 * layer_bytes,
    )
    low, products = call(
        functools.partial(low_kernel, count, layers), [edge, f32((count * SUB, fields * SUB))],
        [ss, ss] + [vs] * 7, (place, half, bottom, inner, bottom_far) + flow + (products,),
        flops=4 * layer_flops, moved=4 * layer_bytes,
    )
    high_a = call(
        functools.partial(high_a_kernel, count, layers), edge_a,
        [ss, ss] + [vs] * 6 + [anys], (place, half, top_a, inner, near_top_a) + flow + (low,),
        flops=layer_flops // 2, moved=2 * layer_bytes,
    )
    high_b, gram = call(
        functools.partial(high_b_kernel, count, layers), [edge_b, f32((count, 128))],
        [ss, ss] + [vs] * 8, (place, half, top_b, inner, near_top_b) + flow + (products, high_a),
        flops=2 * layer_flops, moved=2 * layer_bytes,
    )
    reach = 1
    while reach < spaces:
        gram = gram + lax.ppermute(gram, "space", [(i, i ^ reach) for i in range(spaces)])
        reach *= 2
    piece = f32((layers, ny // segs, nz))
    solved, factor, along, shadow, *parts = call(
        functools.partial(solve_kernel, count, layers, segs, float(layers * ny * nz * spaces)),
        [f32((count, 128)), f32((count, count)), f32((1, count)), f32((layers, ny, nz))] + [piece] * segs,
        [ss] + [vs] * 6, (place, gram, low, mid, high_a, high_b, early),
        flops=4 * layer_flops, moved=4 * layer_bytes,
    )
    gradient = parts[0]
    for k in range(1, segs):
        gradient = gradient + lax.ppermute(parts[k], "seg", [(i, i ^ k) for i in range(segs)])
    basis = call(
        functools.partial(basis_kernel, count, layers), f32((count, layers, ny, nz)),
        [ss, ss] + [vs] * 4, (place, solved, low, mid, high_a, high_b),
        flops=8 * layer_flops, moved=8 * layer_bytes,
    )
    return basis[None], factor[None], along, shadow[None], gradient


def solution(mesh):
    return jax.shard_map(
        window,
        mesh=mesh,
        in_specs=(
            P("seg", None, "space", None, None),
            P("seg", "space", None, None),
            P("seg", None, "space", None, None),
            P("seg", "space", None, None),
            P("seg", "space", None, None),
            P("seg"),
        ),
        out_specs=(
            P("seg", None, "space", None, None),
            P("seg", None, None),
            P("seg", None),
            P("seg", "space", None, None),
            P("space", "seg", None),
        ),
        check_vma=False,
    )
```

time: 91.7 us -> 79.9 us (0.87)
  local copies, waits for them, and re-layouts: 8.57 us -> 0.72 us
  starting transfers between devices: 19.3 us -> 14.4 us
  Pallas kernels: 17 us -> 21.1 us
  waiting for transfers between devices: 44 us -> 41.1 us
    ppermute x10 -> x12, starting transfers between devices: 19.3 us -> 14.4 us  [the longest x1 6.1 us: window(): halo_far = lax.ppermute(far, 'space', pair_two)]
    unnamed x24 -> x14, local copies, waits for them, and re-layouts: 5.32 us -> 0.72 us
    pallas_call x7 -> x12, Pallas kernels: 17 us -> 21.1 us  [call(): pl.pallas_call(body, out_shape=outs, in_specs=specs, out_specs=jax.tree.m...]
    ppermute x10 -> x12, waiting for transfers between devices: 44 us -> 41.1 us  [the longest x1 12.2 us: window(): halo_a = lax.ppermute(near_a, 'space', pair_one)]
    slice x3 -> x0, local copies, waits for them, and re-layouts: 1.46 us -> none  [the longest x1 0.76 us: body(): early_layers = [top[count]]]
    squeeze x1 -> x0, local copies, waits for them, and re-layouts: 1.18 us -> none  [body(): inner[0]]
  transfers between devices with their start and end apart: 10 -> 12, of which waited for: 5 -> 8; matrix products, arithmetic and copies ran while one was open for 4% -> 0% of each run, Pallas kernels for 11% -> 18%
where the time goes in v2:
time: 79.9 us; the launch traced here: 79.7 us
  waiting for transfers between devices  41.1 us (51%)
  Pallas kernels  21.1 us (26%)
  starting transfers between devices  14.4 us (18%)
  between operations  1.63 us (2%)
    pallas_call x12, Pallas kernels, call(): pl.pallas_call(body, out_shape=outs, in_specs=specs, out_specs=jax.tree.m...  21.1 us
    ppermute x1, waiting for transfers between devices, window(): halo_a = lax.ppermute(near_a, 'space', pair_one)  12.2 us
    ppermute x3, waiting for transfers between devices, window(): lax.ppermute(gram, 'space', [(i, i ^ reach) for i in range(spaces)])  10.4 us
    ppermute x1, waiting for transfers between devices, window(): halo_far = lax.ppermute(far, 'space', pair_two)  8.87 us
    ppermute x1, starting transfers between devices, window(): halo_far = lax.ppermute(far, 'space', pair_two)  6.1 us
    ppermute x1, waiting for transfers between devices, window(): near_top_b = lax.ppermute(top_b, 'space', pair_one)  4.82 us
    ppermute x1, starting transfers between devices, window(): bottom_far = lax.ppermute(bottom, 'space', pair_two)  4.5 us
    ppermute x1, waiting for transfers between devices, window(): halo_b = lax.ppermute(near_b, 'space', pair_one)  4.23 us
  transfers between devices with their start and end apart: 12, of which 8 were waited for; matrix products, arithmetic and copies ran while one was open for 0% of the time, Pallas kernels for 18%

profile of v2, /device:TPU:0, one launch (start us, length us, event | category | flops | bytes accessed | tf_op | source)
XLA Modules:
  0.0 79.7 jit_solution(9123709373069830314)
XLA Ops:
  0.7 1.9 %shard_map.102 = f32[17,64,128]{2,1,0:T(8,128)S(1)} custom-call(s32[2]{0:T(128)S(1)} %pad_add_fusion.place, f32[16,4,64,128]{3,2,1,0:T(8,128)} %bitcast.17, f32[4,64,128]{2,1,0:T(8,128)} %bitcast.47), custom_call_target="tpu_custom_call" | custom-call | bytes 1114112 | tf_op jit(solution)/shard_map/pallas_call | solution.py:26
  2.6 6.1 %collective-permute-start.2 = (f32[17,64,128]{2,1,0:T(8,128)S(1)}, f32[17,64,128]{2,1,0:T(8,128)}, u32[]{:S(2)}, u32[]{:S(2)}) collective-permute-start(f32[17,64,128]{2,1,0:T(8,128)S(1)} %shard_map.102), channel_id=1, source_target_pairs={{0,7},{1,2},{2,1},{3,4},{4,3},{5,6},{6,5},{7,0},{8,15},{9,10},{10,... | collective-permute-start | bytes 1671176 | tf_op jit(solution)/shard_map/ppermute | solution.py:362
  8.7 2.3 %shard_map.101 = (f32[9,64,128]{2,1,0:T(8,128)}, f32[8,64,128]{2,1,0:T(8,128)S(1)}) custom-call(s32[2]{0:T(128)S(1)} %pad_add_fusion.place, f32[16,4,64,128]{3,2,1,0:T(8,128)} %bitcast.18, f32[4,64,128]{2,1,0:T(8,128)} %bitcast.48), custom_call_target="tpu_custom_call" | custom-call | bytes 1114112 | tf_op jit(solution)/shard_map/pallas_call | solution.py:26
  11.1 0.7 copy-done.5
  12.7 8.9 %collective-permute-done.2.halo = f32[17,64,128]{2,1,0:T(8,128)} collective-permute-done((f32[17,64,128]{2,1,0:T(8,128)S(1)}, f32[17,64,128]{2,1,0:T(8,128)}, u32[]{:S(2)}, u32[]{:S(2)}) %collective-permute-start.2) | collective-permute-done | bytes 557088 | tf_op jit(solution)/shard_map/ppermute | solution.py:362
  21.6 1.4 %shard_map.103.order.bottom = f32[17,64,128]{2,1,0:T(8,128)S(1)} custom-call(s32[2]{0:T(128)S(1)} %pad_add_fusion.place, f32[2]{0:T(128)S(1)} %pad_maximum_fusion.half, f32[16,4,64,128]{3,2,1,0:T(8,128)S(1)} %bitcast.19, f32[4,64,128]{2,1,0:T(8,128)S(1)} %bitcast.49, f32[17,64,128]{2,1,0:T(8,128)} %collective-permute-done.2.halo, ...), custom_call_target="tpu_custom_call" | custom-call | flops 1810432 | bytes 2228224 | tf_op jit(solution)/shard_map/pallas_call | solution.py:26
  23.0 4.5 %collective-permute-start.4 = (f32[17,64,128]{2,1,0:T(8,128)S(1)}, f32[17,64,128]{2,1,0:T(8,128)S(1)}, u32[]{:S(2)}, u32[]{:S(2)}) collective-permute-start(f32[17,64,128]{2,1,0:T(8,128)S(1)} %shard_map.103.order.bottom), channel_id=1, source_target_pairs={{0,7},{1,2},{2,1},{3,4},{4,3},{5,6},{6,5},{7,0},{8,15},{9,10},{10,... | collective-permute-start | bytes 1671176 | tf_op jit(solution)/shard_map/ppermute | solution.py:373
  27.5 12.2 %collective-permute-done.1.halo = f32[9,64,128]{2,1,0:T(8,128)} collective-permute-done((f32[9,64,128]{2,1,0:T(8,128)}, f32[9,64,128]{2,1,0:T(8,128)}, u32[]{:S(2)}, u32[]{:S(2)}) %collective-permute-start.1) | collective-permute-done | bytes 294944 | tf_op jit(solution)/shard_map/ppermute | solution.py:355
  39.8 1.2 %shard_map.104.order.top_a.top = f32[9,64,128]{2,1,0:T(8,128)S(1)} custom-call(s32[2]{0:T(128)S(1)} %pad_add_fusion.place, f32[2]{0:T(128)S(1)} %pad_maximum_fusion.half, f32[16,4,64,128]{3,2,1,0:T(8,128)S(1)} %bitcast.20, f32[4,64,128]{2,1,0:T(8,128)S(1)} %bitcast.50, f32[9,64,128]{2,1,0:T(8,128)} %collective-permute-done.1.halo, ...), custom_call_target="tpu_custom_call" | custom-call | flops 905216 | bytes 1114112 | tf_op jit(solution)/shard_map/pallas_call | solution.py:26
  41.0 4.2 %collective-permute-done.halo = f32[8,64,128]{2,1,0:T(8,128)S(1)} collective-permute-done((f32[8,64,128]{2,1,0:T(8,128)S(1)}, f32[8,64,128]{2,1,0:T(8,128)S(1)}, u32[]{:S(2)}, u32[]{:S(2)}) %collective-permute-start) | collective-permute-done | bytes 262176 | tf_op jit(solution)/shard_map/ppermute | solution.py:356
  45.3 0.8 shard_map.105.top_b.top
  46.1 1.2 %shard_map.106.inner = f32[2,17,64,128]{3,2,1,0:T(8,128)S(1)} custom-call(s32[2]{0:T(128)S(1)} %pad_add_fusion.place, f32[2]{0:T(128)S(1)} %pad_maximum_fusion.half, f32[16,4,64,128]{3,2,1,0:T(8,128)S(1)} %bitcast.22, f32[4,64,128]{2,1,0:T(8,128)S(1)} %bitcast.52, f32[3,4,64,128]{3,2,1,0:T(8,128)S(1)} %bitcast.26, f32[4,64,128]{2,1,0:T(8,128)S(1)} %bitcast.34, ...), custom_call_target="tpu_custom_call" | custom-call | flops 3620864 | bytes 3342336 | tf_op jit(solution)/shard_map/pallas_call | solution.py:26
  47.3 2.2 %shard_map.107 = (f32[2,17,64,128]{3,2,1,0:T(8,128)S(1)}, f32[128,136]{1,0:T(8,128)S(1)}, f32[4,64,128]{2,1,0:T(8,128)S(1)}) custom-call(s32[2]{0:T(128)S(1)} %pad_add_fusion.place, f32[2]{0:T(128)S(1)} %pad_maximum_fusion.half, f32[17,64,128]{2,1,0:T(8,128)S(1)} %shard_map.103.order.bottom, f32[2,17,64,128]{3,2,1,0:T(8,128)S(1)} %shard_map.106.inner, ...), custom_call_target="tpu_custom_call" | custom-call | flops 14483456 | bytes 3342336 | tf_op jit(solution)/shard_map/pallas_call | solution.py:26
  49.5 1.5 %shard_map.108 = (f32[17,64,128]{2,1,0:T(8,128)S(1)}, f32[128,136]{1,0:T(8,128)S(1)}) custom-call(s32[2]{0:T(128)S(1)} %pad_add_fusion.place, f32[2]{0:T(128)S(1)} %pad_maximum_fusion.half, f32[17,64,128]{2,1,0:T(8,128)S(1)} %shard_map.103.order.bottom, f32[2,17,64,128]{3,2,1,0:T(8,128)S(1)} %shard_map.106.inner, ...), custom_call_target="tpu_custom_call" | custom-call | flops 7241728 | bytes 2228224 | tf_op jit(solution)/shard_map/pallas_call | solution.py:26
  51.6 0.8 shard_map.109.out_a.high_a
  52.4 4.8 %collective-permute-done.3.halo = f32[8,64,128]{2,1,0:T(8,128)S(1)} collective-permute-done((f32[8,64,128]{2,1,0:T(8,128)S(1)}, f32[8,64,128]{2,1,0:T(8,128)S(1)}, u32[]{:S(2)}, u32[]{:S(2)}) %collective-permute-start.3) | collective-permute-done | bytes 262176 | tf_op jit(solution)/shard_map/ppermute | solution.py:385
  57.2 1.5 %shard_map.110 = (f32[8,64,128]{2,1,0:T(8,128)S(1)}, f32[16,128]{1,0:T(8,128)S(1)}) custom-call(s32[2]{0:T(128)S(1)} %pad_add_fusion.place, f32[2]{0:T(128)S(1)} %pad_maximum_fusion.half, f32[8,64,128]{2,1,0:T(8,128)S(1)} %shard_map.105.top_b.top, f32[2,17,64,128]{3,2,1,0:T(8,128)S(1)} %shard_map.106.inner, f32[8,64,128]{2,1,0:T(8,128)S(1)} %collective-permute-done.3.halo, ...), custom_call_target="tpu_custom_call" | custom-call | flops 3620864 | bytes 1114112 | tf_op jit(solution)/shard_map/pallas_call | solution.py:26
  58.7 3.7 %collective-permute-done.6 = f32[16,128]{1,0:T(8,128)S(1)} collective-permute-done((f32[16,128]{1,0:T(8,128)S(1)}, f32[16,128]{1,0:T(8,128)S(1)}, u32[]{:S(2)}, u32[]{:S(2)}) %collective-permute-start.6) | collective-permute-done | bytes 8224 | tf_op jit(solution)/shard_map/ppermute | solution.py:409
  62.4 3.6 %collective-permute-done.7 = f32[16,128]{1,0:T(8,128)S(1)} collective-permute-done((f32[16,128]{1,0:T(8,128)S(1)}, f32[16,128]{1,0:T(8,128)S(1)}, u32[]{:S(2)}, u32[]{:S(2)}) %collective-permute-start.7) | collective-permute-done | bytes 8224 | tf_op jit(solution)/shard_map/ppermute | solution.py:409
  66.0 1.5 %collective-permute-start.8 = (f32[16,128]{1,0:T(8,128)S(1)}, f32[16,128]{1,0:T(8,128)S(1)}, u32[]{:S(2)}, u32[]{:S(2)}) collective-permute-start(f32[16,128]{1,0:T(8,128)S(1)} %add.48), channel_id=1, source_target_pairs={{0,4},{1,5},{2,6},{3,7},{4,0},{5,1},{6,2},{7,3},{8,12},{9,13},{10,... | collective-permute-start | bytes 24584 | tf_op jit(solution)/shard_map/ppermute | solution.py:409
  67.5 3.0 %collective-permute-done.8 = f32[16,128]{1,0:T(8,128)S(1)} collective-permute-done((f32[16,128]{1,0:T(8,128)S(1)}, f32[16,128]{1,0:T(8,128)S(1)}, u32[]{:S(2)}, u32[]{:S(2)}) %collective-permute-start.8) | collective-permute-done | bytes 8224 | tf_op jit(solution)/shard_map/ppermute | solution.py:409
  70.6 3.0 %shard_map.111 = (f32[16,128]{1,0:T(8,128)S(1)}, f32[16,16]{1,0:T(8,128)}, f32[1,16]{1,0:T(1,128)}, f32[4,64,128]{2,1,0:T(8,128)}, f32[4,16,128]{2,1,0:T(8,128)S...) custom-call(s32[2]{0:T(128)S(1)} %pad_add_fusion.place, ...), custom_call_target="tpu_custom_call" | custom-call | flops 7241728 | bytes 2228224 | tf_op jit(solution)/shard_map/pallas_call | solution.py:26
  73.6 1.5 %collective-permute-start.10 = (f32[4,16,128]{2,1,0:T(8,128)S(1)}, f32[4,16,128]{2,1,0:T(8,128)S(1)}, u32[]{:S(2)}, u32[]{:S(2)}) collective-permute-start(f32[4,16,128]{2,1,0:T(8,128)S(1)} %get-tuple-element.37), channel_id=1, source_target_pairs={{0,16},{8,24},{16,0},{24,8},{1,17},{9,25},{17,1},{25,9},{2,18},{10... | collective-permute-start | bytes 98312 | tf_op jit(solution)/shard_map/ppermute | solution.py:420
  75.7 3.3 %shard_map.112 = f32[16,4,64,128]{3,2,1,0:T(8,128)} custom-call(s32[2]{0:T(128)S(1)} %pad_add_fusion.place, f32[16,128]{1,0:T(8,128)S(1)} %get-tuple-element.31.solved, f32[17,64,128]{2,1,0:T(8,128)S(1)} %get-tuple-element.26.order.low, f32[2,17,64,128]{3,2,1,0:T(8,128)S(1)} %get-tuple-element.28.mid, f32[9,64,128]{2,1,0:T(8,128)S(1)} %shard_map.109.out_a.high_a, ...), custom_call_target="tpu_custom_call" | custom-call | flops 14483456 | bytes 4456448 | tf_op jit(solution)/shard_map/pallas_call | solution.py:26
  (32 shorter events, 2.2 us)
Async XLA Ops:
  0.7 20.9 %copy-start = (f32[1,16,4,64,128]{4,3,2,1,0:T(8,128)S(1)}, f32[1,16,4,64,128]{4,3,2,1,0:T(8,128)}, u32[]{:S(2)}) copy-start(f32[1,16,4,64,128]{4,3,2,1,0:T(8,128)} %param.6) | copy-start | bytes 6291460
  0.7 20.9 %copy-start.1 = (f32[1,3,4,64,128]{4,3,2,1,0:T(8,128)S(1)}, f32[1,3,4,64,128]{4,3,2,1,0:T(8,128)}, u32[]{:S(2)}) copy-start(f32[1,3,4,64,128]{4,3,2,1,0:T(8,128)} %param.8) | copy-start | bytes 1179652
  0.7 20.9 %copy-start.2 = (f32[1,4,64,128]{3,2,1,0:T(8,128)S(1)}, f32[1,4,64,128]{3,2,1,0:T(8,128)}, u32[]{:S(2)}) copy-start(f32[1,4,64,128]{3,2,1,0:T(8,128)} %param.9) | copy-start | bytes 393220
  0.7 20.9 %copy-start.3 = (f32[1,4,64,128]{3,2,1,0:T(8,128)S(1)}, f32[1,4,64,128]{3,2,1,0:T(8,128)}, u32[]{:S(2)}) copy-start(f32[1,4,64,128]{3,2,1,0:T(8,128)} %param.10) | copy-start | bytes 393220
  0.7 20.9 %copy-start.4 = (f32[1,4,64,128]{3,2,1,0:T(8,128)S(1)}, f32[1,4,64,128]{3,2,1,0:T(8,128)}, u32[]{:S(2)}) copy-start(f32[1,4,64,128]{3,2,1,0:T(8,128)} %param.7) | copy-start | bytes 393220
  2.6 18.9 %collective-permute-start.2 = (f32[17,64,128]{2,1,0:T(8,128)S(1)}, f32[17,64,128]{2,1,0:T(8,128)}, u32[]{:S(2)}, u32[]{:S(2)}) collective-permute-start(f32[17,64,128]{2,1,0:T(8,128)S(1)} %shard_map.102), channel_id=1, source_target_pairs={{0,7},{1,2},{2,1},{3,4},{4,3},{5,6},{6,5},{7,0},{8,15},{9,10},{10,... | collective-permute-start | bytes 1671176 | tf_op jit(solution)/shard_map/ppermute | solution.py:362
  11.1 0.7 copy-start.5
  11.8 28.0 %collective-permute-start.1 = (f32[9,64,128]{2,1,0:T(8,128)}, f32[9,64,128]{2,1,0:T(8,128)}, u32[]{:S(2)}, u32[]{:S(2)}) collective-permute-start(f32[9,64,128]{2,1,0:T(8,128)} %get-tuple-element.23), channel_id=1, source_target_pairs={{0,1},{1,0},{2,3},{3,2},{4,5},{5,4},{6,7},{7,6},{8,9},{9,8},{10,11... | collective-permute-start | bytes 884744 | tf_op jit(solution)/shard_map/ppermute | solution.py:355
  12.6 14.9 %copy-start.6 = (f32[8,64,128]{2,1,0:T(8,128)S(1)}, f32[8,64,128]{2,1,0:T(8,128)}, u32[]{:S(2)}) copy-start(f32[8,64,128]{2,1,0:T(8,128)} %copy-done.5) | copy-start | bytes 786436
  23.0 26.5 %collective-permute-start.4 = (f32[17,64,128]{2,1,0:T(8,128)S(1)}, f32[17,64,128]{2,1,0:T(8,128)S(1)}, u32[]{:S(2)}, u32[]{:S(2)}) collective-permute-start(f32[17,64,128]{2,1,0:T(8,128)S(1)} %shard_map.103.order.bottom), channel_id=1, source_target_pairs={{0,7},{1,2},{2,1},{3,4},{4,3},{5,6},{6,5},{7,0},{8,15},{9,10},{10,... | collective-permute-start | bytes 1671176 | tf_op jit(solution)/shard_map/ppermute | solution.py:373
  27.5 17.7 %collective-permute-start = (f32[8,64,128]{2,1,0:T(8,128)S(1)}, f32[8,64,128]{2,1,0:T(8,128)S(1)}, u32[]{:S(2)}, u32[]{:S(2)}) collective-permute-start(f32[8,64,128]{2,1,0:T(8,128)S(1)} %copy-done.6), channel_id=1, source_target_pairs={{0,1},{1,0},{2,3},{3,2},{4,5},{5,4},{6,7},{7,6},{8,9},{9,8},{10,11... | collective-permute-start | bytes 786440 | tf_op jit(solution)/shard_map/ppermute | solution.py:356
  41.0 10.6 %collective-permute-start.5 = (f32[9,64,128]{2,1,0:T(8,128)S(1)}, f32[9,64,128]{2,1,0:T(8,128)S(1)}, u32[]{:S(2)}, u32[]{:S(2)}) collective-permute-start(f32[9,64,128]{2,1,0:T(8,128)S(1)} %shard_map.104.order.top_a.top), channel_id=1, source_target_pairs={{0,1},{1,0},{2,3},{3,2},{4,5},{5,4},{6,7},{7,6},{8,9},{9,8},{10,11... | collective-permute-start | bytes 884744 | tf_op jit(solution)/shard_map/ppermute | solution.py:379
  46.0 11.2 %collective-permute-start.3 = (f32[8,64,128]{2,1,0:T(8,128)S(1)}, f32[8,64,128]{2,1,0:T(8,128)S(1)}, u32[]{:S(2)}, u32[]{:S(2)}) collective-permute-start(f32[8,64,128]{2,1,0:T(8,128)S(1)} %shard_map.105.top_b.top), channel_id=1, source_target_pairs={{0,1},{1,0},{2,3},{3,2},{4,5},{5,4},{6,7},{7,6},{8,9},{9,8},{10,11... | collective-permute-start | bytes 786440 | tf_op jit(solution)/shard_map/ppermute | solution.py:385
  58.7 3.7 %collective-permute-start.6 = (f32[16,128]{1,0:T(8,128)S(1)}, f32[16,128]{1,0:T(8,128)S(1)}, u32[]{:S(2)}, u32[]{:S(2)}) collective-permute-start(f32[16,128]{1,0:T(8,128)S(1)} %get-tuple-element.27), channel_id=1, source_target_pairs={{0,1},{1,0},{2,3},{3,2},{4,5},{5,4},{6,7},{7,6},{8,9},{9,8},{10,11... | collective-permute-start | bytes 24584 | tf_op jit(solution)/shard_map/ppermute | solution.py:409
  62.4 3.7 %collective-permute-start.7 = (f32[16,128]{1,0:T(8,128)S(1)}, f32[16,128]{1,0:T(8,128)S(1)}, u32[]{:S(2)}, u32[]{:S(2)}) collective-permute-start(f32[16,128]{1,0:T(8,128)S(1)} %add.47), channel_id=1, source_target_pairs={{0,2},{1,3},{2,0},{3,1},{4,6},{5,7},{6,4},{7,5},{8,10},{9,11},{10,... | collective-permute-start | bytes 24584 | tf_op jit(solution)/shard_map/ppermute | solution.py:409
  66.0 4.6 %collective-permute-start.8 = (f32[16,128]{1,0:T(8,128)S(1)}, f32[16,128]{1,0:T(8,128)S(1)}, u32[]{:S(2)}, u32[]{:S(2)}) collective-permute-start(f32[16,128]{1,0:T(8,128)S(1)} %add.48), channel_id=1, source_target_pairs={{0,4},{1,5},{2,6},{3,7},{4,0},{5,1},{6,2},{7,3},{8,12},{9,13},{10,... | collective-permute-start | bytes 24584 | tf_op jit(solution)/shard_map/ppermute | solution.py:409
  73.6 5.5 %collective-permute-start.10 = (f32[4,16,128]{2,1,0:T(8,128)S(1)}, f32[4,16,128]{2,1,0:T(8,128)S(1)}, u32[]{:S(2)}, u32[]{:S(2)}) collective-permute-start(f32[4,16,128]{2,1,0:T(8,128)S(1)} %get-tuple-element.37), channel_id=1, source_target_pairs={{0,16},{8,24},{16,0},{24,8},{1,17},{9,25},{17,1},{25,9},{2,18},{10... | collective-permute-start | bytes 98312 | tf_op jit(solution)/shard_map/ppermute | solution.py:420
  75.1 4.0 %collective-permute-start.11 = (f32[4,16,128]{2,1,0:T(8,128)S(1)}, f32[4,16,128]{2,1,0:T(8,128)S(1)}, u32[]{:S(2)}, u32[]{:S(2)}) collective-permute-start(f32[4,16,128]{2,1,0:T(8,128)S(1)} %get-tuple-element.38), channel_id=1, source_target_pairs={{0,24},{8,16},{16,8},{24,0},{1,25},{9,17},{17,9},{25,1},{2,26},{10... | collective-permute-start | bytes 98312 | tf_op jit(solution)/shard_map/ppermute | solution.py:420
  75.1 4.0 %collective-permute-start.9 = (f32[4,16,128]{2,1,0:T(8,128)S(1)}, f32[4,16,128]{2,1,0:T(8,128)S(1)}, u32[]{:S(2)}, u32[]{:S(2)}) collective-permute-start(f32[4,16,128]{2,1,0:T(8,128)S(1)} %get-tuple-element.36), channel_id=1, source_target_pairs={{0,8},{8,0},{16,24},{24,16},{1,9},{9,1},{17,25},{25,17},{2,10},{10... | collective-permute-start | bytes 98312 | tf_op jit(solution)/shard_map/ppermute | solution.py:420

commit v3 on v2

--- a/solution.py
+++ b/solution.py
@@ -10,6 +10,7 @@
 
 
 SUB = 8
+TURNS = 800
 HIGH = lax.Precision.HIGHEST
 VMEM_SPEC = pl.BlockSpec(memory_space=pltpu.VMEM)
 SMEM_SPEC = pl.BlockSpec(memory_space=pltpu.SMEM)
@@ -22,15 +23,15 @@
     return 1.0 + 0.5 * jnp.sin(2.0 * math.pi * phase_step.astype(jnp.float32) / 64.0)
 
 
-def call(body, outs, specs, args, scratch=(), flops=0, moved=0):
+def call(body, outs, specs, args, scratch=(), flops=0, moved=0, out_specs=None, grant=16):
     return pl.pallas_call(
         body,
         out_shape=outs,
         in_specs=specs,
-        out_specs=jax.tree.map(lambda _: VMEM_SPEC, outs),
+        out_specs=out_specs or jax.tree.map(lambda _: VMEM_SPEC, outs),
         scratch_shapes=scratch,
         cost_estimate=pl.CostEstimate(flops=flops, transcendentals=0, bytes_accessed=moved),
-        compiler_params=pltpu.CompilerParams(vmem_limit_bytes=20 * 1024 * 1024),
+        compiler_params=pltpu.CompilerParams(vmem_limit_bytes=grant * 1024 * 1024),
     )(*args)
 
 
@@ -38,19 +39,29 @@
     return position + odd * (layers - 1 - 2 * position)
 
 
-def pack_kernel(count, layers, positions, cuts, place, dirs, adj, *rest):
-    outs, sems = rest[:-1], rest[-1]
-    odd = place[0]
-    copies = []
-    for k, (out, position) in enumerate(zip(outs, positions)):
-        layer = layer_of(odd, position, layers)
-        stop = min(cuts[k + 1], count)
-        size = stop - cuts[k]
-        copies.append(
-            pltpu.make_async_copy(dirs.at[pl.ds(cuts[k], size), layer], out.at[pl.ds(0, size)], sems.at[k])
-        )
-        if cuts[k + 1] > count:
-            copies.append(pltpu.make_async_copy(adj.at[layer], out.at[size], sems.at[2]))
+def pack_kernel(count, layers, position, start, stop, place, dirs, adj, out, sems):
+    layer = layer_of(place[0], position, layers)
+    size = min(stop, count) - start
+    copies = [
+        pltpu.make_async_copy(dirs.at[pl.ds(start, size), layer], out.at[pl.ds(0, size)], sems.at[0])
+    ]
+    if stop > count:
+        copies.append(pltpu.make_async_copy(adj.at[layer], out.at[size], sems.at[1]))
+    for copy in copies:
+        copy.start()
+    for copy in copies:
+        copy.wait()
+
+
+def pack_both(count, layers, position, cut, place, dirs, adj, first, second, sems):
+    layer = layer_of(place[0], position, layers)
+    copies = [
+        pltpu.make_async_copy(dirs.at[pl.ds(0, cut), layer], first, sems.at[0]),
+        pltpu.make_async_copy(
+            dirs.at[pl.ds(cut, count - cut), layer], second.at[pl.ds(0, count - cut)], sems.at[1]
+        ),
+        pltpu.make_async_copy(adj.at[layer], second.at[count - cut], sems.at[2]),
+    ]
     for copy in copies:
         copy.start()
     for copy in copies:
@@ -154,7 +165,15 @@
     )
 
 
-def top_kernel(count, layers, start, place, half, dirs, adj, halo, vel, dif, src, order, edge):
+def top_kernel(
+    count, layers, start, turns, place, half, dirs, adj, halo, vel, dif, src, order, edge, turned
+):
+    def turn(step, total):
+        turned[0] = turned[0] + step
+        return total
+
+    turned[0] = 0
+    lax.fori_loop(0, turns * (place[1] % 2), turn, 0)
     odd = place[0]
     _, _, ny, nz = dirs.shape
     here, far = layer_of(odd, layers - 1, layers), layer_of(odd, layers - 2, layers)
@@ -267,8 +286,7 @@
 
 
 def solve_kernel(
-    count, layers, pieces, cells, place, gram, low, mid, high_a, high_b, early,
-    solved, factor, along, shadow, *parts,
+    count, layers, pieces, cells, place, gram, low, mid, high_a, high_b, early, solved, shadow, *parts
 ):
     odd, seg = place[0], place[1]
     _, ny, nz = low.shape
@@ -277,12 +295,16 @@
     lane = lax.broadcasted_iota(jnp.int32, shape, 1)
     table = jnp.where(lane <= count, gram[...] / cells, 0.0)
     table = jnp.where(lane == row + count + 1, 1.0, table)
+    scale = jnp.ones(shape, jnp.float32)
+    columns = [jnp.broadcast_to(table[:, j : j + 1], shape) for j in range(count)]
     for k in range(count):
-        pivot_row = table[k : k + 1, :]
-        root = jnp.sqrt(pivot_row[:, k : k + 1])
-        scaled = pivot_row / root
-        column = table[:, k : k + 1] / root
-        table = jnp.where(row == k, scaled, jnp.where(row > k, table - column * scaled, table))
+        pivot = jnp.broadcast_to(columns[k][k : k + 1, :], shape)
+        scale = jnp.where(row == k, pivot, scale)
+        ratio = jnp.where(row > k, columns[k] * (1.0 / pivot), 0.0)
+        for j in range(k + 1, count):
+            columns[j] = columns[j] - ratio * jnp.broadcast_to(columns[j][k : k + 1, :], shape)
+        table = table - ratio * jnp.broadcast_to(table[k : k + 1, :], shape)
+    table = table / jnp.sqrt(scale)
     table = jnp.where((lane < count) & (lane < row), 0.0, table)
     solved[...] = table
     weights = jnp.sum(table[:, count : count + 1] * table, axis=0, keepdims=True)
@@ -303,27 +325,37 @@
         begin = pl.multiple_of((seg ^ k) * step, step)
         rows = pl.ds(begin, step)
         part[...] = shadow[:, rows, :] + early[:, rows, :]
+
+
+def basis_kernel(
+    count, layers, place, weights, solved, shadow, low, mid, high_a, high_b,
+    out, factor, along, shadow_out, held, sems,
+):
+    odd = place[0]
+    _, ny, _ = low.shape
+    block = min(ny, 8 * SUB)
+    copies = [pltpu.make_async_copy(shadow, shadow_out, sems.at[count])]
+    copies[0].start()
+    table = solved[...]
     factor[...] = table[:, :count]
     eye = (
         lax.broadcasted_iota(jnp.int32, (count, count), 0) == lax.broadcasted_iota(jnp.int32, (count, count), 1)
     )
     along[...] = jnp.sum(jnp.where(eye, table[:, count : count + 1], 0.0), axis=0, keepdims=True)
-
-
-def basis_kernel(count, layers, place, solved, low, mid, high_a, high_b, out):
-    odd = place[0]
-    _, ny, _ = low.shape
-    block = min(ny, 8 * SUB)
-    for position in range(layers):
-        layer = layer_of(odd, position, layers)
-        read = result_at(position, layers, low, mid, high_a, high_b)
-        for base in range(0, ny, block):
-            rows = slice(base, base + block)
-            for i in range(count):
-                total = solved[i, count + 1] * read(0, rows)
+    for i in range(count):
+        for position in range(layers):
+            layer = layer_of(odd, position, layers)
+            read = result_at(position, layers, low, mid, high_a, high_b)
+            for base in range(0, ny, block):
+                rows = slice(base, base + block)
+                total = weights[i, count + 1] * read(0, rows)
                 for j in range(1, i + 1):
-                    total = total + solved[i, count + 1 + j] * read(j, rows)
-                out[i, layer, rows, :] = total
+                    total = total + weights[i, count + 1 + j] * read(j, rows)
+                held[i, layer, rows, :] = total
+        copies.append(pltpu.make_async_copy(held.at[i], out.at[i], sems.at[i]))
+        copies[-1].start()
+    for copy in copies:
+        copy.wait()
 
 
 def window(directions, adjoint, velocity, diffusivity, objective_source, segment_start):
@@ -331,7 +363,7 @@
         directions[0], adjoint[0], velocity[0], diffusivity[0], objective_source[0],
     )
     count, layers, ny, nz = dirs.shape
-    fields, part_a = count + 1, (count + 2) // 2
+    fields, part_a = count + 1, (2 * count) // 3
     spaces, segs = lax.axis_size("space"), lax.axis_size("seg")
     assert spaces & (spaces - 1) == 0 and segs & (segs - 1) == 0 and layers >= 3
     odd = lax.axis_index("space") % 2
@@ -347,18 +379,22 @@
     flow = (vel, dif, src)
 
     dirs_hbm, adj_hbm = (pltpu.with_memory_space_constraint(x, pltpu.HBM) for x in (dirs, adj))
+
+    def pack(position, start, stop, shape):
+        return call(
+            functools.partial(pack_kernel, count, layers, position, start, stop), shape,
+            [ss, hs, hs], (place, dirs_hbm, adj_hbm),
+            scratch=[pltpu.SemaphoreType.DMA((2,))], moved=2 * layer_bytes, grant=2,
+        )
+
     near_a, near_b = call(
-        functools.partial(pack_kernel, count, layers, (layers - 1, layers - 1), (0, part_a, fields)),
-        [edge_a, edge_b], [ss, hs, hs], (place, dirs_hbm, adj_hbm),
-        scratch=[pltpu.SemaphoreType.DMA((3,))], moved=2 * layer_bytes,
+        functools.partial(pack_both, count, layers, layers - 1, part_a), [edge_a, edge_b],
+        [ss, hs, hs], (place, dirs_hbm, adj_hbm),
+        scratch=[pltpu.SemaphoreType.DMA((3,))], moved=2 * layer_bytes, grant=3,
     )
     halo_a = lax.ppermute(near_a, "space", pair_one)
     halo_b = lax.ppermute(near_b, "space", pair_one)
-    (far,) = call(
-        functools.partial(pack_kernel, count, layers, (0,), (0, fields)),
-        [edge], [ss, hs, hs], (place, dirs_hbm, adj_hbm),
-        scratch=[pltpu.SemaphoreType.DMA((3,))], moved=2 * layer_bytes,
-    )
+    far = pack(0, 0, fields, edge)
     halo_far = lax.ppermute(far, "space", pair_two)
     inner = call(
         functools.partial(inner_kernel, count, layers), f32((layers - 2, fields, ny, nz)),
@@ -372,14 +408,16 @@
     )
     bottom_far = lax.ppermute(bottom, "space", pair_two)
     top_a = call(
-        functools.partial(top_kernel, count, layers, 0), edge_a,
+        functools.partial(top_kernel, count, layers, 0, 0), edge_a,
         [ss, ss] + [vs] * 6 + [anys], (place, half, dirs, adj, halo_a) + flow + (bottom,),
+        scratch=[pltpu.SMEM((1,), jnp.int32)],
         flops=layer_flops // 2, moved=2 * layer_bytes,
     )
     near_top_a = lax.ppermute(top_a, "space", pair_one)
     top_b = call(
-        functools.partial(top_kernel, count, layers, part_a), edge_b,
+        functools.partial(top_kernel, count, layers, part_a, TURNS), edge_b,
         [ss, ss] + [vs] * 6 + [anys], (place, half, dirs, adj, halo_b) + flow + (top_a,),
+        scratch=[pltpu.SMEM((1,), jnp.int32)],
         flops=layer_flops // 2, moved=2 * layer_bytes,
     )
     near_top_b = lax.ppermute(top_b, "space", pair_one)
@@ -409,21 +447,23 @@
         gram = gram + lax.ppermute(gram, "space", [(i, i ^ reach) for i in range(spaces)])
         reach *= 2
     piece = f32((layers, ny // segs, nz))
-    solved, factor, along, shadow, *parts = call(
+    solved, shadow, *parts = call(
         functools.partial(solve_kernel, count, layers, segs, float(layers * ny * nz * spaces)),
-        [f32((count, 128)), f32((count, count)), f32((1, count)), f32((layers, ny, nz))] + [piece] * segs,
+        [f32((count, 128)), f32((layers, ny, nz))] + [piece] * segs,
         [ss] + [vs] * 6, (place, gram, low, mid, high_a, high_b, early),
         flops=4 * layer_flops, moved=4 * layer_bytes,
     )
     gradient = parts[0]
     for k in range(1, segs):
         gradient = gradient + lax.ppermute(parts[k], "seg", [(i, i ^ k) for i in range(segs)])
-    basis = call(
-        functools.partial(basis_kernel, count, layers), f32((count, layers, ny, nz)),
-        [ss, ss] + [vs] * 4, (place, solved, low, mid, high_a, high_b),
-        flops=8 * layer_flops, moved=8 * layer_bytes,
-    )
-    return basis[None], factor[None], along, shadow[None], gradient
+    basis, factor, along, shadow_out = call(
+        functools.partial(basis_kernel, count, layers),
+        [f32((count, layers, ny, nz)), f32((count, count)), f32((1, count)), f32((layers, ny, nz))],
+        [ss, ss] + [vs] * 6, (place, solved, solved, shadow, low, mid, high_a, high_b),
+        scratch=[pltpu.VMEM((count, layers, ny, nz), jnp.float32), pltpu.SemaphoreType.DMA((count + 1,))],
+        flops=8 * layer_flops, moved=8 * layer_bytes, out_specs=[hs, vs, vs, hs],
+    )
+    return basis[None], factor[None], along, shadow_out[None], gradient
 
 
 def solution(mesh):

time: 79.9 us -> 76.1 us (0.952)
  waiting for transfers between devices: 41.1 us -> 38.5 us
  Pallas kernels: 21.1 us -> 19.2 us
    ppermute x1, waiting for transfers between devices: 4.82 us -> 1.67 us  [window(): near_top_b = lax.ppermute(top_b, 'space', pair_one)]
    pallas_call x12, Pallas kernels: 21.1 us -> 19.2 us  [call(): pl.pallas_call(body, out_shape=outs, in_specs=specs, out_specs=out_specs...]
  transfers between devices with their start and end apart: 12 -> 12, of which waited for: 8 -> 8; matrix products, arithmetic and copies ran while one was open for 0% -> 0% of each run, Pallas kernels for 18% -> 19%
where the time goes in v3:
time: 76.1 us; the launch traced here: 75.9 us
  waiting for transfers between devices  38.5 us (51%)
  Pallas kernels  19.2 us (25%)
  starting transfers between devices  15 us (20%)
  between operations  1.67 us (2%)
  other arithmetic  0.79 us (1%)
    pallas_call x12, Pallas kernels, call(): pl.pallas_call(body, out_shape=outs, in_specs=specs, out_specs=out_specs...  19.2 us
    ppermute x1, waiting for transfers between devices, window(): halo_a = lax.ppermute(near_a, 'space', pair_one)  13 us
    ppermute x3, waiting for transfers between devices, window(): lax.ppermute(gram, 'space', [(i, i ^ reach) for i in range(spaces)])  10.4 us
    ppermute x1, waiting for transfers between devices, window(): halo_far = lax.ppermute(far, 'space', pair_two)  8.87 us
    ppermute x1, starting transfers between devices, window(): halo_far = lax.ppermute(far, 'space', pair_two)  6.1 us
    ppermute x1, starting transfers between devices, window(): bottom_far = lax.ppermute(bottom, 'space', pair_two)  4.5 us
    ppermute x1, waiting for transfers between devices, window(): halo_b = lax.ppermute(near_b, 'space', pair_one)  3.5 us
    ppermute x3, starting transfers between devices, window(): lax.ppermute(parts[k], 'seg', [(i, i ^ k) for i in range(segs)])  2.7 us
  transfers between devices with their start and end apart: 12, of which 8 were waited for; matrix products, arithmetic and copies ran while one was open for 0% of the time, Pallas kernels for 19%

profile of v3, /device:TPU:0, one launch (start us, length us, event | category | flops | bytes accessed | tf_op | source)
XLA Modules:
  0.0 75.9 jit_solution(11366616868007865132)
XLA Ops:
  0.7 1.9 %shard_map.102 = f32[17,64,128]{2,1,0:T(8,128)S(1)} custom-call(s32[2]{0:T(128)S(1)} %pad_add_fusion.place, f32[16,4,64,128]{3,2,1,0:T(8,128)} %bitcast.17, f32[4,64,128]{2,1,0:T(8,128)} %bitcast.47), custom_call_target="tpu_custom_call" | custom-call | bytes 1114112 | tf_op jit(solution)/shard_map/pallas_call | solution.py:27
  2.6 6.1 %collective-permute-start.2 = (f32[17,64,128]{2,1,0:T(8,128)S(1)}, f32[17,64,128]{2,1,0:T(8,128)}, u32[]{:S(2)}, u32[]{:S(2)}) collective-permute-start(f32[17,64,128]{2,1,0:T(8,128)S(1)} %shard_map.102), channel_id=1, source_target_pairs={{0,7},{1,2},{2,1},{3,4},{4,3},{5,6},{6,5},{7,0},{8,15},{9,10},{10,... | collective-permute-start | bytes 1671176 | tf_op jit(solution)/shard_map/ppermute | solution.py:398
  8.7 2.3 %shard_map.101 = (f32[10,64,128]{2,1,0:T(8,128)}, f32[7,64,128]{2,1,0:T(8,128)S(1)}) custom-call(s32[2]{0:T(128)S(1)} %pad_add_fusion.place, f32[16,4,64,128]{3,2,1,0:T(8,128)} %bitcast.18, f32[4,64,128]{2,1,0:T(8,128)} %bitcast.48), custom_call_target="tpu_custom_call" | custom-call | bytes 1114112 | tf_op jit(solution)/shard_map/pallas_call | solution.py:27
  12.7 8.9 %collective-permute-done.2.halo = f32[17,64,128]{2,1,0:T(8,128)} collective-permute-done((f32[17,64,128]{2,1,0:T(8,128)S(1)}, f32[17,64,128]{2,1,0:T(8,128)}, u32[]{:S(2)}, u32[]{:S(2)}) %collective-permute-start.2) | collective-permute-done | bytes 557088 | tf_op jit(solution)/shard_map/ppermute | solution.py:398
  21.6 1.4 %shard_map.103.order.bottom = f32[17,64,128]{2,1,0:T(8,128)S(1)} custom-call(s32[2]{0:T(128)S(1)} %pad_add_fusion.place, f32[2]{0:T(128)S(1)} %pad_maximum_fusion.half, f32[16,4,64,128]{3,2,1,0:T(8,128)S(1)} %bitcast.19, f32[4,64,128]{2,1,0:T(8,128)S(1)} %bitcast.49, f32[17,64,128]{2,1,0:T(8,128)} %collective-permute-done.2.halo, ...), custom_call_target="tpu_custom_call" | custom-call | flops 1810432 | bytes 2228224 | tf_op jit(solution)/shard_map/pallas_call | solution.py:27
  23.0 4.5 %collective-permute-start.4 = (f32[17,64,128]{2,1,0:T(8,128)S(1)}, f32[17,64,128]{2,1,0:T(8,128)S(1)}, u32[]{:S(2)}, u32[]{:S(2)}) collective-permute-start(f32[17,64,128]{2,1,0:T(8,128)S(1)} %shard_map.103.order.bottom), channel_id=1, source_target_pairs={{0,7},{1,2},{2,1},{3,4},{4,3},{5,6},{6,5},{7,0},{8,15},{9,10},{10,... | collective-permute-start | bytes 1671176 | tf_op jit(solution)/shard_map/ppermute | solution.py:409
  27.5 13.0 %collective-permute-done.1.halo = f32[10,64,128]{2,1,0:T(8,128)} collective-permute-done((f32[10,64,128]{2,1,0:T(8,128)}, f32[10,64,128]{2,1,0:T(8,128)}, u32[]{:S(2)}, u32[]{:S(2)}) %collective-permute-start.1) | collective-permute-done | bytes 327712 | tf_op jit(solution)/shard_map/ppermute | solution.py:395
  40.5 1.2 %shard_map.104.order.top_a.top = f32[10,64,128]{2,1,0:T(8,128)S(1)} custom-call(s32[2]{0:T(128)S(1)} %pad_add_fusion.place, f32[2]{0:T(128)S(1)} %pad_maximum_fusion.half, f32[16,4,64,128]{3,2,1,0:T(8,128)S(1)} %bitcast.20, f32[4,64,128]{2,1,0:T(8,128)S(1)} %bitcast.50, f32[10,64,128]{2,1,0:T(8,128)} %collective-permute-done.1.halo, ...), custom_call_target="tpu_custom_call" | custom-call | flops 905216 | bytes 1114112 | tf_op jit(solution)/shard_map/pallas_call | solution.py:27
  41.8 3.5 %collective-permute-done.halo = f32[7,64,128]{2,1,0:T(8,128)S(1)} collective-permute-done((f32[7,64,128]{2,1,0:T(8,128)S(1)}, f32[7,64,128]{2,1,0:T(8,128)S(1)}, u32[]{:S(2)}, u32[]{:S(2)}) %collective-permute-start) | collective-permute-done | bytes 229408 | tf_op jit(solution)/shard_map/ppermute | solution.py:396
  46.2 1.2 %shard_map.106.inner = f32[2,17,64,128]{3,2,1,0:T(8,128)S(1)} custom-call(s32[2]{0:T(128)S(1)} %pad_add_fusion.place, f32[2]{0:T(128)S(1)} %pad_maximum_fusion.half, f32[16,4,64,128]{3,2,1,0:T(8,128)S(1)} %bitcast.22, f32[4,64,128]{2,1,0:T(8,128)S(1)} %bitcast.52, f32[3,4,64,128]{3,2,1,0:T(8,128)S(1)} %bitcast.26, f32[4,64,128]{2,1,0:T(8,128)S(1)} %bitcast.34, ...), custom_call_target="tpu_custom_call" | custom-call | flops 3620864 | bytes 3342336 | tf_op jit(solution)/shard_map/pallas_call | solution.py:27
  47.4 2.2 %shard_map.107 = (f32[2,17,64,128]{3,2,1,0:T(8,128)S(1)}, f32[128,136]{1,0:T(8,128)S(1)}, f32[4,64,128]{2,1,0:T(8,128)S(1)}) custom-call(s32[2]{0:T(128)S(1)} %pad_add_fusion.place, f32[2]{0:T(128)S(1)} %pad_maximum_fusion.half, f32[17,64,128]{2,1,0:T(8,128)S(1)} %shard_map.103.order.bottom, f32[2,17,64,128]{3,2,1,0:T(8,128)S(1)} %shard_map.106.inner, ...), custom_call_target="tpu_custom_call" | custom-call | flops 14483456 | bytes 3342336 | tf_op jit(solution)/shard_map/pallas_call | solution.py:27
  49.6 1.5 %shard_map.108 = (f32[17,64,128]{2,1,0:T(8,128)S(1)}, f32[128,136]{1,0:T(8,128)S(1)}) custom-call(s32[2]{0:T(128)S(1)} %pad_add_fusion.place, f32[2]{0:T(128)S(1)} %pad_maximum_fusion.half, f32[17,64,128]{2,1,0:T(8,128)S(1)} %shard_map.103.order.bottom, f32[2,17,64,128]{3,2,1,0:T(8,128)S(1)} %shard_map.106.inner, ...), custom_call_target="tpu_custom_call" | custom-call | flops 7241728 | bytes 2228224 | tf_op jit(solution)/shard_map/pallas_call | solution.py:27
  51.1 1.2 %collective-permute-done.5.halo = f32[10,64,128]{2,1,0:T(8,128)S(1)} collective-permute-done((f32[10,64,128]{2,1,0:T(8,128)S(1)}, f32[10,64,128]{2,1,0:T(8,128)S(1)}, u32[]{:S(2)}, u32[]{:S(2)}) %collective-permute-start.5) | collective-permute-done | bytes 327712 | tf_op jit(solution)/shard_map/ppermute | solution.py:416
  52.3 0.8 %shard_map.109.out_a.high_a = f32[10,64,128]{2,1,0:T(8,128)S(1)} custom-call(s32[2]{0:T(128)S(1)} %pad_add_fusion.place, f32[2]{0:T(128)S(1)} %pad_maximum_fusion.half, f32[10,64,128]{2,1,0:T(8,128)S(1)} %shard_map.104.order.top_a.top, f32[2,17,64,128]{3,2,1,0:T(8,128)S(1)} %shard_map.106.inner, f32[10,64,128]{2,1,0:T(8,128)S(1)} %collective-permute-done.5.halo, ...), custom_call_target="tpu_custom_call" | custom-call | flops 905216 | bytes 1114112 | tf_op jit(solution)/shard_map/pallas_call | solution.py:27
  53.0 1.7 %collective-permute-done.3.halo = f32[7,64,128]{2,1,0:T(8,128)S(1)} collective-permute-done((f32[7,64,128]{2,1,0:T(8,128)S(1)}, f32[7,64,128]{2,1,0:T(8,128)S(1)}, u32[]{:S(2)}, u32[]{:S(2)}) %collective-permute-start.3) | collective-permute-done | bytes 229408 | tf_op jit(solution)/shard_map/ppermute | solution.py:423
  54.7 1.5 %shard_map.110 = (f32[7,64,128]{2,1,0:T(8,128)S(1)}, f32[16,128]{1,0:T(8,128)S(1)}) custom-call(s32[2]{0:T(128)S(1)} %pad_add_fusion.place, f32[2]{0:T(128)S(1)} %pad_maximum_fusion.half, f32[7,64,128]{2,1,0:T(8,128)S(1)} %shard_map.105.top_b.top, f32[2,17,64,128]{3,2,1,0:T(8,128)S(1)} %shard_map.106.inner, f32[7,64,128]{2,1,0:T(8,128)S(1)} %collective-permute-done.3.halo, ...), custom_call_target="tpu_custom_call" | custom-call | flops 3620864 | bytes 1114112 | tf_op jit(solution)/shard_map/pallas_call | solution.py:27
  56.2 3.7 %collective-permute-done.6 = f32[16,128]{1,0:T(8,128)S(1)} collective-permute-done((f32[16,128]{1,0:T(8,128)S(1)}, f32[16,128]{1,0:T(8,128)S(1)}, u32[]{:S(2)}, u32[]{:S(2)}) %collective-permute-start.6) | collective-permute-done | bytes 8224 | tf_op jit(solution)/shard_map/ppermute | solution.py:447
  59.9 3.6 %collective-permute-done.7 = f32[16,128]{1,0:T(8,128)S(1)} collective-permute-done((f32[16,128]{1,0:T(8,128)S(1)}, f32[16,128]{1,0:T(8,128)S(1)}, u32[]{:S(2)}, u32[]{:S(2)}) %collective-permute-start.7) | collective-permute-done | bytes 8224 | tf_op jit(solution)/shard_map/ppermute | solution.py:447
  63.5 1.5 %collective-permute-start.8 = (f32[16,128]{1,0:T(8,128)S(1)}, f32[16,128]{1,0:T(8,128)S(1)}, u32[]{:S(2)}, u32[]{:S(2)}) collective-permute-start(f32[16,128]{1,0:T(8,128)S(1)} %add.48), channel_id=1, source_target_pairs={{0,4},{1,5},{2,6},{3,7},{4,0},{5,1},{6,2},{7,3},{8,12},{9,13},{10,... | collective-permute-start | bytes 24584 | tf_op jit(solution)/shard_map/ppermute | solution.py:447
  65.0 3.0 %collective-permute-done.8 = f32[16,128]{1,0:T(8,128)S(1)} collective-permute-done((f32[16,128]{1,0:T(8,128)S(1)}, f32[16,128]{1,0:T(8,128)S(1)}, u32[]{:S(2)}, u32[]{:S(2)}) %collective-permute-start.8) | collective-permute-done | bytes 8224 | tf_op jit(solution)/shard_map/ppermute | solution.py:447
  68.1 1.2 %shard_map.111 = (f32[16,128]{1,0:T(8,128)S(1)}, f32[4,64,128]{2,1,0:T(8,128)S(1)}, f32[4,16,128]{2,1,0:T(8,128)S(1)}, f32[4,16,128]{2,1,0:T(8,128)S(1)}, f32[4,...) custom-call(s32[2]{0:T(128)S(1)} %pad_add_fusion.place, f32[16,128]{1,0:T(8,128)S(1)} %add.49.gram, ...), custom_call_target="tpu_custom_call" | custom-call | flops 7241728 | bytes 2228224 | tf_op jit(solution)/shard_map/pallas_call | solution.py:27
  69.3 1.6 %collective-permute-start.10 = (f32[4,16,128]{2,1,0:T(8,128)S(1)}, f32[4,16,128]{2,1,0:T(8,128)S(1)}, u32[]{:S(2)}, u32[]{:S(2)}) collective-permute-start(f32[4,16,128]{2,1,0:T(8,128)S(1)} %get-tuple-element.41), channel_id=1, source_target_pairs={{0,16},{8,24},{16,0},{24,8},{1,17},{9,25},{17,1},{25,9},{2,18},{10... | collective-permute-start | bytes 98312 | tf_op jit(solution)/shard_map/ppermute | solution.py:458
  70.9 1.1 %collective-permute-start.11 = (f32[4,16,128]{2,1,0:T(8,128)S(1)}, f32[4,16,128]{2,1,0:T(8,128)S(1)}, u32[]{:S(2)}, u32[]{:S(2)}) collective-permute-start(f32[4,16,128]{2,1,0:T(8,128)S(1)} %get-tuple-element.42), channel_id=1, source_target_pairs={{0,24},{8,16},{16,8},{24,0},{1,25},{9,17},{17,9},{25,1},{2,26},{10... | collective-permute-start | bytes 98312 | tf_op jit(solution)/shard_map/ppermute | solution.py:458
  72.0 3.2 %shard_map.112 = (f32[16,4,64,128]{3,2,1,0:T(8,128)}, f32[16,16]{1,0:T(8,128)}, f32[1,16]{1,0:T(1,128)}, f32[4,64,128]{2,1,0:T(8,128)}) custom-call(s32[2]{0:T(128)S(1)} %pad_add_fusion.place, f32[16,128]{1,0:T(8,128)S(1)} %get-tuple-element.33.weights.solved, f32[16,128]{1,0:T(8,128)S(1)} %get-tuple-element.33.weights.solved, ...), custom_call_target="tpu_custom_call" | custom-call | flops 14483456 | bytes 4456448 | tf_op jit(solution)/shard_map/pallas_call | solution.py:27
  (32 shorter events, 2.4 us)
Async XLA Ops:
  0.7 20.8 %copy-start = (f32[1,16,4,64,128]{4,3,2,1,0:T(8,128)S(1)}, f32[1,16,4,64,128]{4,3,2,1,0:T(8,128)}, u32[]{:S(2)}) copy-start(f32[1,16,4,64,128]{4,3,2,1,0:T(8,128)} %param.6) | copy-start | bytes 6291460
  0.7 20.8 %copy-start.1 = (f32[1,3,4,64,128]{4,3,2,1,0:T(8,128)S(1)}, f32[1,3,4,64,128]{4,3,2,1,0:T(8,128)}, u32[]{:S(2)}) copy-start(f32[1,3,4,64,128]{4,3,2,1,0:T(8,128)} %param.8) | copy-start | bytes 1179652
  0.7 20.8 %copy-start.2 = (f32[1,4,64,128]{3,2,1,0:T(8,128)S(1)}, f32[1,4,64,128]{3,2,1,0:T(8,128)}, u32[]{:S(2)}) copy-start(f32[1,4,64,128]{3,2,1,0:T(8,128)} %param.9) | copy-start | bytes 393220
  0.7 20.8 %copy-start.3 = (f32[1,4,64,128]{3,2,1,0:T(8,128)S(1)}, f32[1,4,64,128]{3,2,1,0:T(8,128)}, u32[]{:S(2)}) copy-start(f32[1,4,64,128]{3,2,1,0:T(8,128)} %param.10) | copy-start | bytes 393220
  0.7 20.9 %copy-start.4 = (f32[1,4,64,128]{3,2,1,0:T(8,128)S(1)}, f32[1,4,64,128]{3,2,1,0:T(8,128)}, u32[]{:S(2)}) copy-start(f32[1,4,64,128]{3,2,1,0:T(8,128)} %param.7) | copy-start | bytes 393220
  2.6 18.9 %collective-permute-start.2 = (f32[17,64,128]{2,1,0:T(8,128)S(1)}, f32[17,64,128]{2,1,0:T(8,128)}, u32[]{:S(2)}, u32[]{:S(2)}) collective-permute-start(f32[17,64,128]{2,1,0:T(8,128)S(1)} %shard_map.102), channel_id=1, source_target_pairs={{0,7},{1,2},{2,1},{3,4},{4,3},{5,6},{6,5},{7,0},{8,15},{9,10},{10,... | collective-permute-start | bytes 1671176 | tf_op jit(solution)/shard_map/ppermute | solution.py:398
  11.1 0.7 copy-start.5
  11.8 28.8 %collective-permute-start.1 = (f32[10,64,128]{2,1,0:T(8,128)}, f32[10,64,128]{2,1,0:T(8,128)}, u32[]{:S(2)}, u32[]{:S(2)}) collective-permute-start(f32[10,64,128]{2,1,0:T(8,128)} %get-tuple-element.25), channel_id=1, source_target_pairs={{0,1},{1,0},{2,3},{3,2},{4,5},{5,4},{6,7},{7,6},{8,9},{9,8},{10,11... | collective-permute-start | bytes 983048 | tf_op jit(solution)/shard_map/ppermute | solution.py:395
  12.6 14.9 %copy-start.6 = (f32[7,64,128]{2,1,0:T(8,128)S(1)}, f32[7,64,128]{2,1,0:T(8,128)}, u32[]{:S(2)}) copy-start(f32[7,64,128]{2,1,0:T(8,128)} %copy-done.5) | copy-start | bytes 688132
  23.0 26.6 %collective-permute-start.4 = (f32[17,64,128]{2,1,0:T(8,128)S(1)}, f32[17,64,128]{2,1,0:T(8,128)S(1)}, u32[]{:S(2)}, u32[]{:S(2)}) collective-permute-start(f32[17,64,128]{2,1,0:T(8,128)S(1)} %shard_map.103.order.bottom), channel_id=1, source_target_pairs={{0,7},{1,2},{2,1},{3,4},{4,3},{5,6},{6,5},{7,0},{8,15},{9,10},{10,... | collective-permute-start | bytes 1671176 | tf_op jit(solution)/shard_map/ppermute | solution.py:409
  27.5 17.8 %collective-permute-start = (f32[7,64,128]{2,1,0:T(8,128)S(1)}, f32[7,64,128]{2,1,0:T(8,128)S(1)}, u32[]{:S(2)}, u32[]{:S(2)}) collective-permute-start(f32[7,64,128]{2,1,0:T(8,128)S(1)} %copy-done.6), channel_id=1, source_target_pairs={{0,1},{1,0},{2,3},{3,2},{4,5},{5,4},{6,7},{7,6},{8,9},{9,8},{10,11... | collective-permute-start | bytes 688136 | tf_op jit(solution)/shard_map/ppermute | solution.py:396
  41.7 10.5 %collective-permute-start.5 = (f32[10,64,128]{2,1,0:T(8,128)S(1)}, f32[10,64,128]{2,1,0:T(8,128)S(1)}, u32[]{:S(2)}, u32[]{:S(2)}) collective-permute-start(f32[10,64,128]{2,1,0:T(8,128)S(1)} %shard_map.104.order.top_a.top), channel_id=1, source_target_pairs={{0,1},{1,0},{2,3},{3,2},{4,5},{5,4},{6,7},{7,6},{8,9},{9,8},{10,11... | collective-permute-start | bytes 983048 | tf_op jit(solution)/shard_map/ppermute | solution.py:416
  46.1 8.6 %collective-permute-start.3 = (f32[7,64,128]{2,1,0:T(8,128)S(1)}, f32[7,64,128]{2,1,0:T(8,128)S(1)}, u32[]{:S(2)}, u32[]{:S(2)}) collective-permute-start(f32[7,64,128]{2,1,0:T(8,128)S(1)} %shard_map.105.top_b.top), channel_id=1, source_target_pairs={{0,1},{1,0},{2,3},{3,2},{4,5},{5,4},{6,7},{7,6},{8,9},{9,8},{10,11... | collective-permute-start | bytes 688136 | tf_op jit(solution)/shard_map/ppermute | solution.py:423
  56.2 3.7 %collective-permute-start.6 = (f32[16,128]{1,0:T(8,128)S(1)}, f32[16,128]{1,0:T(8,128)S(1)}, u32[]{:S(2)}, u32[]{:S(2)}) collective-permute-start(f32[16,128]{1,0:T(8,128)S(1)} %get-tuple-element.29), channel_id=1, source_target_pairs={{0,1},{1,0},{2,3},{3,2},{4,5},{5,4},{6,7},{7,6},{8,9},{9,8},{10,11... | collective-permute-start | bytes 24584 | tf_op jit(solution)/shard_map/ppermute | solution.py:447
  59.9 3.7 %collective-permute-start.7 = (f32[16,128]{1,0:T(8,128)S(1)}, f32[16,128]{1,0:T(8,128)S(1)}, u32[]{:S(2)}, u32[]{:S(2)}) collective-permute-start(f32[16,128]{1,0:T(8,128)S(1)} %add.47), channel_id=1, source_target_pairs={{0,2},{1,3},{2,0},{3,1},{4,6},{5,7},{6,4},{7,5},{8,10},{9,11},{10,... | collective-permute-start | bytes 24584 | tf_op jit(solution)/shard_map/ppermute | solution.py:447
  63.5 4.6 %collective-permute-start.8 = (f32[16,128]{1,0:T(8,128)S(1)}, f32[16,128]{1,0:T(8,128)S(1)}, u32[]{:S(2)}, u32[]{:S(2)}) collective-permute-start(f32[16,128]{1,0:T(8,128)S(1)} %add.48), channel_id=1, source_target_pairs={{0,4},{1,5},{2,6},{3,7},{4,0},{5,1},{6,2},{7,3},{8,12},{9,13},{10,... | collective-permute-start | bytes 24584 | tf_op jit(solution)/shard_map/ppermute | solution.py:447
  69.3 5.9 %collective-permute-start.10 = (f32[4,16,128]{2,1,0:T(8,128)S(1)}, f32[4,16,128]{2,1,0:T(8,128)S(1)}, u32[]{:S(2)}, u32[]{:S(2)}) collective-permute-start(f32[4,16,128]{2,1,0:T(8,128)S(1)} %get-tuple-element.41), channel_id=1, source_target_pairs={{0,16},{8,24},{16,0},{24,8},{1,17},{9,25},{17,1},{25,9},{2,18},{10... | collective-permute-start | bytes 98312 | tf_op jit(solution)/shard_map/ppermute | solution.py:458
  70.9 4.4 %collective-permute-start.11 = (f32[4,16,128]{2,1,0:T(8,128)S(1)}, f32[4,16,128]{2,1,0:T(8,128)S(1)}, u32[]{:S(2)}, u32[]{:S(2)}) collective-permute-start(f32[4,16,128]{2,1,0:T(8,128)S(1)} %get-tuple-element.42), channel_id=1, source_target_pairs={{0,24},{8,16},{16,8},{24,0},{1,25},{9,17},{17,9},{25,1},{2,26},{10... | collective-permute-start | bytes 98312 | tf_op jit(solution)/shard_map/ppermute | solution.py:458
  72.0 3.3 %collective-permute-start.9 = (f32[4,16,128]{2,1,0:T(8,128)S(1)}, f32[4,16,128]{2,1,0:T(8,128)S(1)}, u32[]{:S(2)}, u32[]{:S(2)}) collective-permute-start(f32[4,16,128]{2,1,0:T(8,128)S(1)} %get-tuple-element.40), channel_id=1, source_target_pairs={{0,8},{8,0},{16,24},{24,16},{1,9},{9,1},{17,25},{25,17},{2,10},{10... | collective-permute-start | bytes 98312 | tf_op jit(solution)/shard_map/ppermute | solution.py:458

commit v4 on v3

--- a/solution.py
+++ b/solution.py
@@ -10,7 +10,7 @@
 
 
 SUB = 8
-TURNS = 800
+TURNS = 950
 HIGH = lax.Precision.HIGHEST
 VMEM_SPEC = pl.BlockSpec(memory_space=pltpu.VMEM)
 SMEM_SPEC = pl.BlockSpec(memory_space=pltpu.SMEM)
@@ -18,8 +18,8 @@
 HBM_SPEC = pl.BlockSpec(memory_space=pltpu.HBM)
 
 
-def modulation(window_start, section):
-    phase_step = (window_start + 2 - section) % 64
+def modulation(window_start, section, shape):
+    phase_step = jnp.full(shape, (window_start + 2 - section) & 63, jnp.int32)
     return 1.0 + 0.5 * jnp.sin(2.0 * math.pi * phase_step.astype(jnp.float32) / 64.0)
 
 
@@ -143,9 +143,11 @@
     return (1 - 2 * place[0]).astype(jnp.float32)
 
 
-def inner_kernel(count, layers, place, half, dirs, adj, vel, dif, src, inner):
+def inner_kernel(count, layers, place, window_start, dirs, adj, vel, dif, src, inner, half):
     odd = place[0]
     _, _, ny, nz = dirs.shape
+    for k in range(2):
+        half[k] = 0.5 * modulation(window_start[0], k + 1, half.shape[1:])
     for position in range(1, layers - 1):
         near, here, far = (layer_of(odd, position + k, layers) for k in (1, 0, -1))
         stencil(
@@ -368,7 +370,6 @@
     assert spaces & (spaces - 1) == 0 and segs & (segs - 1) == 0 and layers >= 3
     odd = lax.axis_index("space") % 2
     place = jnp.stack([odd, lax.axis_index("seg")]).astype(jnp.int32)
-    half = jnp.stack([0.5 * modulation(segment_start[0], k) for k in (1, 2)])
     pair_one = [(i, i ^ 1) for i in range(spaces)]
     pair_two = [(i, (i + 1) % spaces if i % 2 else (i - 1) % spaces) for i in range(spaces)]
     f32 = functools.partial(jax.ShapeDtypeStruct, dtype=jnp.float32)
@@ -396,27 +397,28 @@
     halo_b = lax.ppermute(near_b, "space", pair_one)
     far = pack(0, 0, fields, edge)
     halo_far = lax.ppermute(far, "space", pair_two)
-    inner = call(
-        functools.partial(inner_kernel, count, layers), f32((layers - 2, fields, ny, nz)),
-        [ss, ss] + [vs] * 5, (place, half, dirs, adj) + flow,
+    inner, half = call(
+        functools.partial(inner_kernel, count, layers),
+        [f32((layers - 2, fields, ny, nz)), f32((2, SUB, nz))],
+        [ss, ss] + [vs] * 5, (place, segment_start, dirs, adj) + flow,
         flops=(layers - 2) * layer_flops, moved=6 * layer_bytes,
     )
     bottom = call(
         functools.partial(bottom_kernel, count, layers), edge,
-        [ss, ss] + [vs] * 6, (place, half, dirs, adj, halo_far) + flow,
+        [ss] + [vs] * 7, (place, half, dirs, adj, halo_far) + flow,
         flops=layer_flops, moved=4 * layer_bytes,
     )
     bottom_far = lax.ppermute(bottom, "space", pair_two)
     top_a = call(
         functools.partial(top_kernel, count, layers, 0, 0), edge_a,
-        [ss, ss] + [vs] * 6 + [anys], (place, half, dirs, adj, halo_a) + flow + (bottom,),
+        [ss] + [vs] * 7 + [anys], (place, half, dirs, adj, halo_a) + flow + (bottom,),
         scratch=[pltpu.SMEM((1,), jnp.int32)],
         flops=layer_flops // 2, moved=2 * layer_bytes,
     )
     near_top_a = lax.ppermute(top_a, "space", pair_one)
     top_b = call(
         functools.partial(top_kernel, count, layers, part_a, TURNS), edge_b,
-        [ss, ss] + [vs] * 6 + [anys], (place, half, dirs, adj, halo_b) + flow + (top_a,),
+        [ss] + [vs] * 7 + [anys], (place, half, dirs, adj, halo_b) + flow + (top_a,),
         scratch=[pltpu.SMEM((1,), jnp.int32)],
         flops=layer_flops // 2, moved=2 * layer_bytes,
     )
@@ -424,22 +426,22 @@
     mid, products, early = call(
         functools.partial(middle_kernel, count, layers),
         [f32((layers - 2, fields, ny, nz)), f32((count * SUB, fields * SUB)), f32((layers, ny, nz))],
-        [ss, ss] + [vs] * 7, (place, half, bottom, inner, top_a, top_b) + flow,
+        [ss] + [vs] * 8, (place, half, bottom, inner, top_a, top_b) + flow,
         flops=4 * (layers - 2) * layer_flops, moved=6 * layer_bytes,
     )
     low, products = call(
         functools.partial(low_kernel, count, layers), [edge, f32((count * SUB, fields * SUB))],
-        [ss, ss] + [vs] * 7, (place, half, bottom, inner, bottom_far) + flow + (products,),
+        [ss] + [vs] * 8, (place, half, bottom, inner, bottom_far) + flow + (products,),
         flops=4 * layer_flops, moved=4 * layer_bytes,
     )
     high_a = call(
         functools.partial(high_a_kernel, count, layers), edge_a,
-        [ss, ss] + [vs] * 6 + [anys], (place, half, top_a, inner, near_top_a) + flow + (low,),
+        [ss] + [vs] * 7 + [anys], (place, half, top_a, inner, near_top_a) + flow + (low,),
         flops=layer_flops // 2, moved=2 * layer_bytes,
     )
     high_b, gram = call(
         functools.partial(high_b_kernel, count, layers), [edge_b, f32((count, 128))],
-        [ss, ss] + [vs] * 8, (place, half, top_b, inner, near_top_b) + flow + (products, high_a),
+        [ss] + [vs] * 9, (place, half, top_b, inner, near_top_b) + flow + (products, high_a),
         flops=2 * layer_flops, moved=2 * layer_bytes,
     )
     reach = 1

time: 76.1 us -> 75.6 us (level)
  waiting for transfers between devices: 38.5 us -> 41.9 us
  Pallas kernels: 19.2 us -> 17.6 us
  starting transfers between devices: 15 us -> 13.7 us
    pallas_call x12, Pallas kernels: 19.2 us -> 17.6 us  [call(): pl.pallas_call(body, out_shape=outs, in_specs=specs, out_specs=out_specs...]
    ppermute x1, waiting for transfers between devices: 1.17 us -> 2.42 us  [window(): near_top_a = lax.ppermute(top_a, 'space', pair_one)]
    ppermute x3, starting transfers between devices: 1.52 us -> 0.68 us  [window(): lax.ppermute(gram, 'space', [(i, i ^ reach) for i in range(spaces)])]
    ppermute x3, waiting for transfers between devices: 10.4 us -> 11.2 us  [window(): lax.ppermute(gram, 'space', [(i, i ^ reach) for i in range(spaces)])]
  transfers between devices with their start and end apart: 12 -> 12, of which waited for: 8 -> 8; matrix products, arithmetic and copies ran while one was open for 0% -> 0% of each run, Pallas kernels for 19% -> 17%
where the time goes in v4:
time: 75.6 us; the launch traced here: 75.4 us
  waiting for transfers between devices  41.9 us (55%)
  Pallas kernels  17.6 us (23%)
  starting transfers between devices  13.7 us (18%)
  between operations  1.48 us (2%)
    pallas_call x12, Pallas kernels, call(): pl.pallas_call(body, out_shape=outs, in_specs=specs, out_specs=out_specs...  17.6 us
    ppermute x1, waiting for transfers between devices, window(): halo_a = lax.ppermute(near_a, 'space', pair_one)  13.5 us
    ppermute x3, waiting for transfers between devices, window(): lax.ppermute(gram, 'space', [(i, i ^ reach) for i in range(spaces)])  11.2 us
    ppermute x1, waiting for transfers between devices, window(): halo_far = lax.ppermute(far, 'space', pair_two)  9.08 us
    ppermute x1, starting transfers between devices, window(): halo_far = lax.ppermute(far, 'space', pair_two)  6.1 us
    ppermute x1, starting transfers between devices, window(): bottom_far = lax.ppermute(bottom, 'space', pair_two)  4.51 us
    ppermute x1, waiting for transfers between devices, window(): halo_b = lax.ppermute(near_b, 'space', pair_one)  4.05 us
    ppermute x1, waiting for transfers between devices, window(): near_top_a = lax.ppermute(top_a, 'space', pair_one)  2.42 us
  transfers between devices with their start and end apart: 12, of which 8 were waited for; matrix products, arithmetic and copies ran while one was open for 0% of the time, Pallas kernels for 17%

profile of v4, /device:TPU:0, one launch (start us, length us, event | category | flops | bytes accessed | tf_op | source)
XLA Modules:
  0.0 75.4 jit_solution(15646949210641965924)
XLA Ops:
  0.7 1.9 %shard_map.103 = f32[17,64,128]{2,1,0:T(8,128)S(1)} custom-call(s32[2]{0:T(128)S(1)} %pad_add_fusion.place, f32[16,4,64,128]{3,2,1,0:T(8,128)} %bitcast.10, f32[4,64,128]{2,1,0:T(8,128)} %bitcast.40), custom_call_target="tpu_custom_call" | custom-call | bytes 1114112 | tf_op jit(solution)/shard_map/pallas_call | solution.py:27
  2.6 6.1 %collective-permute-start.2 = (f32[17,64,128]{2,1,0:T(8,128)S(1)}, f32[17,64,128]{2,1,0:T(8,128)S(1)}, u32[]{:S(2)}, u32[]{:S(2)}) collective-permute-start(f32[17,64,128]{2,1,0:T(8,128)S(1)} %shard_map.103), channel_id=1, source_target_pairs={{0,7},{1,2},{2,1},{3,4},{4,3},{5,6},{6,5},{7,0},{8,15},{9,10},{10,... | collective-permute-start | bytes 1671176 | tf_op jit(solution)/shard_map/ppermute | solution.py:399
  8.7 1.6 %shard_map.102 = (f32[10,64,128]{2,1,0:T(8,128)S(1)}, f32[7,64,128]{2,1,0:T(8,128)S(1)}) custom-call(s32[2]{0:T(128)S(1)} %pad_add_fusion.place, f32[16,4,64,128]{3,2,1,0:T(8,128)} %bitcast.11, f32[4,64,128]{2,1,0:T(8,128)} %bitcast.41), custom_call_target="tpu_custom_call" | custom-call | bytes 1114112 | tf_op jit(solution)/shard_map/pallas_call | solution.py:27
  11.1 1.3 %shard_map.101 = (f32[2,17,64,128]{3,2,1,0:T(8,128)S(1)}, f32[2,8,128]{2,1,0:T(8,128)S(1)}) custom-call(s32[2]{0:T(128)S(1)} %pad_add_fusion.place, s32[1]{0:T(128)S(6)} %copy.11.window_start, f32[16,4,64,128]{3,2,1,0:T(8,128)S(1)} %bitcast.12, f32[4,64,128]{2,1,0:T(8,128)S(1)} %bitcast.42, f32[3,4,64,128]{3,2,1,0:T(8,128)S(1)} %bitcast.16, ...), custom_call_target="tpu_custom_call" | custom-call | flops 3620864 | bytes 3342336 | tf_op jit(solution)/shard_map/pallas_call | solution.py:27
  12.4 9.1 %collective-permute-done.2.halo = f32[17,64,128]{2,1,0:T(8,128)S(1)} collective-permute-done((f32[17,64,128]{2,1,0:T(8,128)S(1)}, f32[17,64,128]{2,1,0:T(8,128)S(1)}, u32[]{:S(2)}, u32[]{:S(2)}) %collective-permute-start.2) | collective-permute-done | bytes 557088 | tf_op jit(solution)/shard_map/ppermute | solution.py:399
  21.5 0.9 %shard_map.104.order.bottom = f32[17,64,128]{2,1,0:T(8,128)S(1)} custom-call(s32[2]{0:T(128)S(1)} %pad_add_fusion.place, f32[2,8,128]{2,1,0:T(8,128)S(1)} %get-tuple-element.26.half, f32[16,4,64,128]{3,2,1,0:T(8,128)S(1)} %bitcast.13, f32[4,64,128]{2,1,0:T(8,128)S(1)} %bitcast.43, f32[17,64,128]{2,1,0:T(8,128)S(1)} %collective-permute-done.2.halo, ...), custom_call_target="tpu_custom_call" | custom-call | flops 1810432 | bytes 2228224 | tf_op jit(solution)/shard_map/pallas_call | solution.py:27
  22.4 4.5 %collective-permute-start.4 = (f32[17,64,128]{2,1,0:T(8,128)S(1)}, f32[17,64,128]{2,1,0:T(8,128)S(1)}, u32[]{:S(2)}, u32[]{:S(2)}) collective-permute-start(f32[17,64,128]{2,1,0:T(8,128)S(1)} %shard_map.104.order.bottom), channel_id=1, source_target_pairs={{0,7},{1,2},{2,1},{3,4},{4,3},{5,6},{6,5},{7,0},{8,15},{9,10},{10,... | collective-permute-start | bytes 1671176 | tf_op jit(solution)/shard_map/ppermute | solution.py:411
  26.9 13.5 %collective-permute-done.1.halo = f32[10,64,128]{2,1,0:T(8,128)S(1)} collective-permute-done((f32[10,64,128]{2,1,0:T(8,128)S(1)}, f32[10,64,128]{2,1,0:T(8,128)S(1)}, u32[]{:S(2)}, u32[]{:S(2)}) %collective-permute-start.1) | collective-permute-done | bytes 327712 | tf_op jit(solution)/shard_map/ppermute | solution.py:396
  40.4 0.8 %shard_map.105.order.top_a.top = f32[10,64,128]{2,1,0:T(8,128)S(1)} custom-call(s32[2]{0:T(128)S(1)} %pad_add_fusion.place, f32[2,8,128]{2,1,0:T(8,128)S(1)} %get-tuple-element.26.half, f32[16,4,64,128]{3,2,1,0:T(8,128)S(1)} %bitcast.14, f32[4,64,128]{2,1,0:T(8,128)S(1)} %bitcast.44, f32[10,64,128]{2,1,0:T(8,128)S(1)} %collective-permute-done.1.halo, ...), custom_call_target="tpu_custom_call" | custom-call | flops 905216 | bytes 1114112 | tf_op jit(solution)/shard_map/pallas_call | solution.py:27
  41.3 4.0 %collective-permute-done.halo = f32[7,64,128]{2,1,0:T(8,128)S(1)} collective-permute-done((f32[7,64,128]{2,1,0:T(8,128)S(1)}, f32[7,64,128]{2,1,0:T(8,128)S(1)}, u32[]{:S(2)}, u32[]{:S(2)}) %collective-permute-start) | collective-permute-done | bytes 229408 | tf_op jit(solution)/shard_map/ppermute | solution.py:397
  45.3 0.7 shard_map.106.top_b.top
  46.1 2.2 %shard_map.107 = (f32[2,17,64,128]{3,2,1,0:T(8,128)S(1)}, f32[128,136]{1,0:T(8,128)S(1)}, f32[4,64,128]{2,1,0:T(8,128)S(1)}) custom-call(s32[2]{0:T(128)S(1)} %pad_add_fusion.place, f32[2,8,128]{2,1,0:T(8,128)S(1)} %get-tuple-element.26.half, f32[17,64,128]{2,1,0:T(8,128)S(1)} %shard_map.104.order.bottom, f32[2,17,64,128]{3,2,1,0:T(8,128)S(1)} %get-tuple-element.29.inner, ...), custom_call_target="tpu_custom_call" | custom-call | flops 14483456 | bytes 3342336 | tf_op jit(solution)/shard_map/pallas_call | solution.py:27
  48.4 1.5 %shard_map.108 = (f32[17,64,128]{2,1,0:T(8,128)S(1)}, f32[128,136]{1,0:T(8,128)S(1)}) custom-call(s32[2]{0:T(128)S(1)} %pad_add_fusion.place, f32[2,8,128]{2,1,0:T(8,128)S(1)} %get-tuple-element.26.half, f32[17,64,128]{2,1,0:T(8,128)S(1)} %shard_map.104.order.bottom, f32[2,17,64,128]{3,2,1,0:T(8,128)S(1)} %get-tuple-element.29.inner, ...), custom_call_target="tpu_custom_call" | custom-call | flops 7241728 | bytes 2228224 | tf_op jit(solution)/shard_map/pallas_call | solution.py:27
  49.8 2.4 %collective-permute-done.5.halo = f32[10,64,128]{2,1,0:T(8,128)S(1)} collective-permute-done((f32[10,64,128]{2,1,0:T(8,128)S(1)}, f32[10,64,128]{2,1,0:T(8,128)S(1)}, u32[]{:S(2)}, u32[]{:S(2)}) %collective-permute-start.5) | collective-permute-done | bytes 327712 | tf_op jit(solution)/shard_map/ppermute | solution.py:418
  52.2 0.8 %shard_map.109.out_a.high_a = f32[10,64,128]{2,1,0:T(8,128)S(1)} custom-call(s32[2]{0:T(128)S(1)} %pad_add_fusion.place, f32[2,8,128]{2,1,0:T(8,128)S(1)} %get-tuple-element.26.half, f32[10,64,128]{2,1,0:T(8,128)S(1)} %shard_map.105.order.top_a.top, f32[2,17,64,128]{3,2,1,0:T(8,128)S(1)} %get-tuple-element.29.inner, ...), custom_call_target="tpu_custom_call" | custom-call | flops 905216 | bytes 1114112 | tf_op jit(solution)/shard_map/pallas_call | solution.py:27
  53.0 1.7 %collective-permute-done.3.halo = f32[7,64,128]{2,1,0:T(8,128)S(1)} collective-permute-done((f32[7,64,128]{2,1,0:T(8,128)S(1)}, f32[7,64,128]{2,1,0:T(8,128)S(1)}, u32[]{:S(2)}, u32[]{:S(2)}) %collective-permute-start.3) | collective-permute-done | bytes 229408 | tf_op jit(solution)/shard_map/ppermute | solution.py:425
  54.7 1.5 %shard_map.110 = (f32[7,64,128]{2,1,0:T(8,128)S(1)}, f32[16,128]{1,0:T(8,128)S(1)}) custom-call(s32[2]{0:T(128)S(1)} %pad_add_fusion.place, f32[2,8,128]{2,1,0:T(8,128)S(1)} %get-tuple-element.26.half, f32[7,64,128]{2,1,0:T(8,128)S(1)} %shard_map.106.top_b.top, f32[2,17,64,128]{3,2,1,0:T(8,128)S(1)} %get-tuple-element.29.inner, ...), custom_call_target="tpu_custom_call" | custom-call | flops 3620864 | bytes 1114112 | tf_op jit(solution)/shard_map/pallas_call | solution.py:27
  56.2 3.7 %collective-permute-done.6 = f32[16,128]{1,0:T(8,128)S(1)} collective-permute-done((f32[16,128]{1,0:T(8,128)S(1)}, f32[16,128]{1,0:T(8,128)S(1)}, u32[]{:S(2)}, u32[]{:S(2)}) %collective-permute-start.6) | collective-permute-done | bytes 8224 | tf_op jit(solution)/shard_map/ppermute | solution.py:449
  59.9 3.6 %collective-permute-done.7 = f32[16,128]{1,0:T(8,128)S(1)} collective-permute-done((f32[16,128]{1,0:T(8,128)S(1)}, f32[16,128]{1,0:T(8,128)S(1)}, u32[]{:S(2)}, u32[]{:S(2)}) %collective-permute-start.7) | collective-permute-done | bytes 8224 | tf_op jit(solution)/shard_map/ppermute | solution.py:449
  63.5 0.7 collective-permute-start.8
  64.2 3.9 %collective-permute-done.8 = f32[16,128]{1,0:T(8,128)S(1)} collective-permute-done((f32[16,128]{1,0:T(8,128)S(1)}, f32[16,128]{1,0:T(8,128)S(1)}, u32[]{:S(2)}, u32[]{:S(2)}) %collective-permute-start.8) | collective-permute-done | bytes 8224 | tf_op jit(solution)/shard_map/ppermute | solution.py:449
  68.1 1.2 %shard_map.111 = (f32[16,128]{1,0:T(8,128)S(1)}, f32[4,64,128]{2,1,0:T(8,128)S(1)}, f32[4,16,128]{2,1,0:T(8,128)S(1)}, f32[4,16,128]{2,1,0:T(8,128)S(1)}, f32[4,...) custom-call(s32[2]{0:T(128)S(1)} %pad_add_fusion.place, f32[16,128]{1,0:T(8,128)S(1)} %add.25.gram, ...), custom_call_target="tpu_custom_call" | custom-call | flops 7241728 | bytes 2228224 | tf_op jit(solution)/shard_map/pallas_call | solution.py:27
  69.3 1.6 %collective-permute-start.10 = (f32[4,16,128]{2,1,0:T(8,128)S(1)}, f32[4,16,128]{2,1,0:T(8,128)S(1)}, u32[]{:S(2)}, u32[]{:S(2)}) collective-permute-start(f32[4,16,128]{2,1,0:T(8,128)S(1)} %get-tuple-element.45), channel_id=1, source_target_pairs={{0,16},{8,24},{16,0},{24,8},{1,17},{9,25},{17,1},{25,9},{2,18},{10... | collective-permute-start | bytes 98312 | tf_op jit(solution)/shard_map/ppermute | solution.py:460
  71.5 3.2 %shard_map.112 = (f32[16,4,64,128]{3,2,1,0:T(8,128)}, f32[16,16]{1,0:T(8,128)}, f32[1,16]{1,0:T(1,128)}, f32[4,64,128]{2,1,0:T(8,128)}) custom-call(s32[2]{0:T(128)S(1)} %pad_add_fusion.place, f32[16,128]{1,0:T(8,128)S(1)} %get-tuple-element.37.weights.solved, f32[16,128]{1,0:T(8,128)S(1)} %get-tuple-element.37.weights.solved, ...), custom_call_target="tpu_custom_call" | custom-call | flops 14483456 | bytes 4456448 | tf_op jit(solution)/shard_map/pallas_call | solution.py:27
  (27 shorter events, 1.6 us)
Async XLA Ops:
  0.7 10.3 %copy-start = (f32[1,16,4,64,128]{4,3,2,1,0:T(8,128)S(1)}, f32[1,16,4,64,128]{4,3,2,1,0:T(8,128)}, u32[]{:S(2)}) copy-start(f32[1,16,4,64,128]{4,3,2,1,0:T(8,128)} %param.6) | copy-start | bytes 6291460
  0.7 10.4 %copy-start.1 = (f32[1,3,4,64,128]{4,3,2,1,0:T(8,128)S(1)}, f32[1,3,4,64,128]{4,3,2,1,0:T(8,128)}, u32[]{:S(2)}) copy-start(f32[1,3,4,64,128]{4,3,2,1,0:T(8,128)} %param.8) | copy-start | bytes 1179652
  0.7 10.4 %copy-start.2 = (f32[1,4,64,128]{3,2,1,0:T(8,128)S(1)}, f32[1,4,64,128]{3,2,1,0:T(8,128)}, u32[]{:S(2)}) copy-start(f32[1,4,64,128]{3,2,1,0:T(8,128)} %param.9) | copy-start | bytes 393220
  0.7 10.4 %copy-start.3 = (f32[1,4,64,128]{3,2,1,0:T(8,128)S(1)}, f32[1,4,64,128]{3,2,1,0:T(8,128)}, u32[]{:S(2)}) copy-start(f32[1,4,64,128]{3,2,1,0:T(8,128)} %param.10) | copy-start | bytes 393220
  0.7 10.4 %copy-start.4 = (f32[1,4,64,128]{3,2,1,0:T(8,128)S(1)}, f32[1,4,64,128]{3,2,1,0:T(8,128)}, u32[]{:S(2)}) copy-start(f32[1,4,64,128]{3,2,1,0:T(8,128)} %param.7) | copy-start | bytes 393220
  2.6 18.8 %collective-permute-start.2 = (f32[17,64,128]{2,1,0:T(8,128)S(1)}, f32[17,64,128]{2,1,0:T(8,128)S(1)}, u32[]{:S(2)}, u32[]{:S(2)}) collective-permute-start(f32[17,64,128]{2,1,0:T(8,128)S(1)} %shard_map.103), channel_id=1, source_target_pairs={{0,7},{1,2},{2,1},{3,4},{4,3},{5,6},{6,5},{7,0},{8,15},{9,10},{10,... | collective-permute-start | bytes 1671176 | tf_op jit(solution)/shard_map/ppermute | solution.py:399
  10.3 30.1 %collective-permute-start.1 = (f32[10,64,128]{2,1,0:T(8,128)S(1)}, f32[10,64,128]{2,1,0:T(8,128)S(1)}, u32[]{:S(2)}, u32[]{:S(2)}) collective-permute-start(f32[10,64,128]{2,1,0:T(8,128)S(1)} %get-tuple-element.28), channel_id=1, source_target_pairs={{0,1},{1,0},{2,3},{3,2},{4,5},{5,4},{6,7},{7,6},{8,9},{9,8},{10,11... | collective-permute-start | bytes 983048 | tf_op jit(solution)/shard_map/ppermute | solution.py:396
  22.4 26.0 %collective-permute-start.4 = (f32[17,64,128]{2,1,0:T(8,128)S(1)}, f32[17,64,128]{2,1,0:T(8,128)S(1)}, u32[]{:S(2)}, u32[]{:S(2)}) collective-permute-start(f32[17,64,128]{2,1,0:T(8,128)S(1)} %shard_map.104.order.bottom), channel_id=1, source_target_pairs={{0,7},{1,2},{2,1},{3,4},{4,3},{5,6},{6,5},{7,0},{8,15},{9,10},{10,... | collective-permute-start | bytes 1671176 | tf_op jit(solution)/shard_map/ppermute | solution.py:411
  26.9 18.4 %collective-permute-start = (f32[7,64,128]{2,1,0:T(8,128)S(1)}, f32[7,64,128]{2,1,0:T(8,128)S(1)}, u32[]{:S(2)}, u32[]{:S(2)}) collective-permute-start(f32[7,64,128]{2,1,0:T(8,128)S(1)} %get-tuple-element.27), channel_id=1, source_target_pairs={{0,1},{1,0},{2,3},{3,2},{4,5},{5,4},{6,7},{7,6},{8,9},{9,8},{10,11... | collective-permute-start | bytes 688136 | tf_op jit(solution)/shard_map/ppermute | solution.py:397
  41.2 11.1 %collective-permute-start.5 = (f32[10,64,128]{2,1,0:T(8,128)S(1)}, f32[10,64,128]{2,1,0:T(8,128)S(1)}, u32[]{:S(2)}, u32[]{:S(2)}) collective-permute-start(f32[10,64,128]{2,1,0:T(8,128)S(1)} %shard_map.105.order.top_a.top), channel_id=1, source_target_pairs={{0,1},{1,0},{2,3},{3,2},{4,5},{5,4},{6,7},{7,6},{8,9},{9,8},{10,11... | collective-permute-start | bytes 983048 | tf_op jit(solution)/shard_map/ppermute | solution.py:418
  46.1 8.6 %collective-permute-start.3 = (f32[7,64,128]{2,1,0:T(8,128)S(1)}, f32[7,64,128]{2,1,0:T(8,128)S(1)}, u32[]{:S(2)}, u32[]{:S(2)}) collective-permute-start(f32[7,64,128]{2,1,0:T(8,128)S(1)} %shard_map.106.top_b.top), channel_id=1, source_target_pairs={{0,1},{1,0},{2,3},{3,2},{4,5},{5,4},{6,7},{7,6},{8,9},{9,8},{10,11... | collective-permute-start | bytes 688136 | tf_op jit(solution)/shard_map/ppermute | solution.py:425
  56.2 3.7 %collective-permute-start.6 = (f32[16,128]{1,0:T(8,128)S(1)}, f32[16,128]{1,0:T(8,128)S(1)}, u32[]{:S(2)}, u32[]{:S(2)}) collective-permute-start(f32[16,128]{1,0:T(8,128)S(1)} %get-tuple-element.33), channel_id=1, source_target_pairs={{0,1},{1,0},{2,3},{3,2},{4,5},{5,4},{6,7},{7,6},{8,9},{9,8},{10,11... | collective-permute-start | bytes 24584 | tf_op jit(solution)/shard_map/ppermute | solution.py:449
  59.9 3.7 %collective-permute-start.7 = (f32[16,128]{1,0:T(8,128)S(1)}, f32[16,128]{1,0:T(8,128)S(1)}, u32[]{:S(2)}, u32[]{:S(2)}) collective-permute-start(f32[16,128]{1,0:T(8,128)S(1)} %add.23), channel_id=1, source_target_pairs={{0,2},{1,3},{2,0},{3,1},{4,6},{5,7},{6,4},{7,5},{8,10},{9,11},{10,... | collective-permute-start | bytes 24584 | tf_op jit(solution)/shard_map/ppermute | solution.py:449
  63.5 4.5 %collective-permute-start.8 = (f32[16,128]{1,0:T(8,128)S(1)}, f32[16,128]{1,0:T(8,128)S(1)}, u32[]{:S(2)}, u32[]{:S(2)}) collective-permute-start(f32[16,128]{1,0:T(8,128)S(1)} %add.24), channel_id=1, source_target_pairs={{0,4},{1,5},{2,6},{3,7},{4,0},{5,1},{6,2},{7,3},{8,12},{9,13},{10,... | collective-permute-start | bytes 24584 | tf_op jit(solution)/shard_map/ppermute | solution.py:449
  69.3 5.5 %collective-permute-start.10 = (f32[4,16,128]{2,1,0:T(8,128)S(1)}, f32[4,16,128]{2,1,0:T(8,128)S(1)}, u32[]{:S(2)}, u32[]{:S(2)}) collective-permute-start(f32[4,16,128]{2,1,0:T(8,128)S(1)} %get-tuple-element.45), channel_id=1, source_target_pairs={{0,16},{8,24},{16,0},{24,8},{1,17},{9,25},{17,1},{25,9},{2,18},{10... | collective-permute-start | bytes 98312 | tf_op jit(solution)/shard_map/ppermute | solution.py:460
  70.8 3.9 %collective-permute-start.11 = (f32[4,16,128]{2,1,0:T(8,128)S(1)}, f32[4,16,128]{2,1,0:T(8,128)S(1)}, u32[]{:S(2)}, u32[]{:S(2)}) collective-permute-start(f32[4,16,128]{2,1,0:T(8,128)S(1)} %get-tuple-element.46), channel_id=1, source_target_pairs={{0,24},{8,16},{16,8},{24,0},{1,25},{9,17},{17,9},{25,1},{2,26},{10... | collective-permute-start | bytes 98312 | tf_op jit(solution)/shard_map/ppermute | solution.py:460
  71.5 3.3 %collective-permute-start.9 = (f32[4,16,128]{2,1,0:T(8,128)S(1)}, f32[4,16,128]{2,1,0:T(8,128)S(1)}, u32[]{:S(2)}, u32[]{:S(2)}) collective-permute-start(f32[4,16,128]{2,1,0:T(8,128)S(1)} %get-tuple-element.44), channel_id=1, source_target_pairs={{0,8},{8,0},{16,24},{24,16},{1,9},{9,1},{17,25},{25,17},{2,10},{10... | collective-permute-start | bytes 98312 | tf_op jit(solution)/shard_map/ppermute | solution.py:460

commit v5 on v4

--- a/solution.py
+++ b/solution.py
@@ -10,7 +10,7 @@
 
 
 SUB = 8
-TURNS = 950
+TURNS = 900
 HIGH = lax.Precision.HIGHEST
 VMEM_SPEC = pl.BlockSpec(memory_space=pltpu.VMEM)
 SMEM_SPEC = pl.BlockSpec(memory_space=pltpu.SMEM)
@@ -143,8 +143,11 @@
     return (1 - 2 * place[0]).astype(jnp.float32)
 
 
-def inner_kernel(count, layers, place, window_start, dirs, adj, vel, dif, src, inner, half):
-    odd = place[0]
+def inner_kernel(count, layers, place, window_start, dirs_far, adj, vel, dif, src, inner, half, dirs, sem):
+    odd = place[0]
+    fetch = pltpu.make_async_copy(dirs_far, dirs, sem)
+    fetch.start()
+    fetch.wait()
     _, _, ny, nz = dirs.shape
     for k in range(2):
         half[k] = 0.5 * modulation(window_start[0], k + 1, half.shape[1:])
@@ -397,10 +400,11 @@
     halo_b = lax.ppermute(near_b, "space", pair_one)
     far = pack(0, 0, fields, edge)
     halo_far = lax.ppermute(far, "space", pair_two)
-    inner, half = call(
+    inner, half, dirs = call(
         functools.partial(inner_kernel, count, layers),
-        [f32((layers - 2, fields, ny, nz)), f32((2, SUB, nz))],
-        [ss, ss] + [vs] * 5, (place, segment_start, dirs, adj) + flow,
+        [f32((layers - 2, fields, ny, nz)), f32((2, SUB, nz)), f32((count, layers, ny, nz))],
+        [ss, ss, hs] + [vs] * 4, (place, segment_start, dirs_hbm, adj) + flow,
+        scratch=[pltpu.SemaphoreType.DMA],
         flops=(layers - 2) * layer_flops, moved=6 * layer_bytes,
     )
     bottom = call(

time: 75.6 us -> 75.3 us (level)
  waiting for transfers between devices: 41.9 us -> 40.3 us
  Pallas kernels: 17.6 us -> 18.9 us
    ppermute x1, waiting for transfers between devices: 9.08 us -> 7.48 us  [window(): halo_far = lax.ppermute(far, 'space', pair_two)]
    pallas_call x12, Pallas kernels: 17.6 us -> 18.9 us  [call(): pl.pallas_call(body, out_shape=outs, in_specs=specs, out_specs=out_specs...]
  transfers between devices with their start and end apart: 12 -> 12, of which waited for: 8 -> 8; matrix products, arithmetic and copies ran while one was open for 0% -> 0% of each run, Pallas kernels for 17% -> 19%
where the time goes in v5:
time: 75.3 us; the launch traced here: 75.1 us
  waiting for transfers between devices  40.3 us (54%)
  Pallas kernels  18.9 us (25%)
  starting transfers between devices  13.7 us (18%)
  between operations  1.47 us (2%)
    pallas_call x12, Pallas kernels, call(): pl.pallas_call(body, out_shape=outs, in_specs=specs, out_specs=out_specs...  18.9 us
    ppermute x1, waiting for transfers between devices, window(): halo_a = lax.ppermute(near_a, 'space', pair_one)  13.5 us
    ppermute x3, waiting for transfers between devices, window(): lax.ppermute(gram, 'space', [(i, i ^ reach) for i in range(spaces)])  11.2 us
    ppermute x1, waiting for transfers between devices, window(): halo_far = lax.ppermute(far, 'space', pair_two)  7.48 us
    ppermute x1, starting transfers between devices, window(): halo_far = lax.ppermute(far, 'space', pair_two)  6.1 us
    ppermute x1, starting transfers between devices, window(): bottom_far = lax.ppermute(bottom, 'space', pair_two)  4.51 us
    ppermute x1, waiting for transfers between devices, window(): halo_b = lax.ppermute(near_b, 'space', pair_one)  4.05 us
    ppermute x1, waiting for transfers between devices, window(): near_top_a = lax.ppermute(top_a, 'space', pair_one)  2.44 us
  transfers between devices with their start and end apart: 12, of which 8 were waited for; matrix products, arithmetic and copies ran while one was open for 0% of the time, Pallas kernels for 19%

profile of v5, /device:TPU:0, one launch (start us, length us, event | category | flops | bytes accessed | tf_op | source)
XLA Modules:
  0.0 75.1 jit_solution(11215367134686390414)
XLA Ops:
  0.7 1.6 %shard_map.103 = f32[17,64,128]{2,1,0:T(8,128)S(1)} custom-call(s32[2]{0:T(128)S(1)} %pad_add_fusion.place, f32[16,4,64,128]{3,2,1,0:T(8,128)} %bitcast.40, f32[4,64,128]{2,1,0:T(8,128)} %bitcast.34), custom_call_target="tpu_custom_call" | custom-call | bytes 1114112 | tf_op jit(solution)/shard_map/pallas_call | solution.py:27
  2.3 6.1 %collective-permute-start.2 = (f32[17,64,128]{2,1,0:T(8,128)S(1)}, f32[17,64,128]{2,1,0:T(8,128)S(1)}, u32[]{:S(2)}, u32[]{:S(2)}) collective-permute-start(f32[17,64,128]{2,1,0:T(8,128)S(1)} %shard_map.103), channel_id=1, source_target_pairs={{0,7},{1,2},{2,1},{3,4},{4,3},{5,6},{6,5},{7,0},{8,15},{9,10},{10,... | collective-permute-start | bytes 1671176 | tf_op jit(solution)/shard_map/ppermute | solution.py:402
  8.4 1.6 %shard_map.102 = (f32[10,64,128]{2,1,0:T(8,128)S(1)}, f32[7,64,128]{2,1,0:T(8,128)S(1)}) custom-call(s32[2]{0:T(128)S(1)} %pad_add_fusion.place, f32[16,4,64,128]{3,2,1,0:T(8,128)} %bitcast.41, f32[4,64,128]{2,1,0:T(8,128)} %bitcast.35), custom_call_target="tpu_custom_call" | custom-call | bytes 1114112 | tf_op jit(solution)/shard_map/pallas_call | solution.py:27
  10.8 2.9 %shard_map.101 = (f32[2,17,64,128]{3,2,1,0:T(8,128)S(1)}, f32[2,8,128]{2,1,0:T(8,128)S(1)}, f32[16,4,64,128]{3,2,1,0:T(8,128)S(1)}) custom-call(s32[2]{0:T(128)S(1)} %pad_add_fusion.place, s32[1]{0:T(128)S(6)} %copy.11.window_start, f32[16,4,64,128]{3,2,1,0:T(8,128)} %bitcast.42, f32[4,64,128]{2,1,0:T(8,128)S(1)} %bitcast.36, ...), custom_call_target="tpu_custom_call" | custom-call | flops 3620864 | bytes 3342336 | tf_op jit(solution)/shard_map/pallas_call | solution.py:27
  13.7 7.5 %collective-permute-done.2.halo = f32[17,64,128]{2,1,0:T(8,128)S(1)} collective-permute-done((f32[17,64,128]{2,1,0:T(8,128)S(1)}, f32[17,64,128]{2,1,0:T(8,128)S(1)}, u32[]{:S(2)}, u32[]{:S(2)}) %collective-permute-start.2) | collective-permute-done | bytes 557088 | tf_op jit(solution)/shard_map/ppermute | solution.py:402
  21.2 0.9 %shard_map.104.order.bottom = f32[17,64,128]{2,1,0:T(8,128)S(1)} custom-call(s32[2]{0:T(128)S(1)} %pad_add_fusion.place, f32[2,8,128]{2,1,0:T(8,128)S(1)} %get-tuple-element.27.half, f32[16,4,64,128]{3,2,1,0:T(8,128)S(1)} %get-tuple-element.28.dirs, f32[4,64,128]{2,1,0:T(8,128)S(1)} %bitcast.37, f32[17,64,128]{2,1,0:T(8,128)S(1)} %collective-permute-done.2.halo, ...), custom_call_target="tpu_custom_call" | custom-call | flops 1810432 | bytes 2228224 | tf_op jit(solution)/shard_map/pallas_call | solution.py:27
  22.1 4.5 %collective-permute-start.4 = (f32[17,64,128]{2,1,0:T(8,128)S(1)}, f32[17,64,128]{2,1,0:T(8,128)S(1)}, u32[]{:S(2)}, u32[]{:S(2)}) collective-permute-start(f32[17,64,128]{2,1,0:T(8,128)S(1)} %shard_map.104.order.bottom), channel_id=1, source_target_pairs={{0,7},{1,2},{2,1},{3,4},{4,3},{5,6},{6,5},{7,0},{8,15},{9,10},{10,... | collective-permute-start | bytes 1671176 | tf_op jit(solution)/shard_map/ppermute | solution.py:415
  26.6 13.5 %collective-permute-done.1.halo = f32[10,64,128]{2,1,0:T(8,128)S(1)} collective-permute-done((f32[10,64,128]{2,1,0:T(8,128)S(1)}, f32[10,64,128]{2,1,0:T(8,128)S(1)}, u32[]{:S(2)}, u32[]{:S(2)}) %collective-permute-start.1) | collective-permute-done | bytes 327712 | tf_op jit(solution)/shard_map/ppermute | solution.py:399
  40.1 0.8 %shard_map.105.order.top_a.top = f32[10,64,128]{2,1,0:T(8,128)S(1)} custom-call(s32[2]{0:T(128)S(1)} %pad_add_fusion.place, f32[2,8,128]{2,1,0:T(8,128)S(1)} %get-tuple-element.27.half, f32[16,4,64,128]{3,2,1,0:T(8,128)S(1)} %get-tuple-element.28.dirs, f32[4,64,128]{2,1,0:T(8,128)S(1)} %bitcast.38, f32[10,64,128]{2,1,0:T(8,128)S(1)} %collective-permute-done.1.halo, ...), custom_call_target="tpu_custom_call" | custom-call | flops 905216 | bytes 1114112 | tf_op jit(solution)/shard_map/pallas_call | solution.py:27
  41.0 4.0 %collective-permute-done.halo = f32[7,64,128]{2,1,0:T(8,128)S(1)} collective-permute-done((f32[7,64,128]{2,1,0:T(8,128)S(1)}, f32[7,64,128]{2,1,0:T(8,128)S(1)}, u32[]{:S(2)}, u32[]{:S(2)}) %collective-permute-start) | collective-permute-done | bytes 229408 | tf_op jit(solution)/shard_map/ppermute | solution.py:400
  45.0 0.7 shard_map.106.top_b.top
  45.9 2.2 %shard_map.107 = (f32[2,17,64,128]{3,2,1,0:T(8,128)S(1)}, f32[128,136]{1,0:T(8,128)S(1)}, f32[4,64,128]{2,1,0:T(8,128)S(1)}) custom-call(s32[2]{0:T(128)S(1)} %pad_add_fusion.place, f32[2,8,128]{2,1,0:T(8,128)S(1)} %get-tuple-element.27.half, f32[17,64,128]{2,1,0:T(8,128)S(1)} %shard_map.104.order.bottom, f32[2,17,64,128]{3,2,1,0:T(8,128)S(1)} %get-tuple-element.31.inner, ...), custom_call_target="tpu_custom_call" | custom-call | flops 14483456 | bytes 3342336 | tf_op jit(solution)/shard_map/pallas_call | solution.py:27
  48.1 1.4 %shard_map.108 = (f32[17,64,128]{2,1,0:T(8,128)S(1)}, f32[128,136]{1,0:T(8,128)S(1)}) custom-call(s32[2]{0:T(128)S(1)} %pad_add_fusion.place, f32[2,8,128]{2,1,0:T(8,128)S(1)} %get-tuple-element.27.half, f32[17,64,128]{2,1,0:T(8,128)S(1)} %shard_map.104.order.bottom, f32[2,17,64,128]{3,2,1,0:T(8,128)S(1)} %get-tuple-element.31.inner, ...), custom_call_target="tpu_custom_call" | custom-call | flops 7241728 | bytes 2228224 | tf_op jit(solution)/shard_map/pallas_call | solution.py:27
  49.5 2.4 %collective-permute-done.5.halo = f32[10,64,128]{2,1,0:T(8,128)S(1)} collective-permute-done((f32[10,64,128]{2,1,0:T(8,128)S(1)}, f32[10,64,128]{2,1,0:T(8,128)S(1)}, u32[]{:S(2)}, u32[]{:S(2)}) %collective-permute-start.5) | collective-permute-done | bytes 327712 | tf_op jit(solution)/shard_map/ppermute | solution.py:422
  52.0 0.8 %shard_map.109.out_a.high_a = f32[10,64,128]{2,1,0:T(8,128)S(1)} custom-call(s32[2]{0:T(128)S(1)} %pad_add_fusion.place, f32[2,8,128]{2,1,0:T(8,128)S(1)} %get-tuple-element.27.half, f32[10,64,128]{2,1,0:T(8,128)S(1)} %shard_map.105.order.top_a.top, f32[2,17,64,128]{3,2,1,0:T(8,128)S(1)} %get-tuple-element.31.inner, ...), custom_call_target="tpu_custom_call" | custom-call | flops 905216 | bytes 1114112 | tf_op jit(solution)/shard_map/pallas_call | solution.py:27
  52.8 1.7 %collective-permute-done.3.halo = f32[7,64,128]{2,1,0:T(8,128)S(1)} collective-permute-done((f32[7,64,128]{2,1,0:T(8,128)S(1)}, f32[7,64,128]{2,1,0:T(8,128)S(1)}, u32[]{:S(2)}, u32[]{:S(2)}) %collective-permute-start.3) | collective-permute-done | bytes 229408 | tf_op jit(solution)/shard_map/ppermute | solution.py:429
  54.4 1.5 %shard_map.110 = (f32[7,64,128]{2,1,0:T(8,128)S(1)}, f32[16,128]{1,0:T(8,128)S(1)}) custom-call(s32[2]{0:T(128)S(1)} %pad_add_fusion.place, f32[2,8,128]{2,1,0:T(8,128)S(1)} %get-tuple-element.27.half, f32[7,64,128]{2,1,0:T(8,128)S(1)} %shard_map.106.top_b.top, f32[2,17,64,128]{3,2,1,0:T(8,128)S(1)} %get-tuple-element.31.inner, ...), custom_call_target="tpu_custom_call" | custom-call | flops 3620864 | bytes 1114112 | tf_op jit(solution)/shard_map/pallas_call | solution.py:27
  55.9 3.7 %collective-permute-done.6 = f32[16,128]{1,0:T(8,128)S(1)} collective-permute-done((f32[16,128]{1,0:T(8,128)S(1)}, f32[16,128]{1,0:T(8,128)S(1)}, u32[]{:S(2)}, u32[]{:S(2)}) %collective-permute-start.6) | collective-permute-done | bytes 8224 | tf_op jit(solution)/shard_map/ppermute | solution.py:453
  59.6 3.6 %collective-permute-done.7 = f32[16,128]{1,0:T(8,128)S(1)} collective-permute-done((f32[16,128]{1,0:T(8,128)S(1)}, f32[16,128]{1,0:T(8,128)S(1)}, u32[]{:S(2)}, u32[]{:S(2)}) %collective-permute-start.7) | collective-permute-done | bytes 8224 | tf_op jit(solution)/shard_map/ppermute | solution.py:453
  63.2 0.7 collective-permute-start.8
  63.9 3.9 %collective-permute-done.8 = f32[16,128]{1,0:T(8,128)S(1)} collective-permute-done((f32[16,128]{1,0:T(8,128)S(1)}, f32[16,128]{1,0:T(8,128)S(1)}, u32[]{:S(2)}, u32[]{:S(2)}) %collective-permute-start.8) | collective-permute-done | bytes 8224 | tf_op jit(solution)/shard_map/ppermute | solution.py:453
  67.8 1.2 %shard_map.111 = (f32[16,128]{1,0:T(8,128)S(1)}, f32[4,64,128]{2,1,0:T(8,128)S(1)}, f32[4,16,128]{2,1,0:T(8,128)S(1)}, f32[4,16,128]{2,1,0:T(8,128)S(1)}, f32[4,...) custom-call(s32[2]{0:T(128)S(1)} %pad_add_fusion.place, f32[16,128]{1,0:T(8,128)S(1)} %add.25.gram, ...), custom_call_target="tpu_custom_call" | custom-call | flops 7241728 | bytes 2228224 | tf_op jit(solution)/shard_map/pallas_call | solution.py:27
  69.0 1.6 %collective-permute-start.10 = (f32[4,16,128]{2,1,0:T(8,128)S(1)}, f32[4,16,128]{2,1,0:T(8,128)S(1)}, u32[]{:S(2)}, u32[]{:S(2)}) collective-permute-start(f32[4,16,128]{2,1,0:T(8,128)S(1)} %get-tuple-element.47), channel_id=1, source_target_pairs={{0,16},{8,24},{16,0},{24,8},{1,17},{9,25},{17,1},{25,9},{2,18},{10... | collective-permute-start | bytes 98312 | tf_op jit(solution)/shard_map/ppermute | solution.py:464
  71.2 3.2 %shard_map.112 = (f32[16,4,64,128]{3,2,1,0:T(8,128)}, f32[16,16]{1,0:T(8,128)}, f32[1,16]{1,0:T(1,128)}, f32[4,64,128]{2,1,0:T(8,128)}) custom-call(s32[2]{0:T(128)S(1)} %pad_add_fusion.place, f32[16,128]{1,0:T(8,128)S(1)} %get-tuple-element.39.weights.solved, f32[16,128]{1,0:T(8,128)S(1)} %get-tuple-element.39.weights.solved, ...), custom_call_target="tpu_custom_call" | custom-call | flops 14483456 | bytes 4456448 | tf_op jit(solution)/shard_map/pallas_call | solution.py:27
  (25 shorter events, 1.6 us)
Async XLA Ops:
  0.7 10.1 %copy-start = (f32[1,3,4,64,128]{4,3,2,1,0:T(8,128)S(1)}, f32[1,3,4,64,128]{4,3,2,1,0:T(8,128)}, u32[]{:S(2)}) copy-start(f32[1,3,4,64,128]{4,3,2,1,0:T(8,128)} %param.8) | copy-start | bytes 1179652
  0.7 10.1 %copy-start.1 = (f32[1,4,64,128]{3,2,1,0:T(8,128)S(1)}, f32[1,4,64,128]{3,2,1,0:T(8,128)}, u32[]{:S(2)}) copy-start(f32[1,4,64,128]{3,2,1,0:T(8,128)} %param.9) | copy-start | bytes 393220
  0.7 10.1 %copy-start.2 = (f32[1,4,64,128]{3,2,1,0:T(8,128)S(1)}, f32[1,4,64,128]{3,2,1,0:T(8,128)}, u32[]{:S(2)}) copy-start(f32[1,4,64,128]{3,2,1,0:T(8,128)} %param.10) | copy-start | bytes 393220
  0.7 10.1 %copy-start.3 = (f32[1,4,64,128]{3,2,1,0:T(8,128)S(1)}, f32[1,4,64,128]{3,2,1,0:T(8,128)}, u32[]{:S(2)}) copy-start(f32[1,4,64,128]{3,2,1,0:T(8,128)} %param.7) | copy-start | bytes 393220
  2.3 18.8 %collective-permute-start.2 = (f32[17,64,128]{2,1,0:T(8,128)S(1)}, f32[17,64,128]{2,1,0:T(8,128)S(1)}, u32[]{:S(2)}, u32[]{:S(2)}) collective-permute-start(f32[17,64,128]{2,1,0:T(8,128)S(1)} %shard_map.103), channel_id=1, source_target_pairs={{0,7},{1,2},{2,1},{3,4},{4,3},{5,6},{6,5},{7,0},{8,15},{9,10},{10,... | collective-permute-start | bytes 1671176 | tf_op jit(solution)/shard_map/ppermute | solution.py:402
  10.0 30.1 %collective-permute-start.1 = (f32[10,64,128]{2,1,0:T(8,128)S(1)}, f32[10,64,128]{2,1,0:T(8,128)S(1)}, u32[]{:S(2)}, u32[]{:S(2)}) collective-permute-start(f32[10,64,128]{2,1,0:T(8,128)S(1)} %get-tuple-element.30), channel_id=1, source_target_pairs={{0,1},{1,0},{2,3},{3,2},{4,5},{5,4},{6,7},{7,6},{8,9},{9,8},{10,11... | collective-permute-start | bytes 983048 | tf_op jit(solution)/shard_map/ppermute | solution.py:399
  22.1 26.0 %collective-permute-start.4 = (f32[17,64,128]{2,1,0:T(8,128)S(1)}, f32[17,64,128]{2,1,0:T(8,128)S(1)}, u32[]{:S(2)}, u32[]{:S(2)}) collective-permute-start(f32[17,64,128]{2,1,0:T(8,128)S(1)} %shard_map.104.order.bottom), channel_id=1, source_target_pairs={{0,7},{1,2},{2,1},{3,4},{4,3},{5,6},{6,5},{7,0},{8,15},{9,10},{10,... | collective-permute-start | bytes 1671176 | tf_op jit(solution)/shard_map/ppermute | solution.py:415
  26.6 18.4 %collective-permute-start = (f32[7,64,128]{2,1,0:T(8,128)S(1)}, f32[7,64,128]{2,1,0:T(8,128)S(1)}, u32[]{:S(2)}, u32[]{:S(2)}) collective-permute-start(f32[7,64,128]{2,1,0:T(8,128)S(1)} %get-tuple-element.29), channel_id=1, source_target_pairs={{0,1},{1,0},{2,3},{3,2},{4,5},{5,4},{6,7},{7,6},{8,9},{9,8},{10,11... | collective-permute-start | bytes 688136 | tf_op jit(solution)/shard_map/ppermute | solution.py:400
  40.9 11.1 %collective-permute-start.5 = (f32[10,64,128]{2,1,0:T(8,128)S(1)}, f32[10,64,128]{2,1,0:T(8,128)S(1)}, u32[]{:S(2)}, u32[]{:S(2)}) collective-permute-start(f32[10,64,128]{2,1,0:T(8,128)S(1)} %shard_map.105.order.top_a.top), channel_id=1, source_target_pairs={{0,1},{1,0},{2,3},{3,2},{4,5},{5,4},{6,7},{7,6},{8,9},{9,8},{10,11... | collective-permute-start | bytes 983048 | tf_op jit(solution)/shard_map/ppermute | solution.py:422
  45.8 8.6 %collective-permute-start.3 = (f32[7,64,128]{2,1,0:T(8,128)S(1)}, f32[7,64,128]{2,1,0:T(8,128)S(1)}, u32[]{:S(2)}, u32[]{:S(2)}) collective-permute-start(f32[7,64,128]{2,1,0:T(8,128)S(1)} %shard_map.106.top_b.top), channel_id=1, source_target_pairs={{0,1},{1,0},{2,3},{3,2},{4,5},{5,4},{6,7},{7,6},{8,9},{9,8},{10,11... | collective-permute-start | bytes 688136 | tf_op jit(solution)/shard_map/ppermute | solution.py:429
  55.9 3.7 %collective-permute-start.6 = (f32[16,128]{1,0:T(8,128)S(1)}, f32[16,128]{1,0:T(8,128)S(1)}, u32[]{:S(2)}, u32[]{:S(2)}) collective-permute-start(f32[16,128]{1,0:T(8,128)S(1)} %get-tuple-element.35), channel_id=1, source_target_pairs={{0,1},{1,0},{2,3},{3,2},{4,5},{5,4},{6,7},{7,6},{8,9},{9,8},{10,11... | collective-permute-start | bytes 24584 | tf_op jit(solution)/shard_map/ppermute | solution.py:453
  59.6 3.7 %collective-permute-start.7 = (f32[16,128]{1,0:T(8,128)S(1)}, f32[16,128]{1,0:T(8,128)S(1)}, u32[]{:S(2)}, u32[]{:S(2)}) collective-permute-start(f32[16,128]{1,0:T(8,128)S(1)} %add.23), channel_id=1, source_target_pairs={{0,2},{1,3},{2,0},{3,1},{4,6},{5,7},{6,4},{7,5},{8,10},{9,11},{10,... | collective-permute-start | bytes 24584 | tf_op jit(solution)/shard_map/ppermute | solution.py:453
  63.2 4.5 %collective-permute-start.8 = (f32[16,128]{1,0:T(8,128)S(1)}, f32[16,128]{1,0:T(8,128)S(1)}, u32[]{:S(2)}, u32[]{:S(2)}) collective-permute-start(f32[16,128]{1,0:T(8,128)S(1)} %add.24), channel_id=1, source_target_pairs={{0,4},{1,5},{2,6},{3,7},{4,0},{5,1},{6,2},{7,3},{8,12},{9,13},{10,... | collective-permute-start | bytes 24584 | tf_op jit(solution)/shard_map/ppermute | solution.py:453
  69.0 5.5 %collective-permute-start.10 = (f32[4,16,128]{2,1,0:T(8,128)S(1)}, f32[4,16,128]{2,1,0:T(8,128)S(1)}, u32[]{:S(2)}, u32[]{:S(2)}) collective-permute-start(f32[4,16,128]{2,1,0:T(8,128)S(1)} %get-tuple-element.47), channel_id=1, source_target_pairs={{0,16},{8,24},{16,0},{24,8},{1,17},{9,25},{17,1},{25,9},{2,18},{10... | collective-permute-start | bytes 98312 | tf_op jit(solution)/shard_map/ppermute | solution.py:464
  70.6 3.9 %collective-permute-start.11 = (f32[4,16,128]{2,1,0:T(8,128)S(1)}, f32[4,16,128]{2,1,0:T(8,128)S(1)}, u32[]{:S(2)}, u32[]{:S(2)}) collective-permute-start(f32[4,16,128]{2,1,0:T(8,128)S(1)} %get-tuple-element.48), channel_id=1, source_target_pairs={{0,24},{8,16},{16,8},{24,0},{1,25},{9,17},{17,9},{25,1},{2,26},{10... | collective-permute-start | bytes 98312 | tf_op jit(solution)/shard_map/ppermute | solution.py:464
  70.8 3.7 %collective-permute-start.9 = (f32[4,16,128]{2,1,0:T(8,128)S(1)}, f32[4,16,128]{2,1,0:T(8,128)S(1)}, u32[]{:S(2)}, u32[]{:S(2)}) collective-permute-start(f32[4,16,128]{2,1,0:T(8,128)S(1)} %get-tuple-element.46), channel_id=1, source_target_pairs={{0,8},{8,0},{16,24},{24,16},{1,9},{9,1},{17,25},{25,17},{2,10},{10... | collective-permute-start | bytes 98312 | tf_op jit(solution)/shard_map/ppermute | solution.py:464
